TPU v7x, 32 devices: a whole 2x2x4 slice. The times are simulated.
32 devices in a mesh: lon: 8 (over y, x, core), lat: 4 (over z).
Axes of the slice: x: 2, y: 2, z: 4, core: 2. Of those that a mesh axis runs over, the one named last changes fastest.
Arguments:
- fields: bfloat16 [1, 64, 64, 1024], P(None, None, 'lat', 'lon'), may hold values from -6 to 6
- cotangent: bfloat16 [1, 64, 64, 1024], P(None, None, 'lat', 'lon'), may hold values from -6 to 6
- ocean_mask: int32 [64, 1024], P('lat', 'lon'), may hold values 0 or 1
- seam_partner: int32 [1024], replicated, may hold values from 0 to 1023, as said below
- depth_weight: bfloat16 [64, 7, 7], replicated, may hold values from -0.875 to 0.875
- norm_gain: bfloat16 [64], replicated, may hold values from 0.5 to 1.5
- layer_norm_bias: bfloat16 [64], replicated, may hold values from -3 to 3
- up_weight: bfloat16 [256, 64], replicated, may hold values from -0.75 to 0.75
- up_bias: bfloat16 [256], replicated, may hold values from -3 to 3
- down_weight: bfloat16 [64, 256], replicated, may hold values from -0.375 to 0.375
- layer_scale: bfloat16 [64], replicated, may hold values from 0.5 to 1.5
Outputs:
- output: bfloat16 [1, 64, 64, 1024], P(None, None, 'lat', 'lon')
- grad_fields: bfloat16 [1, 64, 64, 1024], P(None, None, 'lat', 'lon')
- grad_depth: float32 [64, 7, 7], replicated
- grad_gain: float32 [64], replicated
- grad_bias: float32 [64], replicated
- grad_up_weight: float32 [256, 64], replicated
- grad_up_bias: float32 [256], replicated
- grad_down_weight: float32 [64, 256], replicated
- grad_scale: float32 [64], replicated
Inputs may be any that keep to these rules, and one draw needn't show every extreme that they name: seam_partner[i] = (s - i) mod 1024 for one whole number s, so it is its own inverse.
All inputs are finite; a program needn't handle non-finite values. No bound on the sum of `ocean_mask` on one device may be relied on, other than what follows from the above.
Results may differ from a plain program's by a relative error of at most 0.0068.
Values may be sent and summed in bfloat16 or wider, within the bound.
No kernel may reach another device: no remote copies, remote signals or barrier semaphores. Data moves between devices by JAX's collectives and lax.ppermute only.
A program may use at most 64 MiB of HBM per device.

v0:
```python
import math

import jax
import jax.numpy as jnp
from jax import lax
from jax.sharding import PartitionSpec as P


def extended_2(cells, sides, width, closed):
    for axis, dim in sides:
        count = lax.axis_size(axis)
        ends = count if closed else count - 1
        head = lax.slice_in_dim(cells, 0, width, axis=dim)
        tail = lax.slice_in_dim(cells, cells.shape[dim] - width, cells.shape[dim], axis=dim)
        cells = jnp.concatenate(
            [
                lax.ppermute(tail, axis, [(i, (i + 1) % count) for i in range(ends)]),
                cells,
                lax.ppermute(head, axis, [((i + 1) % count, i) for i in range(ends)]),
            ],
            axis=dim,
        )
    return cells


def gelu_slope(pre):
    cdf = 0.5 * (1.0 + lax.erf(pre / math.sqrt(2.0)))
    return cdf + pre * jnp.exp(-0.5 * pre * pre) / math.sqrt(2.0 * math.pi)


def cell_terms(
    conv, field, cot, mask, norm_gain, layer_norm_bias, up_weight, up_bias, down_weight, layer_scale
):
    mean_c = jnp.mean(conv, axis=0, keepdims=True)
    centered_input = conv - mean_c
    var_c = jnp.mean(centered_input * centered_input, axis=0, keepdims=True)
    reciprocal_deviation = lax.rsqrt(var_c + 1e-06)
    standardized_input = centered_input * reciprocal_deviation
    layer_norm_gain = norm_gain.astype(jnp.float32)[:, None]
    normalized_output = (
        standardized_input * layer_norm_gain + layer_norm_bias.astype(jnp.float32)[:, None]
    ).astype(jnp.bfloat16)
    pre = (
        jnp.dot(up_weight, normalized_output, preferred_element_type=jnp.float32)
        + up_bias.astype(jnp.float32)[:, None]
    )
    hidden = jax.nn.gelu(pre, approximate=False).astype(jnp.bfloat16)
    branch = jnp.dot(down_weight, hidden, preferred_element_type=jnp.float32)
    scale = layer_scale.astype(jnp.float32)[:, None]
    out = (mask * (field.astype(jnp.float32) + scale * branch)).astype(jnp.bfloat16)
    grad_in = mask * cot.astype(jnp.float32)
    d_branch = (grad_in * scale).astype(jnp.bfloat16)
    g_scale = jnp.sum(grad_in * branch, axis=1)
    contract_cells = (((1,), (1,)), ((), ()))
    contract_first = (((0,), (0,)), ((), ()))
    g_down = lax.dot_general(d_branch, hidden, contract_cells, preferred_element_type=jnp.float32)
    d_hidden = lax.dot_general(
        down_weight, d_branch, contract_first, preferred_element_type=jnp.float32
    )
    d_pre = (d_hidden * gelu_slope(pre)).astype(jnp.bfloat16)
    g_up_b = jnp.sum(d_pre.astype(jnp.float32), axis=1)
    g_up_w = lax.dot_general(
        d_pre, normalized_output, contract_cells, preferred_element_type=jnp.float32
    )
    normalized_gradient = lax.dot_general(
        up_weight, d_pre, contract_first, preferred_element_type=jnp.float32
    )
    gain_gradient = jnp.sum(normalized_gradient * standardized_input, axis=1)
    g_bias = jnp.sum(normalized_gradient, axis=1)
    gradient_through_norm = normalized_gradient * layer_norm_gain
    convolution_gradient = reciprocal_deviation * (
        gradient_through_norm
        - jnp.mean(gradient_through_norm, axis=0, keepdims=True)
        - standardized_input
        * jnp.mean(gradient_through_norm * standardized_input, axis=0, keepdims=True)
    )
    return (
        out,
        convolution_gradient.astype(jnp.bfloat16),
        (gain_gradient, g_bias, g_up_w, g_up_b, g_down, g_scale),
    )


def make_picker(wanted, carry, piece):
    width = piece.shape[3]
    inside = (wanted >= 0) & (wanted < width)
    picked = jnp.take(piece, jnp.clip(wanted, 0, width - 1), axis=3)
    return jnp.where(inside[None, None, None, :], picked, carry)


def shards(
    fields,
    cotangent,
    ocean_mask,
    seam_partner,
    depth_weight,
    norm_gain,
    layer_norm_bias,
    up_weight,
    up_bias,
    down_weight,
    layer_scale,
):
    samples, chans, rows, cols = fields.shape
    total_lon = seam_partner.shape[0]
    lon_start = lax.axis_index("lon") * cols
    positions = (lon_start + jnp.arange(-3, cols + 3, dtype=jnp.int32)) % total_lon
    partner_cols = jnp.take(seam_partner, positions)
    own_partner = partner_cols[3 : cols + 3]
    is_top = lax.axis_index("lat") == lax.axis_size("lat") - 1
    weight_f = depth_weight.astype(jnp.float32)
    mask_f = ocean_mask.astype(jnp.float32)
    lon_padded = extended_2(fields, (("lon", 3),), 3, True)
    banded = extended_2(lon_padded, (("lat", 2),), 3, False)
    upper = fields[:, :, rows - 3 :, :][:, :, ::-1, :]
    fold_init = jnp.zeros((samples, chans, 3, cols + 6), jnp.bfloat16)
    folded = make_picker(partner_cols, fold_init, lax.all_gather(upper, "lon", axis=3, tiled=True))
    top_rows = jnp.where(is_top, folded, banded[:, :, rows + 3 :, :])
    extended = jnp.concatenate([banded[:, :, : rows + 3, :], top_rows], axis=2)
    conv = jnp.zeros((samples, chans, rows, cols), jnp.float32)
    for row_tap in range(7):
        for col_tap in range(7):
            conv = conv + weight_f[:, row_tap, col_tap][None, :, None, None] * extended[
                :, :, row_tap : row_tap + rows, col_tap : col_tap + cols
            ].astype(jnp.float32)
    mask_flat = mask_f.reshape(1, rows * cols)
    out_s, dconv_s, parts = cell_terms(
        conv[0].reshape(chans, rows * cols),
        fields[0].reshape(chans, rows * cols),
        cotangent[0].reshape(chans, rows * cols),
        mask_flat,
        norm_gain,
        layer_norm_bias,
        up_weight,
        up_bias,
        down_weight,
        layer_scale,
    )
    outputs = [out_s.reshape(chans, rows, cols)]
    dconv_list = [dconv_s.reshape(chans, rows, cols)]
    output = jnp.stack(outputs)
    convolution_gradient = jnp.stack(dconv_list)
    d_conv_f = convolution_gradient.astype(jnp.float32)
    taps = []
    for row_tap in range(7):
        line = []
        for col_tap in range(7):
            line.append(
                jnp.sum(
                    d_conv_f
                    * extended[:, :, row_tap : row_tap + rows, col_tap : col_tap + cols].astype(
                        jnp.float32
                    ),
                    axis=(0, 2, 3),
                )
            )
        taps.append(jnp.stack(line, axis=1))
    g_depth = jnp.stack(taps, axis=1)
    lon_back = extended_2(convolution_gradient, (("lon", 3),), 3, True)
    band_back = extended_2(lon_back, (("lat", 2),), 3, False)
    deeper = jnp.pad(band_back, ((0, 0), (0, 0), (0, 3), (0, 0)))
    spread = jnp.zeros((samples, chans, rows + 3, cols), jnp.float32)
    for row_tap in range(7):
        for col_tap in range(7):
            spread = spread + weight_f[:, row_tap, col_tap][None, :, None, None] * deeper[
                :, :, 6 - row_tap : 9 - row_tap + rows, 6 - col_tap : 6 - col_tap + cols
            ].astype(jnp.float32)
    own = spread[:, :, :rows, :]
    margin = spread[:, :, rows:, :]
    back_init = jnp.zeros((samples, chans, 3, cols), jnp.float32)
    back = make_picker(
        own_partner,
        back_init,
        lax.all_gather(margin.astype(jnp.bfloat16), "lon", axis=3, tiled=True).astype(jnp.float32),
    )
    extra = back[:, :, ::-1, :]
    own = own.at[:, :, rows - 3 :, :].add(jnp.where(is_top, extra, 0.0))
    grad_fields = (mask_f[None, None] * cotangent.astype(jnp.float32) + own).astype(jnp.bfloat16)
    gain_gradient, g_bias, g_up_w, g_up_b, g_down, g_scale = parts
    summed = lax.psum(
        (g_depth, gain_gradient, g_bias, g_up_w, g_up_b, g_down, g_scale), ("lon", "lat")
    )
    return (
        output,
        grad_fields,
        summed[0],
        summed[1],
        summed[2],
        summed[3],
        summed[4],
        summed[5],
        summed[6],
    )


def solution(mesh):
    placed = (
        P(None, None, "lat", "lon"),
        P(None, None, "lat", "lon"),
        P("lat", "lon"),
        P(),
        P(),
        P(),
        P(),
        P(),
        P(),
        P(),
        P(),
    )
    return jax.shard_map(
        shards,
        mesh=mesh,
        in_specs=placed,
        out_specs=(
            P(None, None, "lat", "lon"),
            P(None, None, "lat", "lon"),
            P(),
            P(),
            P(),
            P(),
            P(),
            P(),
            P(),
        ),
        check_vma=False,
    )
```

profile of v0, /device:TPU:0, one launch (start us, length us, event | category | flops | bytes accessed | tf_op | source)
XLA Modules:
  0.0 222.9 jit_solution(4524636427650985264)
XLA Ops:
  7.2 1.6 copy.94
  9.4 2.9 %collective-permute-start.1 = (bf16[1,64,16,3]{1,2,3,0:T(8,128)(2,1)S(1)}, bf16[1,64,16,3]{1,2,3,0:T(8,128)(2,1)S(1)}, u32[]{:S(2)}, u32[]{:S(2)}) collective-permute-start(bf16[1,64,16,3]{1,2,3,0:T(8,128)(2,1)S(1)} %get-tuple-element.148), channel_id=1, source_target_pairs={{4,0},{8,4},{12,8},{16,12},{20,16},{24,20},{28,24},{0,28},{5,1},{9... | collective-permute-start | bytes 18440 | tf_op jit(solution)/shard_map/ppermute | solution.py:19
  14.1 1.9 gather_fusion
  19.1 1.4 copy.95
  20.7 1.3 collective-permute-start.3
  22.0 10.4 %all_gather.6 = bf16[1,64,3,1024]{3,1,2,0:T(8,128)(2,1)S(1)} all-gather(bf16[1,64,3,128]{3,1,2,0:T(8,128)(2,1)S(1)} %rev.6), channel_id=1, replica_groups=mesh['lon'=8,'lat'=4] {'lon'}, dimensions={3}, use_global_device_ids=true | all-gather | bytes 442368 | tf_op jit(solution)/shard_map/all_gather | solution.py:117
  33.1 1.1 copy.108
  35.5 4.6 %collective-permute-start.2 = (bf16[1,64,3,134]{1,2,3,0:T(4,128)(2,1)S(1)}, bf16[1,64,3,134]{1,2,3,0:T(4,128)(2,1)S(1)}, u32[]{:S(2)}, u32[]{:S(2)}) collective-permute-start(bf16[1,64,3,134]{1,2,3,0:T(4,128)(2,1)S(1)} %get-tuple-element.143), channel_id=1, source_target_pairs={{0,1},{1,2},{2,3},{4,5},{5,6},{6,7},{8,9},{9,10},{10,11},{12,13},{... | collective-permute-start | bytes 154376 | tf_op jit(solution)/shard_map/ppermute | solution.py:17
  40.5 3.0 %collective-permute-done.2 = bf16[1,64,3,134]{1,2,3,0:T(4,128)(2,1)S(1)} collective-permute-done((bf16[1,64,3,134]{1,2,3,0:T(4,128)(2,1)S(1)}, bf16[1,64,3,134]{1,2,3,0:T(4,128)(2,1)S(1)}, u32[]{:S(2)}, u32[]{:S(2)}) %collective-permute-start.2) | collective-permute-done | bytes 51488 | tf_op jit(solution)/shard_map/ppermute | solution.py:17
  44.3 11.1 %fusion.134 = (f32[16,128]{0,1:T(8,128)S(1)}, f32[1,64,16,128]{1,2,3,0:T(8,128)S(1)}) fusion(bf16[1,64,19,134]{1,2,3,0:T(8,128)(2,1)S(1)} %get-tuple-element.142, f32[64]{0:T(128)S(1)} %get-tuple-element.152, f32[64]{0:T(128)S(1)} %get-tuple-element.153, f32[64]{0:T(128)S(1)} %get-tuple-element.154, f32[64]{0:T(128)S(1)} %get-tuple-element.155, ...), kind=kLoop, calls=%fused_computation.375 | loop fusion | flops 20051968 | bytes 11829504 | tf_op jit(solution)/shard_map/reduce_sum | solution.py:34
  55.4 1.3 copy.103
  57.7 6.9 %fusion.5 = (bf16[256,2048]{0,1:T(8,128)(2,1)}, f32[256,2048]{0,1:T(8,128)S(1)}) fusion(f32[256]{0:T(256)S(1)} %convert_element_type.474, bf16[256,64]{0,1:T(8,128)(2,1)S(1)} %copy-done, f32[64]{0:T(128)S(1)} %convert_element_type.472, f32[64]{0:T(128)S(1)} %convert_element_type.471, f32[2048]{0:T(1024)S(1)} %rsqrt_bitcast_fusion, ...), kind=kOutput, calls=%fused_computation.62 | convolution fusion | flops 102367232 | bytes 3720704 | tf_op jit(solution)/shard_map/dot_general | solution.py:44
  64.6 2.7 %convert_reduce_fusion = (f32[256]{0:T(256)}, bf16[256,2048]{0,1:T(8,128)(2,1)S(1)}) fusion(f32[256,2048]{0,1:T(8,128)S(1)} %get-tuple-element.206, bf16[64,256]{1,0:T(8,128)(2,1)S(1)} %copy-done.8, f32[8,8,16,128]{3,2,1,0:T(8,128)S(1)} %bitcast.273, f32[64]{0:T(128)} %convert_element_type.420, f32[2048]{0:T(1024)S(1)} %get-tuple-element.201), kind=kOutput, calls=%fused_computation.67 | convolution fusion | flops 73793280 | bytes 3712256 | tf_op jit(solution)/shard_map/dot_general | solution.py:57
  68.3 1.1 fusion.121
  70.2 1.6 fusion.112
  71.9 4.1 %fusion.113 = (f32[64]{0:T(128)}, f32[64]{0:T(128)}, f32[64]{0:T(128)}, f32[64]{0:T(128)}, f32[64]{0:T(128)}, /*index=5*/f32[64]{0:T(128)}, f32[64]{0:T(128)}, f...) fusion(bf16[1,64,16,128]{1,2,3,0:T(8,128)(2,1)S(1)} %copy.114, ...), kind=kLoop, calls=%fused_computation.227 | loop fusion | flops 7207808 | bytes 4985344 | tf_op jit(solution)/shard_map/reduce_sum | solution.py:149
  76.0 4.1 %fusion.85 = (f32[64]{0:T(128)}, f32[64]{0:T(128)S(1)}, f32[64]{0:T(128)S(1)}, f32[64]{0:T(128)S(1)}, f32[64]{0:T(128)S(1)}, /*index=5*/f32[64]{0:T(128)S(1)}, f...) fusion(bf16[1,64,16,128]{1,2,3,0:T(8,128)(2,1)S(1)} %copy.114, ...), kind=kLoop, calls=%fused_computation.199 | loop fusion | flops 7207808 | bytes 4985344 | tf_op jit(solution)/shard_map/reduce_sum | solution.py:149
  80.2 1.7 fusion.132
  82.3 1.9 multiply_reduce_fusion.1
  84.5 2.6 %collective-permute-start.5 = (bf16[1,64,16,3]{3,1,2,0:T(8,128)(2,1)S(1)}, bf16[1,64,16,3]{3,1,2,0:T(8,128)(2,1)S(1)}, u32[]{:S(2)}, u32[]{:S(2)}) collective-permute-start(bf16[1,64,16,3]{3,1,2,0:T(8,128)(2,1)S(1)} %get-tuple-element.150), channel_id=1, source_target_pairs={{4,0},{8,4},{12,8},{16,12},{20,16},{24,20},{28,24},{0,28},{5,1},{9... | collective-permute-start | bytes 18440 | tf_op jit(solution)/shard_map/ppermute | solution.py:19
  88.1 1.2 fusion.92
  89.7 3.4 %collective-permute-done.4 = bf16[1,64,16,3]{3,1,2,0:T(8,128)(2,1)S(1)} collective-permute-done((bf16[1,64,16,3]{3,1,2,0:T(8,128)(2,1)S(1)}, bf16[1,64,16,3]{3,1,2,0:T(8,128)(2,1)S(1)}, u32[]{:S(2)}, u32[]{:S(2)}) %collective-permute-start.4) | collective-permute-done | bytes 6176 | tf_op jit(solution)/shard_map/ppermute | solution.py:17
  93.2 4.4 %collective-permute-start.6 = (bf16[1,64,3,134]{3,1,2,0:T(8,128)(2,1)S(1)}, bf16[1,64,3,134]{3,1,2,0:T(8,128)(2,1)S(1)}, u32[]{:S(2)}, u32[]{:S(2)}) collective-permute-start(bf16[1,64,3,134]{3,1,2,0:T(8,128)(2,1)S(1)} %get-tuple-element.140), channel_id=1, source_target_pairs={{0,1},{1,2},{2,3},{4,5},{5,6},{6,7},{8,9},{9,10},{10,11},{12,13},{... | collective-permute-start | bytes 154376 | tf_op jit(solution)/shard_map/ppermute | solution.py:17
  97.6 1.3 collective-permute-start.7
  99.5 41.6 %all-reduce.1 = (f32[64,7,7]{0,2,1:T(8,128)}, f32[64]{0:T(128)}, f32[64]{0:T(128)}, f32[256]{0:T(256)}, f32[64]{0:T(128)}) all-reduce(f32[64,7,7]{0,2,1:T(8,128)S(1)} %constant_dynamic-update-slice_fusion, f32[64]{0:T(128)} %get-tuple-element.108, f32[64]{0:T(128)S(1)} %reduce_sum.567, ...), channel_id=1, replica_groups=mesh['lon'=8,'lat'=4] {'lon','lat'}, use_global_device_ids=true, to_apply=%region_53.54 | all-reduce | flops 3584 | bytes 28672 | tf_op jit(solution)/shard_map/psum | solution.py:180
  142.3 6.3 %multiply_add_fusion = f32[1,64,19,128]{3,1,2,0:T(8,128)S(1)} fusion(bf16[1,64,19,134]{3,1,2,0:T(8,128)(2,1)S(1)} %get-tuple-element.138, bf16[1,64,22,134]{3,1,2,0:T(8,128)(2,1)S(1)} %pad_maximum_fusion.1, bf16[1,64,19,134]{3,1,2,0:T(8,128)(2,1)S(1)} %get-tuple-element.137, f32[64]{0:T(128)S(1)} %copy-done.13, f32[64]{0:T(128)S(1)} %copy-done.15, ...), kind=kLoop, calls=%fused_computation.239 | loop fusion | flops 22724608 | bytes 10082304 | tf_op jit(solution)/shard_map/add | solution.py:165
  148.6 10.4 %all_gather.7 = bf16[1,64,3,1024]{3,1,2,0:T(8,128)(2,1)S(1)} all-gather(bf16[1,64,3,128]{3,1,2,0:T(8,128)(2,1)S(1)} %slice.1226), channel_id=1, replica_groups=mesh['lon'=8,'lat'=4] {'lon'}, dimensions={3}, use_global_device_ids=true | all-gather | bytes 442368 | tf_op jit(solution)/shard_map/all_gather | solution.py:174
  159.8 1.6 bitcast_convert_fusion
  161.4 2.5 %gather_fusion.2 = f32[128,64,3]{1,2,0:T(4,128)S(1)} fusion(f32[64,3,1024]{0,1,2:T(4,128)} %bitcast_convert_fusion, s32[1024]{0:T(1024)} %pad_clamp_fusion), kind=kCustom, calls=%fused_computation.2 | custom fusion | bytes 197120 | tf_op jit(solution)/shard_map/jit(_take)/gather | solution.py:87
  165.1 48.1 %all-reduce.5.cloned.1.call-done = (f32[256,64]{0,1:T(8,128)}, f32[64,256]{1,0:T(8,128)}) async-done(((f32[256,64]{0,1:T(8,128)}, f32[64,256]{1,0:T(8,128)}), (f32[256,64]{0,1:T(8,128)}, f32[64,256]{1,0:T(8,128)})) %all-reduce.5.cloned.1.call-update) | async-done | bytes 131088 | tf_op jit(solution)/shard_map/psum | solution.py:180
  213.1 1.5 copy.159
  214.6 1.5 copy.160
  (337 shorter events, 15.5 us)
Async XLA Ops:
  7.2 50.5 %copy-start = (bf16[256,64]{0,1:T(8,128)(2,1)S(1)}, bf16[256,64]{0,1:T(8,128)(2,1)}, u32[]{:S(2)}) copy-start(bf16[256,64]{0,1:T(8,128)(2,1)} %param.20) | copy-start | bytes 98308
  7.2 205.9 %all-reduce.5.cloned.1.call-start = ((), (), s32[]{:S(2)}) async-start(), calls=%async_computation | async-start | bytes 262144 | tf_op jit(solution)/shard_map/psum | solution.py:180
  8.8 11.7 %collective-permute-start = (bf16[1,64,16,3]{1,2,3,0:T(8,128)(2,1)S(1)}, bf16[1,64,16,3]{1,2,3,0:T(8,128)(2,1)S(1)}, u32[]{:S(2)}, u32[]{:S(2)}) collective-permute-start(bf16[1,64,16,3]{1,2,3,0:T(8,128)(2,1)S(1)} %get-tuple-element.147), channel_id=1, source_target_pairs={{0,4},{4,8},{8,12},{12,16},{16,20},{20,24},{24,28},{28,0},{1,5},{5... | collective-permute-start | bytes 18440 | tf_op jit(solution)/shard_map/ppermute | solution.py:17
  9.4 11.1 %collective-permute-start.1 = (bf16[1,64,16,3]{1,2,3,0:T(8,128)(2,1)S(1)}, bf16[1,64,16,3]{1,2,3,0:T(8,128)(2,1)S(1)}, u32[]{:S(2)}, u32[]{:S(2)}) collective-permute-start(bf16[1,64,16,3]{1,2,3,0:T(8,128)(2,1)S(1)} %get-tuple-element.148), channel_id=1, source_target_pairs={{4,0},{8,4},{12,8},{16,12},{20,16},{24,20},{28,24},{0,28},{5,1},{9... | collective-permute-start | bytes 18440 | tf_op jit(solution)/shard_map/ppermute | solution.py:19
  20.7 19.4 %collective-permute-start.3 = (bf16[1,64,3,134]{1,2,3,0:T(4,128)(2,1)S(1)}, bf16[1,64,3,134]{1,2,3,0:T(4,128)(2,1)S(1)}, u32[]{:S(2)}, u32[]{:S(2)}) collective-permute-start(bf16[1,64,3,134]{1,2,3,0:T(4,128)(2,1)S(1)} %get-tuple-element.144), channel_id=1, source_target_pairs={{1,0},{2,1},{3,2},{5,4},{6,5},{7,6},{9,8},{10,9},{11,10},{13,12},{... | collective-permute-start | bytes 154376 | tf_op jit(solution)/shard_map/ppermute | solution.py:19
  35.5 8.0 %collective-permute-start.2 = (bf16[1,64,3,134]{1,2,3,0:T(4,128)(2,1)S(1)}, bf16[1,64,3,134]{1,2,3,0:T(4,128)(2,1)S(1)}, u32[]{:S(2)}, u32[]{:S(2)}) collective-permute-start(bf16[1,64,3,134]{1,2,3,0:T(4,128)(2,1)S(1)} %get-tuple-element.143), channel_id=1, source_target_pairs={{0,1},{1,2},{2,3},{4,5},{5,6},{6,7},{8,9},{9,10},{10,11},{12,13},{... | collective-permute-start | bytes 154376 | tf_op jit(solution)/shard_map/ppermute | solution.py:17
  84.4 8.7 %collective-permute-start.4 = (bf16[1,64,16,3]{3,1,2,0:T(8,128)(2,1)S(1)}, bf16[1,64,16,3]{3,1,2,0:T(8,128)(2,1)S(1)}, u32[]{:S(2)}, u32[]{:S(2)}) collective-permute-start(bf16[1,64,16,3]{3,1,2,0:T(8,128)(2,1)S(1)} %get-tuple-element.149), channel_id=1, source_target_pairs={{0,4},{4,8},{8,12},{12,16},{16,20},{20,24},{24,28},{28,0},{1,5},{5... | collective-permute-start | bytes 18440 | tf_op jit(solution)/shard_map/ppermute | solution.py:17
  84.5 8.6 %collective-permute-start.5 = (bf16[1,64,16,3]{3,1,2,0:T(8,128)(2,1)S(1)}, bf16[1,64,16,3]{3,1,2,0:T(8,128)(2,1)S(1)}, u32[]{:S(2)}, u32[]{:S(2)}) collective-permute-start(bf16[1,64,16,3]{3,1,2,0:T(8,128)(2,1)S(1)} %get-tuple-element.150), channel_id=1, source_target_pairs={{4,0},{8,4},{12,8},{16,12},{20,16},{24,20},{28,24},{0,28},{5,1},{9... | collective-permute-start | bytes 18440 | tf_op jit(solution)/shard_map/ppermute | solution.py:19
  93.2 47.8 %collective-permute-start.6 = (bf16[1,64,3,134]{3,1,2,0:T(8,128)(2,1)S(1)}, bf16[1,64,3,134]{3,1,2,0:T(8,128)(2,1)S(1)}, u32[]{:S(2)}, u32[]{:S(2)}) collective-permute-start(bf16[1,64,3,134]{3,1,2,0:T(8,128)(2,1)S(1)} %get-tuple-element.140), channel_id=1, source_target_pairs={{0,1},{1,2},{2,3},{4,5},{5,6},{6,7},{8,9},{9,10},{10,11},{12,13},{... | collective-permute-start | bytes 154376 | tf_op jit(solution)/shard_map/ppermute | solution.py:17
  97.6 43.4 %collective-permute-start.7 = (bf16[1,64,3,134]{3,1,2,0:T(8,128)(2,1)S(1)}, bf16[1,64,3,134]{3,1,2,0:T(8,128)(2,1)S(1)}, u32[]{:S(2)}, u32[]{:S(2)}) collective-permute-start(bf16[1,64,3,134]{3,1,2,0:T(8,128)(2,1)S(1)} %get-tuple-element.139), channel_id=1, source_target_pairs={{1,0},{2,1},{3,2},{5,4},{6,5},{7,6},{9,8},{10,9},{11,10},{13,12},{... | collective-permute-start | bytes 154376 | tf_op jit(solution)/shard_map/ppermute | solution.py:19
  99.1 42.8 %copy-start.15 = (f32[64]{0:T(128)S(1)}, f32[64]{0:T(128)}, u32[]{:S(2)}) copy-start(f32[64]{0:T(128)} %copy-done.14) | copy-start | bytes 772
  99.1 42.8 %copy-start.17 = (f32[64]{0:T(128)S(1)}, f32[64]{0:T(128)}, u32[]{:S(2)}) copy-start(f32[64]{0:T(128)} %copy-done.16) | copy-start | bytes 772
  99.1 42.8 %copy-start.19 = (f32[64]{0:T(128)S(1)}, f32[64]{0:T(128)}, u32[]{:S(2)}) copy-start(f32[64]{0:T(128)} %copy-done.18) | copy-start | bytes 772
  99.1 42.8 %copy-start.21 = (f32[64]{0:T(128)S(1)}, f32[64]{0:T(128)}, u32[]{:S(2)}) copy-start(f32[64]{0:T(128)} %copy-done.20) | copy-start | bytes 772
  99.1 42.8 %copy-start.23 = (f32[64]{0:T(128)S(1)}, f32[64]{0:T(128)}, u32[]{:S(2)}) copy-start(f32[64]{0:T(128)} %copy-done.22) | copy-start | bytes 772
  99.1 42.8 %copy-start.25 = (f32[64]{0:T(128)S(1)}, f32[64]{0:T(128)}, u32[]{:S(2)}) copy-start(f32[64]{0:T(128)} %copy-done.24) | copy-start | bytes 772
  99.2 42.8 %copy-start.27 = (f32[64]{0:T(128)S(1)}, f32[64]{0:T(128)}, u32[]{:S(2)}) copy-start(f32[64]{0:T(128)} %copy-done.26) | copy-start | bytes 772
  99.2 42.8 %copy-start.29 = (f32[64]{0:T(128)S(1)}, f32[64]{0:T(128)}, u32[]{:S(2)}) copy-start(f32[64]{0:T(128)} %copy-done.28) | copy-start | bytes 772
  99.2 42.8 %copy-start.31 = (f32[64]{0:T(128)S(1)}, f32[64]{0:T(128)}, u32[]{:S(2)}) copy-start(f32[64]{0:T(128)} %copy-done.30) | copy-start | bytes 772
  99.2 42.8 %copy-start.33 = (f32[64]{0:T(128)S(1)}, f32[64]{0:T(128)}, u32[]{:S(2)}) copy-start(f32[64]{0:T(128)} %copy-done.32) | copy-start | bytes 772
  99.2 42.8 %copy-start.35 = (f32[64]{0:T(128)S(1)}, f32[64]{0:T(128)}, u32[]{:S(2)}) copy-start(f32[64]{0:T(128)} %copy-done.34) | copy-start | bytes 772
  99.2 42.8 %copy-start.37 = (f32[64]{0:T(128)S(1)}, f32[64]{0:T(128)}, u32[]{:S(2)}) copy-start(f32[64]{0:T(128)} %copy-done.36) | copy-start | bytes 772
  99.2 42.8 %copy-start.39 = (f32[64]{0:T(128)S(1)}, f32[64]{0:T(128)}, u32[]{:S(2)}) copy-start(f32[64]{0:T(128)} %copy-done.38) | copy-start | bytes 772
  99.2 42.8 %copy-start.41 = (f32[64]{0:T(128)S(1)}, f32[64]{0:T(128)}, u32[]{:S(2)}) copy-start(f32[64]{0:T(128)} %copy-done.40) | copy-start | bytes 772
  99.2 42.8 %copy-start.43 = (f32[64]{0:T(128)S(1)}, f32[64]{0:T(128)}, u32[]{:S(2)}) copy-start(f32[64]{0:T(128)} %copy-done.42) | copy-start | bytes 772
  99.2 42.8 %copy-start.45 = (f32[64]{0:T(128)S(1)}, f32[64]{0:T(128)}, u32[]{:S(2)}) copy-start(f32[64]{0:T(128)} %copy-done.44) | copy-start | bytes 772
  99.3 42.8 %copy-start.47 = (f32[64]{0:T(128)S(1)}, f32[64]{0:T(128)}, u32[]{:S(2)}) copy-start(f32[64]{0:T(128)} %copy-done.46) | copy-start | bytes 772
  99.3 42.8 %copy-start.49 = (f32[64]{0:T(128)S(1)}, f32[64]{0:T(128)}, u32[]{:S(2)}) copy-start(f32[64]{0:T(128)} %copy-done.48) | copy-start | bytes 772
  99.3 42.8 %copy-start.51 = (f32[64]{0:T(128)S(1)}, f32[64]{0:T(128)}, u32[]{:S(2)}) copy-start(f32[64]{0:T(128)} %copy-done.50) | copy-start | bytes 772
  99.3 42.8 %copy-start.53 = (f32[64]{0:T(128)S(1)}, f32[64]{0:T(128)}, u32[]{:S(2)}) copy-start(f32[64]{0:T(128)} %copy-done.52) | copy-start | bytes 772
  99.3 42.8 %copy-start.55 = (f32[64]{0:T(128)S(1)}, f32[64]{0:T(128)}, u32[]{:S(2)}) copy-start(f32[64]{0:T(128)} %copy-done.54) | copy-start | bytes 772
  99.3 42.8 %copy-start.57 = (f32[64]{0:T(128)S(1)}, f32[64]{0:T(128)}, u32[]{:S(2)}) copy-start(f32[64]{0:T(128)} %copy-done.56) | copy-start | bytes 772
  (107 other events, 2268.7 us)
Sparse Core Ops, SparseCore 0:
  88.0 125.1 all-reduce.4
where the time goes:
time: 224 us; the launch traced here: 223 us
  blocking collectives  62.4 us (28%)
  waiting for transfers between devices  54.5 us (24%)
  other arithmetic  36.6 us (16%)
  local copies, waits for them, and re-layouts  20.1 us (9%)
  starting transfers between devices  17.7 us (8%)
  between operations  16.3 us (7%)
  matrix products  15.3 us (7%)
    psum x1, waiting for transfers between devices, shards(): lax.psum((g_depth, gain_gradient, g_bias, g_up_w, g_up_b, g_down, g_scale...  48.1 us
    psum x1, blocking collectives, shards(): lax.psum((g_depth, gain_gradient, g_bias, g_up_w, g_up_b, g_down, g_scale...  41.6 us
    reduce_sum x4, other arithmetic, shards(): jnp.sum(d_conv_f * extended[:, :, row_tap:row_tap + rows, col_tap:col_tap...  11.1 us
    reduce_sum x1, other arithmetic, cell_terms(): mean_c = jnp.mean(conv, axis=0, keepdims=True)  11.1 us
    all_gather x1, blocking collectives, shards(): lax.all_gather(margin.astype(jnp.bfloat16), 'lon', axis=3, tiled=True)  10.4 us
    all_gather x1, blocking collectives, shards(): lax.all_gather(upper, 'lon', axis=3, tiled=True)  10.4 us
    ppermute x4, starting transfers between devices, extended_2(): lax.ppermute(tail, axis, [(i, (i + 1) % count) for i in range(ends)])  9.55 us
    ppermute x4, starting transfers between devices, extended_2(): lax.ppermute(head, axis, [((i + 1) % count, i) for i in range(ends)])  8.15 us
  transfers between devices with their start and end apart: 9, of which 3 were waited for; matrix products, arithmetic and copies ran while one was open for 12% of the time, Pallas kernels for 0%

commit v1 on v0

v1 whole, which is shorter than its diff:
```python
import functools
import math

import jax
import jax.numpy as jnp
from jax import lax
from jax.experimental import pallas as pl
from jax.experimental.pallas import tpu as pltpu
from jax.sharding import PartitionSpec as P

BF = jnp.bfloat16
F32 = jnp.float32
LANES = 128
NT = (((1,), (1,)), ((), ()))


def shift(x, amount, axis=1):
    size = x.shape[axis]
    amount %= size
    return x if amount == 0 else pltpu.roll(x, amount, axis)


def lane_iota(shape):
    return lax.broadcasted_iota(jnp.int32, shape, 1)


def pack_kernel(flags, fields, cot, mask, ft, gt, first, second, plane):
    chans, rows, _ = fields.shape
    groups = chans // 8
    sea = mask[...].astype(F32)
    for turn, dst in ((0, ft), (1, gt)):
        for c in range(chans):
            if turn == 0:
                cell = fields[c].astype(F32)
            else:
                cell = cot[c].astype(F32) * sea
            plane[turn, c * rows : (c + 1) * rows, :] = cell
        for r in range(rows):
            parts = [plane[turn, pl.ds(g * 8 * rows + r, 8, stride=rows), :] for g in range(groups)]
            dst[r] = jnp.concatenate(parts, axis=0).astype(BF)

    def edge(dst, top):
        base = rows - 6 if top else 0
        gbase = rows - 3 if top else 0
        dst[0:6] = ft[base : base + 6]
        dst[6:9] = gt[gbase : gbase + 3]

    @pl.when(flags[0] == 0)
    def _():
        edge(first, True)
        edge(second, False)

    @pl.when(flags[0] == 1)
    def _():
        edge(first, False)
        edge(second, True)


def edge_kernel(fold_first, flags, partner, got_a, got_b, got_c, ft, gt, low, up, sent_l, sent_r):
    rows, chans, cols = ft.shape

    @pl.when(flags[0] == 1)
    def _():
        low[...] = got_a[...]

    @pl.when(flags[0] == 0)
    def _():
        low[...] = got_b[...]

    @pl.when(flags[1] == 1)
    def _():
        got_1 = got_a if fold_first else got_b
        src = lax.broadcasted_iota(jnp.int32, (cols, cols), 0)
        want = jnp.broadcast_to(partner[...], (cols, cols))
        pick_1 = (src + flags[2] == want).astype(F32).astype(BF)
        pick_2 = (src + flags[3] == want).astype(F32).astype(BF)
        for k in range(9):
            m = 5 - k if k < 6 else 14 - k
            mixed = jnp.dot(got_1[m], pick_1, preferred_element_type=F32)
            mixed = mixed + jnp.dot(got_c[m], pick_2, preferred_element_type=F32)
            up[k] = mixed.astype(BF)

    @pl.when((flags[1] == 0) & (flags[0] == 0))
    def _():
        up[...] = got_a[...]

    @pl.when((flags[1] == 0) & (flags[0] == 1))
    def _():
        up[...] = got_b[...]

    lane = lane_iota((chans, LANES))
    acc = {key: jnp.zeros((chans, LANES), F32) for key in ((0, 0), (0, 1), (1, 0), (1, 1))}

    def place(side, value, source, lane_to, width):
        moved = shift(value, lane_to - source)
        for half in (0, 1):
            lo = max(lane_to - half * LANES, 0)
            hi = min(lane_to + width - half * LANES, LANES)
            if lo < hi:
                acc[side, half] = jnp.where((lane >= lo) & (lane < hi), moved, acc[side, half])

    for r in range(rows + 12):
        if r < 6:
            value = low[r]
        elif r < rows + 6:
            value = ft[r - 6]
        else:
            value = up[r - rows - 6]
        value = value.astype(F32)
        place(1, value, cols - 6, 9 * r, 6)
        place(0, value, 0, 9 * r + 3, 6)
    for r in range(rows + 6):
        if r < 3:
            value = low[6 + r]
        elif r < rows + 3:
            value = gt[r - 3]
        else:
            value = up[6 + r - rows - 3]
        value = value.astype(F32)
        place(1, value, cols - 3, 9 * r + 6, 3)
        place(0, value, 0, 9 * r, 3)
    for side, dst in ((0, sent_l), (1, sent_r)):
        dst[...] = jnp.concatenate([acc[side, 0], acc[side, 1]], axis=1).astype(BF)


def normal_terms(v):
    cdf = 0.5 * (1.0 + lax.erf(v * (1.0 / math.sqrt(2.0))))
    dens = jnp.exp(-0.5 * v * v) * (1.0 / math.sqrt(2.0 * math.pi))
    return cdf, dens


def main_kernel(
    ft,
    gt,
    low,
    up,
    sent_l,
    sent_r,
    got_l,
    got_r,
    mask,
    taps,
    taps_up,
    vecs,
    up_aug,
    up_t,
    down,
    down_t,
    out,
    grad,
    red,
    ext,
    side_in,
    side_s,
    moved,
    conv,
    cots,
    dconv,
    wide,
    wide_up,
    plane,
    g_down,
    g_up,
    sums,
):
    rows, chans, cols = ft.shape
    groups = chans // 8
    ext_rows = rows + 12
    mid_rows = rows + 6
    sides = mid_rows
    hidden_n = up_t.shape[1]

    for r in range(ext_rows):
        if r < 6:
            ext[r] = low[r].astype(F32)
        elif r < rows + 6:
            ext[r] = ft[r - 6].astype(F32)
        else:
            ext[r] = up[r - rows - 6].astype(F32)
    for r in range(rows):
        cots[r] = gt[r].astype(F32)
    for r in range(3):
        cots[rows + r] = low[6 + r].astype(F32)
        cots[rows + 3 + r] = up[6 + r].astype(F32)
    lane2 = lane_iota((chans, 2 * LANES))
    slot = lane2 % 9
    from_l = got_l[...].astype(F32)
    from_r = got_r[...].astype(F32)
    side_in[0] = jnp.where(slot < 6, from_l, shift(sent_l[...].astype(F32), 3))
    side_in[1] = jnp.where(slot >= 3, from_r, shift(sent_r[...].astype(F32), -3))
    valid = (slot < 3) & (lane2 < 9 * mid_rows)
    for side, value in ((0, shift(from_l, -6)), (1, from_r)):
        value = jnp.where(valid, value, 0.0)
        cots[sides + 2 * side] = value[:, :LANES]
        cots[sides + 2 * side + 1] = value[:, LANES:]

    lane = lane_iota((8, LANES))

    def row_slot(r):
        return rows + r if r < 3 else r - 3 if r < rows + 3 else r

    def edge_lanes(lo, hi, start):
        if start + 2 < LANES:
            return lo
        if start >= LANES:
            return hi
        return jnp.where(lane < 64, hi, lo)

    def neighbour(left, right, start):
        r_part = shift(edge_lanes(right[0], right[1], start), -start)
        l_part = shift(edge_lanes(left[0], left[1], start), LANES - 3 - start)
        return jnp.where(lane < 64, r_part, l_part)

    def slide(value, side, s):
        if s == 0:
            return value
        if s > 0:
            return shift(jnp.where(lane < s, side, value), -s)
        return shift(jnp.where(lane >= LANES + s, side, value), -s)

    def conv_group(g, _):
        at = pl.ds(pl.multiple_of(g * 8, 8), 8)
        plain = taps[at, :]
        turned = taps_up[at, :]
        for t in range(49):
            wide[t, at, :] = jnp.broadcast_to(plain[:, t : t + 1], (8, LANES))
            wide_up[t, at, :] = jnp.broadcast_to(turned[:, t : t + 1], (8, LANES))
        pair = [[side_in[s, at, 0:LANES], side_in[s, at, LANES : 2 * LANES]] for s in (0, 1)]
        for r in range(ext_rows):
            side_s[r] = neighbour(pair[0], pair[1], 9 * r + 3)
        acc = [None] * mid_rows
        for q in range(7):
            w = [wide[a * 7 + q, at, :] for a in range(7)]
            wu = [wide_up[a * 7 + q, at, :] for a in range(7)]
            for r in range(ext_rows):
                value = slide(ext[r, at, :], side_s[r], q - 3)
                moved[q, r, at, :] = value
                for a in range(7):
                    o = r - a
                    if 0 <= o < mid_rows:
                        term = value * (wu[a] if o >= rows + 3 else w[a])
                        acc[o] = term if acc[o] is None else acc[o] + term
        for o in range(mid_rows):
            conv[row_slot(o), at, :] = acc[o]
        first_up = 9 * (rows + 3)
        for side in (0, 1):
            lo, hi = pair[side]
            acc_lo = jnp.zeros((8, LANES), F32)
            acc_hi = jnp.zeros((8, LANES), F32)
            for a in range(7):
                for q in range(7):
                    d = 9 * a + q
                    r_lo, r_hi = shift(lo, -d), shift(hi, -d)
                    x_lo = r_lo if d == 0 else jnp.where(lane < LANES - d, r_lo, r_hi)
                    w = wide[a * 7 + q, at, :]
                    wu = wide_up[a * 7 + q, at, :]
                    acc_lo = acc_lo + x_lo * jnp.where(lane >= first_up, wu, w)
                    acc_hi = acc_hi + r_hi * jnp.where(lane >= first_up - LANES, wu, w)
            conv[sides + 2 * side, at, :] = acc_lo
            conv[sides + 2 * side + 1, at, :] = acc_hi
        return 0

    lax.fori_loop(0, groups, conv_group, 0)

    g_down[...] = jnp.zeros_like(g_down)
    g_up[...] = jnp.zeros_like(g_up)
    sums[...] = jnp.zeros_like(sums)
    pad_rows = up_aug.shape[1] - chans
    ones = (lax.broadcasted_iota(jnp.int32, (pad_rows, 2 * LANES), 0) == 0).astype(F32).astype(BF)

    def twice(x):
        return jnp.concatenate([x, x], axis=1)

    def pair_of(ref, u):
        return jnp.concatenate([ref[u], ref[u + 1]], axis=1)

    def block(u, own):
        gain, bias, scale = twice(vecs[0]), twice(vecs[1]), twice(vecs[2])
        x = pair_of(conv, u)
        centred = x - jnp.mean(x, axis=0, keepdims=True)
        var = jnp.mean(centred * centred, axis=0, keepdims=True)
        rstd = lax.rsqrt(var + 1e-06)
        xhat = centred * rstd
        normed = (xhat * gain + bias).astype(BF)
        normed = jnp.concatenate([normed, ones], axis=0)
        pre = jnp.dot(up_aug[...], normed, preferred_element_type=F32)
        cdf, dens = normal_terms(pre)
        g = pair_of(cots, u)
        d_branch = (g * scale).astype(BF)
        d_hidden = jnp.dot(down_t[...], d_branch, preferred_element_type=F32)
        d_pre = (d_hidden * (cdf + pre * dens)).astype(BF)
        d_normed = jnp.dot(up_t[...], d_pre, preferred_element_type=F32)
        if own:
            hidden = (pre * cdf).astype(BF)
            branch = jnp.dot(down[...], hidden, preferred_element_type=F32)
            sea = [mask[pl.ds(u + k, 1), :].astype(F32) for k in (0, 1)]
            fields = jnp.concatenate([ext[u + 6], ext[u + 7]], axis=1)
            res = (fields + scale * branch) * jnp.concatenate(sea, axis=1)
            for k in (0, 1):
                for gr in range(groups):
                    plane[0, pl.ds(gr * 8 * rows + u + k, 8, stride=rows), :] = res[
                        gr * 8 : gr * 8 + 8, k * LANES : (k + 1) * LANES
                    ]
            g_down[...] += lax.dot_general(d_branch, hidden, NT, preferred_element_type=F32)
            g_up[...] += lax.dot_general(normed, d_pre, NT, preferred_element_type=F32)
            for k, value in enumerate((d_normed * xhat, d_normed, g * branch)):
                sums[k] += value[:, :LANES] + value[:, LANES:]
        gd = d_normed * gain
        m1 = jnp.mean(gd, axis=0, keepdims=True)
        m2 = jnp.mean(gd * xhat, axis=0, keepdims=True)
        dx = (rstd * (gd - m1 - xhat * m2)).astype(BF).astype(F32)
        dconv[u] = dx[:, :LANES]
        dconv[u + 1] = dx[:, LANES:]

    def own_block(b, _):
        block(b * 2, True)
        return 0

    def halo_block(b, _):
        block(rows + b * 2, False)
        return 0

    lax.fori_loop(0, rows // 2, own_block, 0)
    lax.fori_loop(0, 5, halo_block, 0)

    def adjoint_group(g, _):
        at = pl.ds(pl.multiple_of(g * 8, 8), 8)
        pair = [[dconv[sides + 2 * s, at, :], dconv[sides + 2 * s + 1, at, :]] for s in (0, 1)]
        for r in range(mid_rows):
            side_s[r] = neighbour(pair[0], pair[1], 9 * r)
        acc = [None] * rows
        for q in range(7):
            w = [wide[(6 - a) * 7 + 6 - q, at, :] for a in range(7)]
            wu = [wide_up[(6 - a) * 7 + 6 - q, at, :] for a in range(7)]
            for r in range(mid_rows):
                value = slide(dconv[row_slot(r), at, :], side_s[r], q - 3)
                for a in range(7):
                    o = r - a
                    if 0 <= o < rows:
                        term = value * (wu[a] if r >= rows + 3 else w[a])
                        acc[o] = term if acc[o] is None else acc[o] + term
        for o in range(rows):
            plane[1, pl.ds(g * (8 * rows) + o, 8, stride=rows), :] = acc[o] + cots[o, at, :]
        line = jnp.zeros((8, LANES), F32)
        own = [dconv[o, at, :] for o in range(rows)]
        for q in range(7):
            tot = [None] * 7
            for r in range(mid_rows):
                value = moved[q, r + 3, at, :]
                for a in range(7):
                    o = r - a
                    if 0 <= o < rows:
                        term = value * own[o]
                        tot[a] = term if tot[a] is None else tot[a] + term
            for a in range(7):
                total = jnp.sum(tot[a], axis=1, keepdims=True)
                line = jnp.where(lane == a * 7 + q, total, line)
        for k in range(3):
            total = jnp.sum(sums[k, at, :], axis=1, keepdims=True)
            line = jnp.where(lane == 49 + k, total, line)
        red[pl.ds(pl.multiple_of(4 * chans + 16 + g * 8, 8), 8), :] = line
        return 0

    lax.fori_loop(0, groups, adjoint_group, 0)

    for h in range(hidden_n // LANES):
        red[h * chans : (h + 1) * chans, :] = g_down[:, h * LANES : (h + 1) * LANES]
        red[(2 + h) * chans : (3 + h) * chans, :] = g_up[0:chans, h * LANES : (h + 1) * LANES]
        red[4 * chans + 8 * h : 4 * chans + 8 * h + 8, :] = g_up[chans : chans + 8, h * LANES : (h + 1) * LANES]
    tail = 5 * chans + 16
    red[tail:, :] = jnp.zeros((red.shape[0] - tail, LANES), F32)
    for c in range(chans):
        out[c] = plane[0, c * rows : (c + 1) * rows, :].astype(BF)
        grad[c] = plane[1, c * rows : (c + 1) * rows, :].astype(BF)


def vmem(n):
    return [pl.BlockSpec(memory_space=pltpu.VMEM)] * n


def smem():
    return pl.BlockSpec(memory_space=pltpu.SMEM)


def shards(
    fields,
    cotangent,
    ocean_mask,
    seam_partner,
    depth_weight,
    norm_gain,
    layer_norm_bias,
    up_weight,
    up_bias,
    down_weight,
    layer_scale,
):
    _, chans, rows, cols = fields.shape
    hidden_n = up_weight.shape[0]
    n_lon, n_lat = lax.axis_size("lon"), lax.axis_size("lat")
    x, z = lax.axis_index("lon"), lax.axis_index("lat")
    odd = z % 2
    is_top = z == n_lat - 1
    sds = jax.ShapeDtypeStruct
    ft, gt, first, second = pl.pallas_call(
        pack_kernel,
        out_shape=[sds((rows, chans, cols), BF)] * 2 + [sds((9, chans, cols), BF)] * 2,
        in_specs=[smem()] + vmem(3),
        out_specs=vmem(4),
        scratch_shapes=[pltpu.VMEM((2, chans * rows, cols), F32)],
        name="pack",
    )(odd.astype(jnp.int32)[None], fields[0], cotangent[0], ocean_mask)

    at = lambda lon, lat: (lon % n_lon) * n_lat + lat
    rounds = [[], []]
    for lat in range(n_lat - 1):
        for lon in range(n_lon):
            rounds[lat % 2] += [(at(lon, lat), at(lon, lat + 1)), (at(lon, lat + 1), at(lon, lat))]
    fold_round = (n_lat - 1) % 2

    def exchange(k):
        def run(first, second):
            mirror = [
                [(at(lon, n_lat - 1), at(k - j - lon, n_lat - 1)) for lon in range(n_lon)] for j in (0, 1)
            ]
            plan = [list(rounds[0]), list(rounds[1])]
            plan[fold_round] += mirror[0]
            axes = ("lon", "lat")
            top = first if fold_round == 0 else second
            return (
                lax.ppermute(first, axes, plan[0]),
                lax.ppermute(second, axes, plan[1]),
                lax.ppermute(top, axes, mirror[1]),
            )

        return run

    turn = seam_partner[0] // cols
    got_a, got_b, got_c = lax.switch(turn, [exchange(k) for k in range(n_lon)], first, second)
    own_partner = lax.dynamic_slice_in_dim(seam_partner, x * cols, cols)[None]
    flags = jnp.stack(
        [
            odd,
            is_top.astype(jnp.int32),
            (turn - x) % n_lon * cols,
            (turn - 1 - x) % n_lon * cols,
        ]
    ).astype(jnp.int32)
    low, up, sent_l, sent_r = pl.pallas_call(
        functools.partial(edge_kernel, fold_round == 0),
        out_shape=[sds((9, chans, cols), BF)] * 2 + [sds((chans, 2 * cols), BF)] * 2,
        in_specs=[smem()] + vmem(6),
        out_specs=vmem(4),
        name="edges",
    )(flags, own_partner, got_a, got_b, got_c, ft, gt)
    got_l = lax.ppermute(sent_r, "lon", [(i, (i + 1) % n_lon) for i in range(n_lon)])
    got_r = lax.ppermute(sent_l, "lon", [(i, (i - 1) % n_lon) for i in range(n_lon)])

    flat = depth_weight.reshape(chans, 49).astype(F32)
    taps = jnp.pad(flat, ((0, 0), (0, LANES - 49)))
    taps_up = jnp.pad(jnp.where(is_top, flat[:, ::-1], flat), ((0, 0), (0, LANES - 49)))
    vecs = jnp.broadcast_to(
        jnp.stack([norm_gain, layer_norm_bias, layer_scale]).astype(F32)[:, :, None], (3, chans, LANES)
    )
    up_aug = jnp.concatenate(
        [up_weight, up_bias[:, None], jnp.zeros((hidden_n, 15), BF)], axis=1
    )
    units = rows + 10
    red_rows = 5 * chans + 32
    output, grad, red = pl.pallas_call(
        main_kernel,
        out_shape=[sds((chans, rows, cols), BF)] * 2 + [sds((red_rows, LANES), F32)],
        in_specs=vmem(16),
        out_specs=vmem(3),
        scratch_shapes=[
            pltpu.VMEM((rows + 12, chans, cols), F32),
            pltpu.VMEM((2, chans, 2 * cols), F32),
            pltpu.VMEM((rows + 12, 8, cols), F32),
            pltpu.VMEM((7, rows + 12, chans, cols), F32),
            pltpu.VMEM((units, chans, cols), F32),
            pltpu.VMEM((units, chans, cols), F32),
            pltpu.VMEM((units, chans, cols), F32),
            pltpu.VMEM((49, chans, LANES), F32),
            pltpu.VMEM((49, chans, LANES), F32),
            pltpu.VMEM((2, chans * rows, cols), F32),
            pltpu.VMEM((chans, hidden_n), F32),
            pltpu.VMEM((chans + 16, hidden_n), F32),
            pltpu.VMEM((3, chans, LANES), F32),
        ],
        name="block",
    )(
        ft,
        gt,
        low,
        up,
        sent_l,
        sent_r,
        got_l,
        got_r,
        ocean_mask,
        taps,
        taps_up,
        vecs,
        up_aug,
        up_weight.T,
        down_weight,
        down_weight.T,
    )

    half = red_rows // 2
    bit = x % 2
    kept = lax.dynamic_slice_in_dim(red, bit * half, half)
    passed = lax.dynamic_slice_in_dim(red, (1 - bit) * half, half)
    flip = lambda y, axis, b: lax.ppermute(y, axis, [(i, i ^ b) for i in range(lax.axis_size(axis))])
    total = kept + flip(passed, "lon", 1)
    for axis, b in [("lon", 1 << i) for i in range(1, n_lon.bit_length() - 1)] + [
        ("lat", 1 << i) for i in range(n_lat.bit_length() - 1)
    ]:
        total = total + flip(total, axis, b)
    other = flip(total, "lon", 1)
    summed = jnp.concatenate([jnp.where(bit == 0, total, other), jnp.where(bit == 0, other, total)], axis=0)
    down_g = jnp.concatenate([summed[:chans], summed[chans : 2 * chans]], axis=1)
    up_g = jnp.concatenate([summed[2 * chans : 3 * chans].T, summed[3 * chans : 4 * chans].T], axis=0)
    up_b_g = jnp.concatenate([summed[4 * chans], summed[4 * chans + 8]])
    small = summed[4 * chans + 16 : 5 * chans + 16]
    return (
        output[None],
        grad[None],
        small[:, :49].reshape(chans, 7, 7),
        small[:, 49],
        small[:, 50],
        up_g,
        up_b_g,
        down_g,
        small[:, 51],
    )


def solution(mesh):
    block = P(None, None, "lat", "lon")
    placed = (block, block, P("lat", "lon")) + (P(),) * 8
    return jax.shard_map(
        shards, mesh=mesh, in_specs=placed, out_specs=(block, block) + (P(),) * 7, check_vma=False
    )
```

time: 224 us -> 80.5 us (0.36)
  blocking collectives: 62.4 us -> 0 us
  waiting for transfers between devices: 54.5 us -> 18.6 us
  other arithmetic: 36.6 us -> 3.26 us
  Pallas kernels: 0 us -> 25.6 us
  matrix products: 15.3 us -> 0 us
  between operations: 16.3 us -> 3.43 us
  local copies, waits for them, and re-layouts: 20.1 us -> 10.2 us
    psum x1 -> x0, waiting for transfers between devices: 48.1 us -> none  [shards(): lax.psum((g_depth, gain_gradient, g_bias, g_up_w, g_up_b, g_down, g_scale...]
    psum x1 -> x0, blocking collectives: 41.6 us -> none  [shards(): lax.psum((g_depth, gain_gradient, g_bias, g_up_w, g_up_b, g_down, g_scale...]
    pallas_call x0 -> x3, Pallas kernels: none -> 25.6 us  [the longest x1 21 us: shards(): pl.pallas_call(main_kernel, out_shape=[sds((chans, rows, cols), BF)] * 2...]
    reduce_sum x7 -> x0, other arithmetic: 23 us -> none  [the longest x4 11.1 us: shards(): jnp.sum(d_conv_f * extended[:, :, row_tap:row_tap + rows, col_tap:col_tap...]
    all_gather x2 -> x0, blocking collectives: 20.8 us -> none  [the longest x1 10.4 us: shards(): lax.all_gather(margin.astype(jnp.bfloat16), 'lon', axis=3, tiled=True)]
    dot_general x6 -> x0, matrix products: 15.3 us -> none  [the longest x1 6.92 us: cell_terms(): jnp.dot(up_weight, normalized_output, preferred_element_type=jnp.float32)]
    ppermute x8 -> x11, waiting for transfers between devices: 6.45 us -> 18.6 us  [the longest x6 14.9 us: shards(): lax.ppermute(y, axis, [(i, i ^ b) for i in range(lax.axis_size(axis))])]
    add x1 -> x5, other arithmetic: 6.3 us -> 0.06 us  [the longest x4 0.05 us: shards(): total = total + flip(total, axis, b)]
  transfers between devices with their start and end apart: 9 -> 11, of which waited for: 3 -> 7; matrix products, arithmetic and copies ran while one was open for 12% -> 4% of each run, Pallas kernels for 0% -> 0%
where the time goes in v1:
time: 80.5 us; the launch traced here: 80 us
  Pallas kernels  25.6 us (32%)
  starting transfers between devices  18.9 us (23%)
  waiting for transfers between devices  18.6 us (23%)
  local copies, waits for them, and re-layouts  10.2 us (13%)
  between operations  3.43 us (4%)
  other arithmetic  3.26 us (4%)
    pallas_call x1, Pallas kernels, shards(): pl.pallas_call(main_kernel, out_shape=[sds((chans, rows, cols), BF)] * 2...  21 us
    ppermute x6, waiting for transfers between devices, shards(): lax.ppermute(y, axis, [(i, i ^ b) for i in range(lax.axis_size(axis))])  14.9 us
    ppermute x6, starting transfers between devices, shards(): lax.ppermute(y, axis, [(i, i ^ b) for i in range(lax.axis_size(axis))])  8.35 us
    ppermute x1, starting transfers between devices, run(): lax.ppermute(first, axes, plan[0])  5.23 us
    ppermute x1, waiting for transfers between devices, run(): lax.ppermute(first, axes, plan[0])  3.66 us
    unnamed x22, local copies, waits for them, and re-layouts  3 us
    ppermute x1, starting transfers between devices, shards(): lax.ppermute(sent_l, 'lon', [(i, (i - 1) % n_lon) for i in range(n_lon)])  2.64 us
    pallas_call x1, Pallas kernels, shards(): pl.pallas_call(functools.partial(edge_kernel, fold_round == 0), out_shape...  2.45 us
  transfers between devices with their start and end apart: 11, of which 7 were waited for; matrix products, arithmetic and copies ran while one was open for 4% of the time, Pallas kernels for 0%

profile of v1, /device:TPU:0, one launch (start us, length us, event | category | flops | bytes accessed | tf_op | source)
XLA Modules:
  0.0 80.0 jit_solution(16295710742686748874)
XLA Ops:
  0.6 1.2 %slice.38 = s32[1]{0:T(128)} slice(s32[1024]{0:T(1024)} %param.22), slice={[0:1]} | slice | bytes 8 | tf_op jit(solution)/shard_map/slice | solution.py:438
  4.5 1.3 %dynamic-slice_bitcast_fusion.partner = s32[1,128]{1,0:T(1,128)} fusion(s32[1024]{0:T(1024)} %param.22, s32[]{:T(128)S(6)} %select_n.56), kind=kLoop, calls=%fused_computation.18 | loop fusion | bytes 1028 | tf_op jit(solution)/shard_map/broadcast_in_dim | solution.py:440
  5.8 2.2 %pack.1 = (bf16[16,64,128]{2,1,0:T(8,128)(2,1)}, bf16[16,64,128]{2,1,0:T(8,128)(2,1)}, bf16[9,64,128]{2,1,0:T(8,128)(2,1)S(1)}, bf16[9,64,128]{2,1,0:T(8,128)(2,1)S(1)}) custom-call(s32[1]{0:T(128)} %bitcast.flags, bf16[64,16,128]{2,1,0:T(8,128)(2,1)} %bitcast.28, bf16[64,16,128]{2,1,0:T(8,128)(2,1)} %bitcast.29, s32[16,128]{1,0:T(8,128)} %mask.3), custom_call_target="tpu_custom_call" | custom-call | tf_op jit(solution)/shard_map/pack/pallas_call | solution.py:405
  8.0 11.5 %conditional.1 = (bf16[9,64,128]{2,1,0:T(8,128)(2,1)}, bf16[9,64,128]{2,1,0:T(8,128)(2,1)}, bf16[9,64,128]{2,1,0:T(8,128)(2,1)}) conditional(s32[]{:T(128)} %clamp.3, (bf16[9,64,128]{2,1,0:T(8,128)(2,1)S(1)}, bf16[9,64,128]{2,1,0:T(8,128)(2,1)S(1)}) %tuple.40, (bf16[9,64,128]{2,1,0:T(8,128)(2,1)S(1)}, ...), branch_computations={%region_0.1_spmd, %region_1.2_spmd, %region_2.3_spmd, %region_3.4_... | conditional | bytes 1769616 | solution.py:439
  8.0 1.3 %collective-permute-start.7 = (bf16[9,64,128]{2,1,0:T(8,128)(2,1)S(1)}, bf16[9,64,128]{2,1,0:T(8,128)(2,1)}, u32[]{:S(2)}, u32[]{:S(2)}) collective-permute-start(bf16[9,64,128]{2,1,0:T(8,128)(2,1)S(1)} %get-tuple-element.37), channel_id=1, source_target_pairs={{1,2},{2,1},{5,6},{6,5},{9,10},{10,9},{13,14},{14,13},{17,18},{18,... | collective-permute-start | bytes 442376 | tf_op jit(solution)/shard_map/cond/branch_2_fun/ppermute | solution.py:432
  9.3 1.3 %collective-permute-start.8 = (bf16[9,64,128]{2,1,0:T(8,128)(2,1)S(1)}, bf16[9,64,128]{2,1,0:T(8,128)(2,1)}, u32[]{:S(2)}, u32[]{:S(2)}) collective-permute-start(bf16[9,64,128]{2,1,0:T(8,128)(2,1)S(1)} %get-tuple-element.37), channel_id=1, source_target_pairs={{3,7},{7,3},{11,31},{15,27},{19,23},{23,19},{27,15},{31,11}} | collective-permute-start | bytes 442376 | tf_op jit(solution)/shard_map/cond/branch_2_fun/ppermute | solution.py:433
  10.6 5.2 %collective-permute-start.6 = (bf16[9,64,128]{2,1,0:T(8,128)(2,1)S(1)}, bf16[9,64,128]{2,1,0:T(8,128)(2,1)}, u32[]{:S(2)}, u32[]{:S(2)}) collective-permute-start(bf16[9,64,128]{2,1,0:T(8,128)(2,1)S(1)} %get-tuple-element.36), channel_id=1, source_target_pairs={{0,1},{1,0},{4,5},{5,4},{8,9},{9,8},{12,13},{13,12},{16,17},{17,16... | collective-permute-start | bytes 442376 | tf_op jit(solution)/shard_map/cond/branch_2_fun/ppermute | solution.py:431
  15.8 3.7 %collective-permute-done.6 = bf16[9,64,128]{2,1,0:T(8,128)(2,1)} collective-permute-done((bf16[9,64,128]{2,1,0:T(8,128)(2,1)S(1)}, bf16[9,64,128]{2,1,0:T(8,128)(2,1)}, u32[]{:S(2)}, u32[]{:S(2)}) %collective-permute-start.6) | collective-permute-done | bytes 147488 | tf_op jit(solution)/shard_map/cond/branch_2_fun/ppermute | solution.py:431
  20.1 2.4 %edges.1 = (bf16[9,64,128]{2,1,0:T(8,128)(2,1)}, bf16[9,64,128]{2,1,0:T(8,128)(2,1)}, bf16[64,256]{1,0:T(8,128)(2,1)}, bf16[64,256]{1,0:T(8,128)(2,1)}) custom-call(s32[4]{0:T(128)} %pad_add_fusion.flags, s32[1,128]{1,0:T(1,128)} %dynamic-slice_bitcast_fusion.partner, bf16[9,64,128]{2,1,0:T(8,128)(2,1)} %get-tuple-element.75.got_a, ...), custom_call_target="tpu_custom_call" | custom-call | tf_op jit(solution)/shard_map/edges/pallas_call | solution.py:449
  22.6 2.6 %collective-permute-start.25 = (bf16[64,256]{1,0:T(8,128)(2,1)}, bf16[64,256]{1,0:T(8,128)(2,1)S(1)}, u32[]{:S(2)}, u32[]{:S(2)}) collective-permute-start(bf16[64,256]{1,0:T(8,128)(2,1)} %get-tuple-element.80.sent_l), channel_id=1, source_target_pairs={{0,28},{4,0},{8,4},{12,8},{16,12},{20,16},{24,20},{28,24},{1,29},{... | collective-permute-start | bytes 98312 | tf_op jit(solution)/shard_map/ppermute | solution.py:457
  25.4 0.6 copy-done.6
  26.1 0.7 copy-done.1
  27.0 0.7 maximum_maximum_fusion.up_aug
  27.7 0.6 copy-done.7
  29.8 0.7 copy.29
  30.5 0.7 broadcast_in_dim.26.vecs
  31.3 21.0 %block.1 = (bf16[64,16,128]{2,1,0:T(8,128)(2,1)}, bf16[64,16,128]{2,1,0:T(8,128)(2,1)}, f32[352,128]{1,0:T(8,128)}) custom-call(bf16[16,64,128]{2,1,0:T(8,128)(2,1)} %get-tuple-element.71.ft, bf16[16,64,128]{2,1,0:T(8,128)(2,1)} %get-tuple-element.72.gt, bf16[9,64,128]{2,1,0:T(8,128)(2,1)} %get-tuple-element.78.low, ...), custom_call_target="tpu_custom_call" | custom-call | tf_op jit(solution)/shard_map/block/pallas_call | solution.py:470
  52.3 1.0 %constant_dynamic-slice_fusion = f32[176,128]{1,0:T(8,128)S(1)} fusion(f32[352,128]{1,0:T(8,128)} %get-tuple-element.84, s32[]{:T(128)S(6)} %select_n.62), kind=kLoop, calls=%fused_computation.19 | loop fusion | bytes 180228 | tf_op jit(solution)/shard_map/dynamic_slice | solution.py:513
  53.3 1.3 %collective-permute-done.26 = f32[176,128]{1,0:T(8,128)S(1)} collective-permute-done((f32[176,128]{1,0:T(8,128)S(1)}, f32[176,128]{1,0:T(8,128)S(1)}, u32[]{:S(2)}, u32[]{:S(2)}) %collective-permute-start.26) | collective-permute-done | bytes 90144 | tf_op jit(solution)/shard_map/ppermute | solution.py:514
  54.6 0.7 collective-permute-start.27
  55.2 4.1 %collective-permute-done.27 = f32[176,128]{1,0:T(8,128)S(1)} collective-permute-done((f32[176,128]{1,0:T(8,128)S(1)}, f32[176,128]{1,0:T(8,128)S(1)}, u32[]{:S(2)}, u32[]{:S(2)}) %collective-permute-start.27) | collective-permute-done | bytes 90144 | tf_op jit(solution)/shard_map/ppermute | solution.py:514
  59.3 1.6 %collective-permute-start.28 = (f32[176,128]{1,0:T(8,128)S(1)}, f32[176,128]{1,0:T(8,128)S(1)}, u32[]{:S(2)}, u32[]{:S(2)}) collective-permute-start(f32[176,128]{1,0:T(8,128)S(1)} %add.51), channel_id=1, source_target_pairs={{0,16},{4,20},{8,24},{12,28},{16,0},{20,4},{24,8},{28,12},{1,17},{... | collective-permute-start | bytes 270344 | tf_op jit(solution)/shard_map/ppermute | solution.py:514
  60.9 3.0 %collective-permute-done.28 = f32[176,128]{1,0:T(8,128)S(1)} collective-permute-done((f32[176,128]{1,0:T(8,128)S(1)}, f32[176,128]{1,0:T(8,128)S(1)}, u32[]{:S(2)}, u32[]{:S(2)}) %collective-permute-start.28) | collective-permute-done | bytes 90144 | tf_op jit(solution)/shard_map/ppermute | solution.py:514
  63.9 1.8 %collective-permute-start.29 = (f32[176,128]{1,0:T(8,128)S(1)}, f32[176,128]{1,0:T(8,128)S(1)}, u32[]{:S(2)}, u32[]{:S(2)}) collective-permute-start(f32[176,128]{1,0:T(8,128)S(1)} %add.52), channel_id=1, source_target_pairs={{0,1},{1,0},{2,3},{3,2},{4,5},{5,4},{6,7},{7,6},{8,9},{9,8},{10,11... | collective-permute-start | bytes 270344 | tf_op jit(solution)/shard_map/ppermute | solution.py:514
  65.7 2.8 %collective-permute-done.29 = f32[176,128]{1,0:T(8,128)S(1)} collective-permute-done((f32[176,128]{1,0:T(8,128)S(1)}, f32[176,128]{1,0:T(8,128)S(1)}, u32[]{:S(2)}, u32[]{:S(2)}) %collective-permute-start.29) | collective-permute-done | bytes 90144 | tf_op jit(solution)/shard_map/ppermute | solution.py:514
  68.5 4.2 %collective-permute-start.30 = (f32[176,128]{1,0:T(8,128)S(1)}, f32[176,128]{1,0:T(8,128)S(1)}, u32[]{:S(2)}, u32[]{:S(2)}) collective-permute-start(f32[176,128]{1,0:T(8,128)S(1)} %add.53), channel_id=1, source_target_pairs={{0,2},{1,3},{2,0},{3,1},{4,6},{5,7},{6,4},{7,5},{8,10},{9,11},{10,... | collective-permute-start | bytes 270344 | tf_op jit(solution)/shard_map/ppermute | solution.py:514
  72.8 2.5 %collective-permute-done.30 = f32[176,128]{1,0:T(8,128)S(1)} collective-permute-done((f32[176,128]{1,0:T(8,128)S(1)}, f32[176,128]{1,0:T(8,128)S(1)}, u32[]{:S(2)}, u32[]{:S(2)}) %collective-permute-start.30) | collective-permute-done | bytes 90144 | tf_op jit(solution)/shard_map/ppermute | solution.py:514
  75.4 1.3 %collective-permute-done.31 = f32[176,128]{1,0:T(8,128)S(1)} collective-permute-done((f32[176,128]{1,0:T(8,128)S(1)}, f32[176,128]{1,0:T(8,128)S(1)}, u32[]{:S(2)}, u32[]{:S(2)}) %collective-permute-start.31) | collective-permute-done | bytes 90144 | tf_op jit(solution)/shard_map/ppermute | solution.py:514
  76.7 0.7 slice_reduce_fusion
  77.5 0.6 reshape.49
  78.2 0.6 pad_maximum_fusion.1
  79.4 0.6 pad_maximum_fusion
  (47 shorter events, 3.3 us)
Async XLA Ops:
  8.0 7.9 %collective-permute-start.7 = (bf16[9,64,128]{2,1,0:T(8,128)(2,1)S(1)}, bf16[9,64,128]{2,1,0:T(8,128)(2,1)}, u32[]{:S(2)}, u32[]{:S(2)}) collective-permute-start(bf16[9,64,128]{2,1,0:T(8,128)(2,1)S(1)} %get-tuple-element.37), channel_id=1, source_target_pairs={{1,2},{2,1},{5,6},{6,5},{9,10},{10,9},{13,14},{14,13},{17,18},{18,... | collective-permute-start | bytes 442376 | tf_op jit(solution)/shard_map/cond/branch_2_fun/ppermute | solution.py:432
  9.3 6.6 %collective-permute-start.8 = (bf16[9,64,128]{2,1,0:T(8,128)(2,1)S(1)}, bf16[9,64,128]{2,1,0:T(8,128)(2,1)}, u32[]{:S(2)}, u32[]{:S(2)}) collective-permute-start(bf16[9,64,128]{2,1,0:T(8,128)(2,1)S(1)} %get-tuple-element.37), channel_id=1, source_target_pairs={{3,7},{7,3},{11,31},{15,27},{19,23},{23,19},{27,15},{31,11}} | collective-permute-start | bytes 442376 | tf_op jit(solution)/shard_map/cond/branch_2_fun/ppermute | solution.py:433
  10.6 8.9 %collective-permute-start.6 = (bf16[9,64,128]{2,1,0:T(8,128)(2,1)S(1)}, bf16[9,64,128]{2,1,0:T(8,128)(2,1)}, u32[]{:S(2)}, u32[]{:S(2)}) collective-permute-start(bf16[9,64,128]{2,1,0:T(8,128)(2,1)S(1)} %get-tuple-element.36), channel_id=1, source_target_pairs={{0,1},{1,0},{4,5},{5,4},{8,9},{9,8},{12,13},{13,12},{16,17},{17,16... | collective-permute-start | bytes 442376 | tf_op jit(solution)/shard_map/cond/branch_2_fun/ppermute | solution.py:431
  20.1 5.1 %copy-start.5 = (bf16[64,7,7]{0,2,1:T(8,128)(2,1)S(1)}, bf16[64,7,7]{0,2,1:T(8,128)(2,1)}, u32[]{:S(2)}) copy-start(bf16[64,7,7]{0,2,1:T(8,128)(2,1)} %param.23) | copy-start | bytes 18820
  22.6 8.0 %collective-permute-start.24 = (bf16[64,256]{1,0:T(8,128)(2,1)}, bf16[64,256]{1,0:T(8,128)(2,1)S(1)}, u32[]{:S(2)}, u32[]{:S(2)}) collective-permute-start(bf16[64,256]{1,0:T(8,128)(2,1)} %get-tuple-element.81.sent_r), channel_id=1, source_target_pairs={{0,4},{4,8},{8,12},{12,16},{16,20},{20,24},{24,28},{28,0},{1,5},{5... | collective-permute-start | bytes 98312 | tf_op jit(solution)/shard_map/ppermute | solution.py:456
  22.6 8.0 %collective-permute-start.25 = (bf16[64,256]{1,0:T(8,128)(2,1)}, bf16[64,256]{1,0:T(8,128)(2,1)S(1)}, u32[]{:S(2)}, u32[]{:S(2)}) collective-permute-start(bf16[64,256]{1,0:T(8,128)(2,1)} %get-tuple-element.80.sent_l), channel_id=1, source_target_pairs={{0,28},{4,0},{8,4},{12,8},{16,12},{20,16},{24,20},{28,24},{1,29},{... | collective-permute-start | bytes 98312 | tf_op jit(solution)/shard_map/ppermute | solution.py:457
  25.4 0.7 copy-start.6
  26.0 0.8 copy-start.1
  27.7 0.7 copy-start.7
  27.7 0.7 copy-start.8
  27.7 0.7 copy-start.9
  29.0 0.8 copy-start.2
  30.5 0.7 copy-start.3
  30.5 0.7 copy-start.4
  52.3 2.3 %copy-start = (f32[352,128]{1,0:T(8,128)S(1)}, f32[352,128]{1,0:T(8,128)}, u32[]{:S(2)}) copy-start(f32[352,128]{1,0:T(8,128)} %get-tuple-element.84) | copy-start | bytes 540676
  53.2 1.3 %collective-permute-start.26 = (f32[176,128]{1,0:T(8,128)S(1)}, f32[176,128]{1,0:T(8,128)S(1)}, u32[]{:S(2)}, u32[]{:S(2)}) collective-permute-start(f32[176,128]{1,0:T(8,128)S(1)} %constant_dynamic-slice_fusion), channel_id=1, source_target_pairs={{0,4},{4,0},{8,12},{12,8},{16,20},{20,16},{24,28},{28,24},{1,5},{5... | collective-permute-start | bytes 270344 | tf_op jit(solution)/shard_map/ppermute | solution.py:514
  54.6 4.7 %collective-permute-start.27 = (f32[176,128]{1,0:T(8,128)S(1)}, f32[176,128]{1,0:T(8,128)S(1)}, u32[]{:S(2)}, u32[]{:S(2)}) collective-permute-start(f32[176,128]{1,0:T(8,128)S(1)} %dynamic-slice_add_fusion), channel_id=1, source_target_pairs={{0,8},{4,12},{8,0},{12,4},{16,24},{20,28},{24,16},{28,20},{1,9},{5... | collective-permute-start | bytes 270344 | tf_op jit(solution)/shard_map/ppermute | solution.py:514
  59.3 4.6 %collective-permute-start.28 = (f32[176,128]{1,0:T(8,128)S(1)}, f32[176,128]{1,0:T(8,128)S(1)}, u32[]{:S(2)}, u32[]{:S(2)}) collective-permute-start(f32[176,128]{1,0:T(8,128)S(1)} %add.51), channel_id=1, source_target_pairs={{0,16},{4,20},{8,24},{12,28},{16,0},{20,4},{24,8},{28,12},{1,17},{... | collective-permute-start | bytes 270344 | tf_op jit(solution)/shard_map/ppermute | solution.py:514
  63.9 4.6 %collective-permute-start.29 = (f32[176,128]{1,0:T(8,128)S(1)}, f32[176,128]{1,0:T(8,128)S(1)}, u32[]{:S(2)}, u32[]{:S(2)}) collective-permute-start(f32[176,128]{1,0:T(8,128)S(1)} %add.52), channel_id=1, source_target_pairs={{0,1},{1,0},{2,3},{3,2},{4,5},{5,4},{6,7},{7,6},{8,9},{9,8},{10,11... | collective-permute-start | bytes 270344 | tf_op jit(solution)/shard_map/ppermute | solution.py:514
  68.5 6.7 %collective-permute-start.30 = (f32[176,128]{1,0:T(8,128)S(1)}, f32[176,128]{1,0:T(8,128)S(1)}, u32[]{:S(2)}, u32[]{:S(2)}) collective-permute-start(f32[176,128]{1,0:T(8,128)S(1)} %add.53), channel_id=1, source_target_pairs={{0,2},{1,3},{2,0},{3,1},{4,6},{5,7},{6,4},{7,5},{8,10},{9,11},{10,... | collective-permute-start | bytes 270344 | tf_op jit(solution)/shard_map/ppermute | solution.py:514
  75.3 1.4 %collective-permute-start.31 = (f32[176,128]{1,0:T(8,128)S(1)}, f32[176,128]{1,0:T(8,128)S(1)}, u32[]{:S(2)}, u32[]{:S(2)}) collective-permute-start(f32[176,128]{1,0:T(8,128)S(1)} %add.54), channel_id=1, source_target_pairs={{0,4},{4,0},{8,12},{12,8},{16,20},{20,16},{24,28},{28,24},{1,5},{5... | collective-permute-start | bytes 270344 | tf_op jit(solution)/shard_map/ppermute | solution.py:514

commit v2 on v1

v2 whole, which is shorter than its diff:
```python
import functools
import math

import jax
import jax.numpy as jnp
from jax import lax
from jax.experimental import pallas as pl
from jax.experimental.pallas import tpu as pltpu
from jax.sharding import PartitionSpec as P

BF = jnp.bfloat16
F32 = jnp.float32
LANES = 128
NT = (((1,), (1,)), ((), ()))


def shift(x, amount, axis=1):
    size = x.shape[axis]
    amount %= size
    return x if amount == 0 else pltpu.roll(x, amount, axis)


def lane_iota(shape):
    return lax.broadcasted_iota(jnp.int32, shape, 1)


def pack_kernel(fields, cot, mask, ft, gt, first, second, plane):
    chans, rows, _ = fields.shape
    groups = chans // 8
    sea = mask[...].astype(F32)
    for turn, dst in ((0, ft), (1, gt)):
        for c in range(chans):
            if turn == 0:
                cell = fields[c].astype(F32)
            else:
                cell = cot[c].astype(F32) * sea
            plane[turn, c * rows : (c + 1) * rows, :] = cell
        for r in range(rows):
            parts = [plane[turn, pl.ds(g * 8 * rows + r, 8, stride=rows), :] for g in range(groups)]
            dst[r] = jnp.concatenate(parts, axis=0).astype(BF)

    def edge(dst, top):
        base = rows - 6 if top else 0
        gbase = rows - 3 if top else 0
        dst[0:6] = ft[base : base + 6]
        dst[6:9] = gt[gbase : gbase + 3]

    odd = lax.axis_index("lat") % 2

    @pl.when(odd == 0)
    def _():
        edge(first, True)
        edge(second, False)

    @pl.when(odd == 1)
    def _():
        edge(first, False)
        edge(second, True)


def field_lane(r):
    return LANES * (r // 14) + 6 * (r % 14)


def cot_lane(g):
    return LANES * (g // 11) + 84 + 3 * (g % 11)


def edge_kernel(fold_first, seam, partner, got_a, got_b, got_c, ft, gt, low, up, sent_l, sent_r):
    rows, chans, cols = ft.shape
    n_lon = partner.shape[0]
    x = lax.axis_index("lon")
    z = lax.axis_index("lat")
    odd = z % 2
    top = z == lax.axis_size("lat") - 1

    @pl.when(odd == 1)
    def _():
        low[...] = got_a[...]

    @pl.when(odd == 0)
    def _():
        low[...] = got_b[...]

    @pl.when(top)
    def _():
        got_1 = got_a if fold_first else got_b
        src = lax.broadcasted_iota(jnp.int32, (cols, cols), 0)
        want = jnp.broadcast_to(partner[pl.ds(x, 1), :], (cols, cols))
        near = (seam[0] // cols - x + n_lon) % n_lon
        far = (near + n_lon - 1) % n_lon
        pick_1 = (src + near * cols == want).astype(F32).astype(BF)
        pick_2 = (src + far * cols == want).astype(F32).astype(BF)
        for k in range(9):
            m = 5 - k if k < 6 else 14 - k
            mixed = jnp.dot(got_1[m], pick_1, preferred_element_type=F32)
            mixed = mixed + jnp.dot(got_c[m], pick_2, preferred_element_type=F32)
            up[k] = mixed.astype(BF)

    @pl.when(jnp.logical_not(top) & (odd == 0))
    def _():
        up[...] = got_a[...]

    @pl.when(jnp.logical_not(top) & (odd == 1))
    def _():
        up[...] = got_b[...]

    lane = lane_iota((chans, LANES))
    acc = {key: jnp.zeros((chans, LANES), F32) for key in ((0, 0), (0, 1), (1, 0), (1, 1))}

    def place(side, value, source, lane_to, width):
        half, at = lane_to // LANES, lane_to % LANES
        moved = shift(value, at - source)
        acc[side, half] = jnp.where((lane >= at) & (lane < at + width), moved, acc[side, half])

    for r in range(rows + 12):
        if r < 6:
            value = low[r]
        elif r < rows + 6:
            value = ft[r - 6]
        else:
            value = up[r - rows - 6]
        value = value.astype(F32)
        place(1, value, cols - 6, field_lane(r), 6)
        place(0, value, 0, field_lane(r), 6)
    for r in range(rows + 6):
        if r < 3:
            value = low[6 + r]
        elif r < rows + 3:
            value = gt[r - 3]
        else:
            value = up[6 + r - rows - 3]
        value = value.astype(F32)
        place(1, value, cols - 3, cot_lane(r), 3)
        place(0, value, 0, cot_lane(r), 3)
    for side, dst in ((0, sent_l), (1, sent_r)):
        dst[...] = jnp.concatenate([acc[side, 0], acc[side, 1]], axis=1).astype(BF)


def weight_kernel(taps, gain, bias, scale, up_b, up_t, down, plain, turned, vecs, up_aug, down_t, line):
    chans, hidden_n = up_t.shape
    line[...] = jnp.zeros_like(line)
    for a in range(7):
        block = taps[a].astype(F32)
        for q in range(7):
            line[0, q, 8 * a : 8 * a + 1, 0:chans] = block[q : q + 1]
            line[1, 6 - q, 48 - 8 * a : 49 - 8 * a, 0:chans] = block[q : q + 1]
    for q in range(7):
        plain[q] = line[0, q].T[:chans]
        turned[q] = line[1, q].T[:chans]
    wide = LANES - chans
    columns = jnp.concatenate(
        [v[...].astype(F32).reshape(1, chans) for v in (gain, bias, scale)] + [jnp.zeros((5, chans), F32)],
        axis=0,
    )
    columns = jnp.concatenate([columns, jnp.zeros((8, wide), F32)], axis=1).T
    for k in range(3):
        vecs[k] = jnp.broadcast_to(columns[:chans, k : k + 1], (chans, LANES))
    tall = jnp.concatenate(
        [
            up_t[...].astype(F32),
            up_b[...].astype(F32).reshape(1, hidden_n),
            jnp.zeros((wide - 1, hidden_n), F32),
        ],
        axis=0,
    )
    up_aug[...] = tall.T[:, : chans + 16].astype(BF)
    tall = jnp.concatenate([down[...].astype(F32), jnp.zeros((wide, hidden_n), F32)], axis=0)
    down_t[...] = tall.T[:, :chans].astype(BF)


def normal_terms(v):
    cdf = 0.5 * (1.0 + lax.erf(v * (1.0 / math.sqrt(2.0))))
    dens = jnp.exp(-0.5 * v * v) * (1.0 / math.sqrt(2.0 * math.pi))
    return cdf, dens


def main_kernel(
    ft,
    gt,
    low,
    up,
    got_l,
    got_r,
    mask,
    plain,
    turned,
    vecs,
    up_aug,
    up_t,
    down,
    down_t,
    out,
    grad,
    kept,
    passed,
    ext,
    rim,
    rhs,
    conv,
    cots,
    dcv,
    plane,
    band,
    band_up,
    prod_1,
    prod_2,
    prod_3,
    g_down,
    g_up,
    sums,
    taps_g,
):
    rows, chans, cols = ft.shape
    groups = chans // 8
    mid = rows + 6
    odd_core = lax.axis_index("lon") % 2
    top = lax.axis_index("lat") == lax.axis_size("lat") - 1
    lane = lane_iota((8, LANES))
    wide = slice(0, LANES), slice(LANES, 2 * LANES)

    for r in range(rows):
        cots[(r + 3) * chans : (r + 4) * chans, :] = gt[r].astype(F32)
    for r in range(3):
        cots[r * chans : (r + 1) * chans, :] = low[6 + r].astype(F32)
        cots[(rows + 3 + r) * chans : (rows + 4 + r) * chans, :] = up[6 + r].astype(F32)
    lane_c = lane_iota((chans, LANES))
    for k, got in ((0, got_l), (1, got_r)):
        first = shift(got[:, wide[0]].astype(F32), -84)
        second = shift(got[:, wide[1]].astype(F32), 33 - 84)
        value = jnp.where(lane_c < 33, first, jnp.where(lane_c < 3 * mid, second, 0.0))
        cots[(mid + k) * chans : (mid + k + 1) * chans, :] = value

    def edge_mask(s):
        return lane < s if s > 0 else lane >= LANES + s

    def at_row(r, g):
        return pl.ds(pl.multiple_of(r * chans + g * 8, 8), 8)

    def conv_group(g, _):
        at = pl.ds(pl.multiple_of(g * 8, 8), 8)
        left = [got_l[at, w].astype(F32) for w in wide]
        right = [got_r[at, w].astype(F32) for w in wide]
        for r0 in range(0, rows + 12, 2):
            pair = []
            for r in (r0, r0 + 1):
                if r < 6:
                    value = low[r, at, :]
                elif r < rows + 6:
                    value = ft[r - 6, at, :]
                else:
                    value = up[r - rows - 6, at, :]
                value = value.astype(F32)
                half, start = field_lane(r) // LANES, field_lane(r) % LANES
                beyond = jnp.where(lane < 64, shift(right[half], -start), shift(left[half], LANES - 6 - start))
                ext[at_row(r, g), :] = value
                rim[at_row(r, g), :] = beyond
                pair.append(jnp.concatenate([value, beyond], axis=1))
            rhs[8 * r0 : 8 * r0 + 16, :] = jnp.concatenate(pair, axis=0).astype(BF)
        for q in range(7):
            one, two = plain[q, at, :], turned[q, at, :]
            above = jnp.where(top, two, one)
            band[q * 80 : q * 80 + 80, :] = jnp.concatenate(
                [pltpu.roll(one, 8 * i, 1, stride=1, stride_axis=0) for i in range(10)], axis=0
            ).astype(BF)
            band_up[q * 32 : q * 32 + 32, :] = jnp.concatenate(
                [pltpu.roll(above, 8 * i, 1, stride=1, stride_axis=0) for i in range(6, 10)], axis=0
            ).astype(BF)
        prod_1[...] = jnp.dot(band[...], rhs[0:128, :], preferred_element_type=F32)
        prod_2[...] = jnp.dot(band[...], rhs[80:208, :], preferred_element_type=F32)
        prod_3[0:224, :] = jnp.dot(band_up[0:224, :], rhs[96:224, :], preferred_element_type=F32)
        sides = [jnp.zeros((8, LANES), F32)] * 2
        for o in range(mid):
            if o < 10:
                prod, step, i = prod_1, 80, o
            elif o < rows + 3:
                prod, step, i = prod_2, 80, o - 10
            else:
                prod, step, i = prod_3, 32, o - 18
            inner = outer = None
            for q in range(7):
                part = slice(q * step + 8 * i, q * step + 8 * i + 8)
                mine, edge = prod[part, wide[0]], prod[part, wide[1]]
                if q != 3:
                    swap = edge_mask(q - 3)
                    mine, edge = jnp.where(swap, edge, mine), jnp.where(swap, mine, edge)
                    mine, edge = shift(mine, 3 - q), shift(edge, 3 - q)
                inner = mine if inner is None else inner + mine
                outer = edge if outer is None else outer + edge
            conv[at_row(o, g), :] = inner
            inside = (lane >= 3 * o) & (lane < 3 * o + 3)
            sides[0] = jnp.where(inside, shift(outer, 3 * o + 3), sides[0])
            sides[1] = jnp.where(inside, shift(outer, 3 * o), sides[1])
        for k in (0, 1):
            conv[at_row(mid + k, g), :] = sides[k]
        return 0

    lax.fori_loop(0, groups, conv_group, 0)

    g_down[...] = jnp.zeros_like(g_down)
    g_up[...] = jnp.zeros_like(g_up)
    sums[...] = jnp.zeros_like(sums)
    pad_rows = up_aug.shape[1] - chans
    ones = (lax.broadcasted_iota(jnp.int32, (pad_rows, 2 * LANES), 0) == 0).astype(F32).astype(BF)

    def twice(x):
        return jnp.concatenate([x, x], axis=1)

    def unit(u):
        return pl.ds(pl.multiple_of(u * chans, chans), chans)

    def pair_of(ref, units):
        return jnp.concatenate([ref[unit(u), :] for u in units], axis=1)

    def block(units, own):
        gain, bias, scale = twice(vecs[0]), twice(vecs[1]), twice(vecs[2])
        x = pair_of(conv, units)
        centred = x - jnp.mean(x, axis=0, keepdims=True)
        var = jnp.mean(centred * centred, axis=0, keepdims=True)
        rstd = lax.rsqrt(var + 1e-06)
        xhat = centred * rstd
        normed = (xhat * gain + bias).astype(BF)
        normed = jnp.concatenate([normed, ones], axis=0)
        pre = jnp.dot(up_aug[...], normed, preferred_element_type=F32)
        cdf, dens = normal_terms(pre)
        g = pair_of(cots, units)
        d_branch = (g * scale).astype(BF)
        d_hidden = jnp.dot(down_t[...], d_branch, preferred_element_type=F32)
        d_pre = (d_hidden * (cdf + pre * dens)).astype(BF)
        d_normed = jnp.dot(up_t[...], d_pre, preferred_element_type=F32)
        if own:
            hidden = (pre * cdf).astype(BF)
            branch = jnp.dot(down[...], hidden, preferred_element_type=F32)
            sea = [mask[pl.ds(u - 3, 1), :].astype(F32) for u in units]
            fields = jnp.concatenate([ext[unit(u + 3), :] for u in units], axis=1)
            res = (fields + scale * branch) * jnp.concatenate(sea, axis=1)
            for k, u in enumerate(units):
                for gr in range(groups):
                    plane[0, pl.ds(gr * 8 * rows + u - 3, 8, stride=rows), :] = res[gr * 8 : gr * 8 + 8, wide[k]]
            g_down[...] += lax.dot_general(d_branch, hidden, NT, preferred_element_type=F32)
            g_up[...] += lax.dot_general(normed, d_pre, NT, preferred_element_type=F32)
            for k, value in enumerate((d_normed * xhat, d_normed, g * branch)):
                sums[k] += value[:, :LANES] + value[:, LANES:]
        gd = d_normed * gain
        m1 = jnp.mean(gd, axis=0, keepdims=True)
        m2 = jnp.mean(gd * xhat, axis=0, keepdims=True)
        dx = (rstd * (gd - m1 - xhat * m2)).astype(BF).astype(F32)
        for k, u in enumerate(units):
            dcv[unit(u), :] = dx[:, wide[k]]

    def own_block(b, _):
        block((b * 2 + 3, b * 2 + 4), True)
        return 0

    def halo_block(b, _):
        one = jnp.where(b < 2, 2 * b, rows + 2 * b)
        two = jnp.where(b == 0, 1, rows + 1 + 2 * b)
        block((one, two), False)
        return 0

    lax.fori_loop(0, rows // 2, own_block, 0)
    lax.fori_loop(0, 4, halo_block, 0)

    def adjoint_group(g, _):
        at = pl.ds(pl.multiple_of(g * 8, 8), 8)
        left, right = dcv[at_row(mid, g), :], dcv[at_row(mid + 1, g), :]
        for r0 in range(0, mid, 2):
            pair = []
            for r in (r0, r0 + 1):
                value = dcv[at_row(r, g), :]
                beyond = jnp.where(lane < 64, shift(right, -3 * r), shift(left, LANES - 3 - 3 * r))
                pair.append(jnp.concatenate([value, beyond], axis=1))
            rhs[8 * r0 : 8 * r0 + 16, :] = jnp.concatenate(pair, axis=0).astype(BF)
        for q in range(7):
            one, two = turned[q, at, :], plain[q, at, :]
            above = jnp.where(top, two, one)
            moved = [pltpu.roll(one, 8 * i, 1, stride=1, stride_axis=0) for i in range(10)]
            band[q * 80 : q * 80 + 80, :] = jnp.concatenate(moved, axis=0).astype(BF)
            late = moved[:3]
            for i in range(3, 6):
                other = pltpu.roll(above, 8 * i, 1, stride=1, stride_axis=0)
                late.append(jnp.where(lane >= 8 * (rows + 3 - 10), other, moved[i]))
            band_up[q * 48 : q * 48 + 48, :] = jnp.concatenate(late, axis=0).astype(BF)
        prod_1[...] = jnp.dot(band[...], rhs[0:128, :], preferred_element_type=F32)
        prod_3[...] = jnp.dot(band_up[:, 0:96], rhs[80:176, :], preferred_element_type=F32)
        for o in range(rows):
            prod, step, i = (prod_1, 80, o) if o < 10 else (prod_3, 48, o - 10)
            inner = cots[at_row(o + 3, g), :]
            for q in range(7):
                part = slice(q * step + 8 * i, q * step + 8 * i + 8)
                mine = prod[part, wide[0]]
                if q != 3:
                    mine = shift(jnp.where(edge_mask(q - 3), prod[part, wide[1]], mine), 3 - q)
                inner = inner + mine
            plane[1, pl.ds(g * (8 * rows) + o, 8, stride=rows), :] = inner
        line = jnp.zeros((8, LANES), F32)
        for q in range(7):
            own = [shift(dcv[at_row(o + 3, g), :], q - 3) for o in range(rows)]
            tot = [None] * 7
            for r in range(mid):
                value = ext[at_row(r + 3, g), :]
                if q != 3:
                    value = jnp.where(edge_mask(q - 3), rim[at_row(r + 3, g), :], value)
                for a in range(7):
                    o = r - a
                    if 0 <= o < rows:
                        term = value * own[o]
                        tot[a] = term if tot[a] is None else tot[a] + term
            for a in range(7):
                total = jnp.sum(tot[a], axis=1, keepdims=True)
                line = jnp.where(lane == 8 * a + q, total, line)
        for k in range(3):
            total = jnp.sum(sums[k, at, :], axis=1, keepdims=True)
            line = jnp.where(lane == 56 + k, total, line)
        taps_g[at, :] = line
        return 0

    lax.fori_loop(0, groups, adjoint_group, 0)
    small = taps_g[...]
    cut = 40

    def fill(lower, upper):
        for h, w in enumerate(wide):
            lower[h * chans : (h + 1) * chans, :] = g_down[:, w]
            upper[h * chans : (h + 1) * chans, :] = g_up[0:chans, w]
            upper[2 * chans + 24 + 8 * h : 2 * chans + 32 + 8 * h, :] = g_up[chans : chans + 8, w]
        lower[2 * chans : 2 * chans + cut, :] = small[:cut]
        upper[2 * chans : 2 * chans + 24, :] = small[cut:]

    @pl.when(odd_core == 0)
    def _():
        fill(kept, passed)

    @pl.when(odd_core == 1)
    def _():
        fill(passed, kept)

    for c in range(chans):
        out[c] = plane[0, c * rows : (c + 1) * rows, :].astype(BF)
        grad[c] = plane[1, c * rows : (c + 1) * rows, :].astype(BF)


def finish_kernel(total, other, g_depth, g_gain, g_bias, g_up, g_up_b, g_down, g_scale):
    chans, hidden_n = g_down.shape

    def unpack(lower, upper):
        for h in range(hidden_n // LANES):
            w = slice(h * LANES, (h + 1) * LANES)
            g_down[:, w] = lower[h * chans : (h + 1) * chans, :]
            g_up[:, w] = upper[h * chans : (h + 1) * chans, :]
            at = 2 * chans + 24 + 8 * h
            g_up_b[w] = upper[at : at + 1, :].reshape(LANES)
        small = jnp.concatenate(
            [
                lower[2 * chans : 2 * chans + 40, :],
                upper[2 * chans : 2 * chans + 24, :],
                jnp.zeros((LANES - chans, LANES), F32),
            ],
            axis=0,
        ).T
        for k, dst in enumerate((g_gain, g_bias, g_scale)):
            dst[...] = small[56 + k : 57 + k, :chans].reshape(chans)
        for a in range(7):
            g_depth[a] = small[8 * a : 8 * a + 7, :chans]

    odd_core = lax.axis_index("lon") % 2

    @pl.when(odd_core == 0)
    def _():
        unpack(total, other)

    @pl.when(odd_core == 1)
    def _():
        unpack(other, total)


def vmem(n):
    return [pl.BlockSpec(memory_space=pltpu.VMEM)] * n


def smem():
    return pl.BlockSpec(memory_space=pltpu.SMEM)


def shards(
    fields,
    cotangent,
    ocean_mask,
    seam_partner,
    depth_weight,
    norm_gain,
    layer_norm_bias,
    up_weight,
    up_bias,
    down_weight,
    layer_scale,
):
    _, chans, rows, cols = fields.shape
    hidden_n = up_weight.shape[0]
    n_lon, n_lat = lax.axis_size("lon"), lax.axis_size("lat")
    sds = jax.ShapeDtypeStruct
    ft, gt, first, second = pl.pallas_call(
        pack_kernel,
        out_shape=[sds((rows, chans, cols), BF)] * 2 + [sds((9, chans, cols), BF)] * 2,
        in_specs=vmem(3),
        out_specs=vmem(4),
        scratch_shapes=[pltpu.VMEM((2, chans * rows, cols), F32)],
        name="pack",
    )(fields[0], cotangent[0], ocean_mask)

    at = lambda lon, lat: (lon % n_lon) * n_lat + lat
    rounds = [[], []]
    for lat in range(n_lat - 1):
        for lon in range(n_lon):
            rounds[lat % 2] += [(at(lon, lat), at(lon, lat + 1)), (at(lon, lat + 1), at(lon, lat))]
    fold_round = (n_lat - 1) % 2

    def exchange(k):
        def run(first, second):
            mirror = [
                [(at(lon, n_lat - 1), at(k - j - lon, n_lat - 1)) for lon in range(n_lon)] for j in (0, 1)
            ]
            plan = [list(rounds[0]), list(rounds[1])]
            plan[fold_round] += mirror[0]
            axes = ("lon", "lat")
            top = first if fold_round == 0 else second
            return (
                lax.ppermute(first, axes, plan[0]),
                lax.ppermute(second, axes, plan[1]),
                lax.ppermute(top, axes, mirror[1]),
            )

        return run

    turn = lax.div(seam_partner[0], jnp.int32(cols))
    got_a, got_b, got_c = lax.switch(turn, [exchange(k) for k in range(n_lon)], first, second)
    low, up, sent_l, sent_r = pl.pallas_call(
        functools.partial(edge_kernel, fold_round == 0),
        out_shape=[sds((9, chans, cols), BF)] * 2 + [sds((chans, 2 * cols), BF)] * 2,
        in_specs=[smem()] + vmem(6),
        out_specs=vmem(4),
        name="edges",
    )(seam_partner, seam_partner.reshape(n_lon, cols), got_a, got_b, got_c, ft, gt)
    got_l = lax.ppermute(sent_r, "lon", [(i, (i + 1) % n_lon) for i in range(n_lon)])
    got_r = lax.ppermute(sent_l, "lon", [(i, (i - 1) % n_lon) for i in range(n_lon)])

    plain, turned, vecs, up_aug, down_t = pl.pallas_call(
        weight_kernel,
        out_shape=[
            sds((7, chans, LANES), F32),
            sds((7, chans, LANES), F32),
            sds((3, chans, LANES), F32),
            sds((hidden_n, chans + 16), BF),
            sds((hidden_n, chans), BF),
        ],
        in_specs=vmem(7),
        out_specs=vmem(5),
        scratch_shapes=[pltpu.VMEM((2, 7, LANES, LANES), F32)],
        name="weights",
    )(
        depth_weight.transpose(1, 2, 0),
        norm_gain,
        layer_norm_bias,
        layer_scale,
        up_bias,
        up_weight.T,
        down_weight,
    )
    units = rows + 8
    big, small = 2 * chans, 40
    output, grad, kept, passed = pl.pallas_call(
        main_kernel,
        out_shape=[sds((chans, rows, cols), BF)] * 2 + [sds((big + small, LANES), F32)] * 2,
        in_specs=vmem(14),
        out_specs=vmem(4),
        scratch_shapes=[
            pltpu.VMEM(((rows + 12) * chans, cols), F32),
            pltpu.VMEM(((rows + 12) * chans, cols), F32),
            pltpu.VMEM(((rows + 12) * 8, 2 * cols), BF),
            pltpu.VMEM((units * chans, cols), F32),
            pltpu.VMEM((units * chans, cols), F32),
            pltpu.VMEM((units * chans, cols), F32),
            pltpu.VMEM((2, chans * rows, cols), F32),
            pltpu.VMEM((7 * 80, LANES), BF),
            pltpu.VMEM((7 * 48, LANES), BF),
            pltpu.VMEM((7 * 80, 2 * cols), F32),
            pltpu.VMEM((7 * 80, 2 * cols), F32),
            pltpu.VMEM((7 * 48, 2 * cols), F32),
            pltpu.VMEM((chans, hidden_n), F32),
            pltpu.VMEM((chans + 16, hidden_n), F32),
            pltpu.VMEM((3, chans, LANES), F32),
            pltpu.VMEM((chans, LANES), F32),
        ],
        name="block",
    )(
        ft,
        gt,
        low,
        up,
        got_l,
        got_r,
        ocean_mask,
        plain,
        turned,
        vecs,
        up_aug,
        up_weight.T,
        down_weight,
        down_t,
    )

    flip = lambda y, axis, b: lax.ppermute(y, axis, [(i, i ^ b) for i in range(lax.axis_size(axis))])
    total = kept + flip(passed, "lon", 1)
    for axis, b in [("lon", 1 << i) for i in range(1, n_lon.bit_length() - 1)] + [
        ("lat", 1 << i) for i in range(n_lat.bit_length() - 1)
    ]:
        total = total + flip(total, axis, b)
    other = flip(total, "lon", 1)
    g_depth, g_gain, g_bias, g_up, g_up_b, g_down, g_scale = pl.pallas_call(
        finish_kernel,
        out_shape=[
            sds((7, 7, chans), F32),
            sds((chans,), F32),
            sds((chans,), F32),
            sds((chans, hidden_n), F32),
            sds((hidden_n,), F32),
            sds((chans, hidden_n), F32),
            sds((chans,), F32),
        ],
        in_specs=vmem(2),
        out_specs=vmem(7),
        name="finish",
    )(total, other)
    return (
        output[None],
        grad[None],
        g_depth.transpose(2, 0, 1),
        g_gain,
        g_bias,
        g_up.T,
        g_up_b,
        g_down,
        g_scale,
    )


def solution(mesh):
    block = P(None, None, "lat", "lon")
    placed = (block, block, P("lat", "lon")) + (P(),) * 8
    return jax.shard_map(
        shards, mesh=mesh, in_specs=placed, out_specs=(block, block) + (P(),) * 7, check_vma=False
    )
```

time: 80.5 us -> 73 us (0.907)
  local copies, waits for them, and re-layouts: 10.2 us -> 2.45 us
  Pallas kernels: 25.6 us -> 28.6 us
  other arithmetic: 3.26 us -> 0.95 us
    pallas_call x0 -> x2, Pallas kernels: none -> 3.99 us  [the longest x1 2.31 us: shards(): pl.pallas_call(weight_kernel, out_shape=[sds((7, chans, LANES), F32), sds...]
    concatenate x4 -> x0, other arithmetic: 2.56 us -> none  [the longest x1 0.72 us: shards(): jnp.concatenate([up_weight, up_bias[:, None], jnp.zeros((hidden_n, 15), B...]
    broadcast_in_dim x4 -> x0, local copies, waits for them, and re-layouts: 2.1 us -> none  [the longest x1 1.27 us: shards(): own_partner = lax.dynamic_slice_in_dim(seam_partner, x * cols, cols)[None]]
    unnamed x22 -> x8, local copies, waits for them, and re-layouts: 3 us -> 1.26 us
    pad x2 -> x0, local copies, waits for them, and re-layouts: 1.21 us -> none  [the longest x1 0.61 us: shards(): taps = jnp.pad(flat, ((0, 0), (0, LANES - 49)))]
    pallas_call x1, Pallas kernels: 21 us -> 20 us  [shards(): pl.pallas_call(main_kernel, out_shape=[sds((chans, rows, cols), BF)] * 2...]
    dynamic_slice x1 -> x0, local copies, waits for them, and re-layouts: 0.97 us -> none  [shards(): passed = lax.dynamic_slice_in_dim(red, (1 - bit) * half, half)]
    add x1, other arithmetic: 0.01 us -> 0.9 us  [shards(): total = kept + flip(passed, 'lon', 1)]
  transfers between devices with their start and end apart: 11 -> 11, of which waited for: 7 -> 7; matrix products, arithmetic and copies ran while one was open for 4% -> 0% of each run, Pallas kernels for 0% -> 3%
where the time goes in v2:
time: 73 us; the launch traced here: 72.2 us
  Pallas kernels  28.6 us (39%)
  starting transfers between devices  19.5 us (27%)
  waiting for transfers between devices  18.1 us (25%)
  between operations  2.65 us (4%)
  local copies, waits for them, and re-layouts  2.45 us (3%)
  other arithmetic  0.95 us (1%)
    pallas_call x1, Pallas kernels, shards(): pl.pallas_call(main_kernel, out_shape=[sds((chans, rows, cols), BF)] * 2...  20 us
    ppermute x6, waiting for transfers between devices, shards(): lax.ppermute(y, axis, [(i, i ^ b) for i in range(lax.axis_size(axis))])  14.5 us
    ppermute x6, starting transfers between devices, shards(): lax.ppermute(y, axis, [(i, i ^ b) for i in range(lax.axis_size(axis))])  8.97 us
    ppermute x1, starting transfers between devices, run(): lax.ppermute(first, axes, plan[0])  5.22 us
    ppermute x1, waiting for transfers between devices, run(): lax.ppermute(first, axes, plan[0])  3.66 us
    ppermute x1, starting transfers between devices, shards(): lax.ppermute(sent_l, 'lon', [(i, (i - 1) % n_lon) for i in range(n_lon)])  2.64 us
    pallas_call x1, Pallas kernels, shards(): pl.pallas_call(functools.partial(edge_kernel, fold_round == 0), out_shape...  2.43 us
    pallas_call x1, Pallas kernels, shards(): pl.pallas_call(weight_kernel, out_shape=[sds((7, chans, LANES), F32), sds...  2.31 us
  transfers between devices with their start and end apart: 11, of which 7 were waited for; matrix products, arithmetic and copies ran while one was open for 0% of the time, Pallas kernels for 3%

profile of v2, /device:TPU:0, one launch (start us, length us, event | category | flops | bytes accessed | tf_op | source)
XLA Modules:
  0.0 72.2 jit_solution(6870597525145000428)
XLA Ops:
  0.6 1.2 %slice.3 = s32[1]{0:T(128)} slice(s32[1024]{0:T(1024)} %seam.1), slice={[0:1]} | slice | bytes 8 | tf_op jit(solution)/shard_map/slice | solution.py:535
  3.8 2.2 %pack.1 = (bf16[16,64,128]{2,1,0:T(8,128)(2,1)}, bf16[16,64,128]{2,1,0:T(8,128)(2,1)}, bf16[9,64,128]{2,1,0:T(8,128)(2,1)S(1)}, bf16[9,64,128]{2,1,0:T(8,128)(2,1)S(1)}) custom-call(bf16[64,16,128]{2,1,0:T(8,128)(2,1)} %bitcast.10, bf16[64,16,128]{2,1,0:T(8,128)(2,1)} %bitcast.11, s32[16,128]{1,0:T(8,128)} %mask.3), custom_call_target="tpu_custom_call" | custom-call | tf_op jit(solution)/shard_map/pack/pallas_call | solution.py:502
  6.0 11.5 %conditional.1 = (bf16[9,64,128]{2,1,0:T(8,128)(2,1)}, bf16[9,64,128]{2,1,0:T(8,128)(2,1)}, bf16[9,64,128]{2,1,0:T(8,128)(2,1)}) conditional(s32[]{:T(128)} %clamp.3, (bf16[9,64,128]{2,1,0:T(8,128)(2,1)S(1)}, bf16[9,64,128]{2,1,0:T(8,128)(2,1)S(1)}) %tuple.40, (bf16[9,64,128]{2,1,0:T(8,128)(2,1)S(1)}, ...), branch_computations={%region_0.0_spmd, %region_1.0_spmd, %region_2.0_spmd, %region_3.0_... | conditional | bytes 1769616 | solution.py:536
  6.0 1.3 %collective-permute-start.13 = (bf16[9,64,128]{2,1,0:T(8,128)(2,1)S(1)}, bf16[9,64,128]{2,1,0:T(8,128)(2,1)}, u32[]{:S(2)}, u32[]{:S(2)}) collective-permute-start(bf16[9,64,128]{2,1,0:T(8,128)(2,1)S(1)} %get-tuple-element.41), channel_id=1, source_target_pairs={{1,2},{2,1},{5,6},{6,5},{9,10},{10,9},{13,14},{14,13},{17,18},{18,... | collective-permute-start | bytes 442376 | tf_op jit(solution)/shard_map/cond/branch_4_fun/ppermute | solution.py:529
  7.3 1.3 %collective-permute-start.14 = (bf16[9,64,128]{2,1,0:T(8,128)(2,1)S(1)}, bf16[9,64,128]{2,1,0:T(8,128)(2,1)}, u32[]{:S(2)}, u32[]{:S(2)}) collective-permute-start(bf16[9,64,128]{2,1,0:T(8,128)(2,1)S(1)} %get-tuple-element.41), channel_id=1, source_target_pairs={{3,15},{7,11},{11,7},{15,3},{19,31},{23,27},{27,23},{31,19}} | collective-permute-start | bytes 442376 | tf_op jit(solution)/shard_map/cond/branch_4_fun/ppermute | solution.py:530
  8.6 5.2 %collective-permute-start.12 = (bf16[9,64,128]{2,1,0:T(8,128)(2,1)S(1)}, bf16[9,64,128]{2,1,0:T(8,128)(2,1)}, u32[]{:S(2)}, u32[]{:S(2)}) collective-permute-start(bf16[9,64,128]{2,1,0:T(8,128)(2,1)S(1)} %get-tuple-element.40), channel_id=1, source_target_pairs={{0,1},{1,0},{4,5},{5,4},{8,9},{9,8},{12,13},{13,12},{16,17},{17,16... | collective-permute-start | bytes 442376 | tf_op jit(solution)/shard_map/cond/branch_4_fun/ppermute | solution.py:528
  13.8 0.0 collective-permute-done.13
  13.8 0.0 collective-permute-done.14
  13.8 3.7 %collective-permute-done.12 = bf16[9,64,128]{2,1,0:T(8,128)(2,1)} collective-permute-done((bf16[9,64,128]{2,1,0:T(8,128)(2,1)S(1)}, bf16[9,64,128]{2,1,0:T(8,128)(2,1)}, u32[]{:S(2)}, u32[]{:S(2)}) %collective-permute-start.12) | collective-permute-done | bytes 147488 | tf_op jit(solution)/shard_map/cond/branch_4_fun/ppermute | solution.py:528
  17.5 2.4 %edges.1 = (bf16[9,64,128]{2,1,0:T(8,128)(2,1)}, bf16[9,64,128]{2,1,0:T(8,128)(2,1)}, bf16[64,256]{1,0:T(8,128)(2,1)}, bf16[64,256]{1,0:T(8,128)(2,1)}) custom-call(s32[1024]{0:T(1024)} %seam.1, s32[8,128]{1,0:T(8,128)} %bitcast.14, bf16[9,64,128]{2,1,0:T(8,128)(2,1)} %get-tuple-element.88.got_a, bf16[9,64,128]{2,1,0:T(8,128)(2,1)} %get-tuple-element.89.got_b, ...), custom_call_target="tpu_custom_call" | custom-call | tf_op jit(solution)/shard_map/edges/pallas_call | solution.py:537
  19.9 0.0 collective-permute-start.24
  19.9 2.6 %collective-permute-start.25 = (bf16[64,256]{1,0:T(8,128)(2,1)}, bf16[64,256]{1,0:T(8,128)(2,1)S(1)}, u32[]{:S(2)}, u32[]{:S(2)}) collective-permute-start(bf16[64,256]{1,0:T(8,128)(2,1)} %get-tuple-element.94), channel_id=1, source_target_pairs={{0,28},{4,0},{8,4},{12,8},{16,12},{20,16},{24,20},{28,24},{1,29},{... | collective-permute-start | bytes 98312 | tf_op jit(solution)/shard_map/ppermute | solution.py:545
  22.6 2.3 %weights.1 = (f32[7,64,128]{2,1,0:T(8,128)}, f32[7,64,128]{2,1,0:T(8,128)}, f32[3,64,128]{2,1,0:T(8,128)}, bf16[256,80]{1,0:T(8,128)(2,1)}, bf16[256,64]{1,0:T(8,128)(2,1)}) custom-call(bf16[7,7,64]{2,1,0:T(8,128)(2,1)} %bitcast.15, bf16[64]{0:T(256)(128)(2,1)} %gain.1, bf16[64]{0:T(256)(128)(2,1)} %bias.1, bf16[64]{0:T(256)(128)(2,1)} %scale.1, ...), custom_call_target="tpu_custom_call" | custom-call | tf_op jit(solution)/shard_map/weights/pallas_call | solution.py:547
  24.9 0.0 collective-permute-done.24.got_l
  24.9 0.6 copy-done.2
  25.5 0.0 copy-done.3
  25.5 20.0 %block.1 = (bf16[64,16,128]{2,1,0:T(8,128)(2,1)}, bf16[64,16,128]{2,1,0:T(8,128)(2,1)}, f32[168,128]{1,0:T(8,128)}, f32[168,128]{1,0:T(8,128)}) custom-call(bf16[16,64,128]{2,1,0:T(8,128)(2,1)} %get-tuple-element.84.ft, bf16[16,64,128]{2,1,0:T(8,128)(2,1)} %get-tuple-element.85.gt, bf16[9,64,128]{2,1,0:T(8,128)(2,1)} %get-tuple-element.91.low, ...), custom_call_target="tpu_custom_call" | custom-call | tf_op jit(solution)/shard_map/block/pallas_call | solution.py:571
  45.5 0.2 collective-permute-start.26
  45.7 1.3 %collective-permute-done.26 = f32[168,128]{1,0:T(8,128)S(1)} collective-permute-done((f32[168,128]{1,0:T(8,128)}, f32[168,128]{1,0:T(8,128)S(1)}, u32[]{:S(2)}, u32[]{:S(2)}) %collective-permute-start.26) | collective-permute-done | bytes 86048 | tf_op jit(solution)/shard_map/ppermute | solution.py:612
  47.0 0.9 %add.15 = f32[168,128]{1,0:T(8,128)S(1)} add(f32[168,128]{1,0:T(8,128)} %get-tuple-element.102, f32[168,128]{1,0:T(8,128)S(1)} %collective-permute-done.26) | non-fusion elementwise | flops 21504 | bytes 258048 | tf_op jit(solution)/shard_map/add | solution.py:613
  47.9 2.3 %collective-permute-start.27 = (f32[168,128]{1,0:T(8,128)S(1)}, f32[168,128]{1,0:T(8,128)S(1)}, u32[]{:S(2)}, u32[]{:S(2)}) collective-permute-start(f32[168,128]{1,0:T(8,128)S(1)} %add.15), channel_id=1, source_target_pairs={{0,8},{4,12},{8,0},{12,4},{16,24},{20,28},{24,16},{28,20},{1,9},{5... | collective-permute-start | bytes 258056 | tf_op jit(solution)/shard_map/ppermute | solution.py:612
  50.2 3.1 %collective-permute-done.27 = f32[168,128]{1,0:T(8,128)S(1)} collective-permute-done((f32[168,128]{1,0:T(8,128)S(1)}, f32[168,128]{1,0:T(8,128)S(1)}, u32[]{:S(2)}, u32[]{:S(2)}) %collective-permute-start.27) | collective-permute-done | bytes 86048 | tf_op jit(solution)/shard_map/ppermute | solution.py:612
  53.2 0.9 %collective-permute-start.28 = (f32[168,128]{1,0:T(8,128)S(1)}, f32[168,128]{1,0:T(8,128)S(1)}, u32[]{:S(2)}, u32[]{:S(2)}) collective-permute-start(f32[168,128]{1,0:T(8,128)S(1)} %add.16), channel_id=1, source_target_pairs={{0,16},{4,20},{8,24},{12,28},{16,0},{20,4},{24,8},{28,12},{1,17},{... | collective-permute-start | bytes 258056 | tf_op jit(solution)/shard_map/ppermute | solution.py:612
  54.2 3.6 %collective-permute-done.28 = f32[168,128]{1,0:T(8,128)S(1)} collective-permute-done((f32[168,128]{1,0:T(8,128)S(1)}, f32[168,128]{1,0:T(8,128)S(1)}, u32[]{:S(2)}, u32[]{:S(2)}) %collective-permute-start.28) | collective-permute-done | bytes 86048 | tf_op jit(solution)/shard_map/ppermute | solution.py:612
  57.8 1.8 %collective-permute-start.29 = (f32[168,128]{1,0:T(8,128)S(1)}, f32[168,128]{1,0:T(8,128)S(1)}, u32[]{:S(2)}, u32[]{:S(2)}) collective-permute-start(f32[168,128]{1,0:T(8,128)S(1)} %add.17), channel_id=1, source_target_pairs={{0,1},{1,0},{2,3},{3,2},{4,5},{5,4},{6,7},{7,6},{8,9},{9,8},{10,11... | collective-permute-start | bytes 258056 | tf_op jit(solution)/shard_map/ppermute | solution.py:612
  59.6 2.7 %collective-permute-done.29 = f32[168,128]{1,0:T(8,128)S(1)} collective-permute-done((f32[168,128]{1,0:T(8,128)S(1)}, f32[168,128]{1,0:T(8,128)S(1)}, u32[]{:S(2)}, u32[]{:S(2)}) %collective-permute-start.29) | collective-permute-done | bytes 86048 | tf_op jit(solution)/shard_map/ppermute | solution.py:612
  62.4 3.7 %collective-permute-start.30 = (f32[168,128]{1,0:T(8,128)S(1)}, f32[168,128]{1,0:T(8,128)S(1)}, u32[]{:S(2)}, u32[]{:S(2)}) collective-permute-start(f32[168,128]{1,0:T(8,128)S(1)} %add.18), channel_id=1, source_target_pairs={{0,2},{1,3},{2,0},{3,1},{4,6},{5,7},{6,4},{7,5},{8,10},{9,11},{10,... | collective-permute-start | bytes 258056 | tf_op jit(solution)/shard_map/ppermute | solution.py:612
  66.1 2.5 %collective-permute-done.30 = f32[168,128]{1,0:T(8,128)S(1)} collective-permute-done((f32[168,128]{1,0:T(8,128)S(1)}, f32[168,128]{1,0:T(8,128)S(1)}, u32[]{:S(2)}, u32[]{:S(2)}) %collective-permute-start.30) | collective-permute-done | bytes 86048 | tf_op jit(solution)/shard_map/ppermute | solution.py:612
  68.6 0.1 collective-permute-start.31
  68.6 1.3 %collective-permute-done.31.other = f32[168,128]{1,0:T(8,128)S(1)} collective-permute-done((f32[168,128]{1,0:T(8,128)S(1)}, f32[168,128]{1,0:T(8,128)S(1)}, u32[]{:S(2)}, u32[]{:S(2)}) %collective-permute-start.31) | collective-permute-done | bytes 86048 | tf_op jit(solution)/shard_map/ppermute | solution.py:612
  69.9 0.6 copy-done.1
  70.6 1.7 %finish.1 = (f32[7,7,64]{2,1,0:T(8,128)}, f32[64]{0:T(128)}, f32[64]{0:T(128)}, f32[64,256]{1,0:T(8,128)}, f32[256]{0:T(256)}, /*index=5*/f32[64,256]{1,0:T(8,128)}, f32[64]{0:T(128)}) custom-call(f32[168,128]{1,0:T(8,128)} %copy-done, f32[168,128]{1,0:T(8,128)} %copy-done.1), custom_call_target="tpu_custom_call" | custom-call | tf_op jit(solution)/shard_map/finish/pallas_call | solution.py:619
  (10 shorter events, 0.1 us)
Async XLA Ops:
  6.0 7.8 %collective-permute-start.13 = (bf16[9,64,128]{2,1,0:T(8,128)(2,1)S(1)}, bf16[9,64,128]{2,1,0:T(8,128)(2,1)}, u32[]{:S(2)}, u32[]{:S(2)}) collective-permute-start(bf16[9,64,128]{2,1,0:T(8,128)(2,1)S(1)} %get-tuple-element.41), channel_id=1, source_target_pairs={{1,2},{2,1},{5,6},{6,5},{9,10},{10,9},{13,14},{14,13},{17,18},{18,... | collective-permute-start | bytes 442376 | tf_op jit(solution)/shard_map/cond/branch_4_fun/ppermute | solution.py:529
  7.3 6.5 %collective-permute-start.14 = (bf16[9,64,128]{2,1,0:T(8,128)(2,1)S(1)}, bf16[9,64,128]{2,1,0:T(8,128)(2,1)}, u32[]{:S(2)}, u32[]{:S(2)}) collective-permute-start(bf16[9,64,128]{2,1,0:T(8,128)(2,1)S(1)} %get-tuple-element.41), channel_id=1, source_target_pairs={{3,15},{7,11},{11,7},{15,3},{19,31},{23,27},{27,23},{31,19}} | collective-permute-start | bytes 442376 | tf_op jit(solution)/shard_map/cond/branch_4_fun/ppermute | solution.py:530
  8.6 8.9 %collective-permute-start.12 = (bf16[9,64,128]{2,1,0:T(8,128)(2,1)S(1)}, bf16[9,64,128]{2,1,0:T(8,128)(2,1)}, u32[]{:S(2)}, u32[]{:S(2)}) collective-permute-start(bf16[9,64,128]{2,1,0:T(8,128)(2,1)S(1)} %get-tuple-element.40), channel_id=1, source_target_pairs={{0,1},{1,0},{4,5},{5,4},{8,9},{9,8},{12,13},{13,12},{16,17},{17,16... | collective-permute-start | bytes 442376 | tf_op jit(solution)/shard_map/cond/branch_4_fun/ppermute | solution.py:528
  19.9 5.0 %collective-permute-start.24 = (bf16[64,256]{1,0:T(8,128)(2,1)}, bf16[64,256]{1,0:T(8,128)(2,1)S(1)}, u32[]{:S(2)}, u32[]{:S(2)}) collective-permute-start(bf16[64,256]{1,0:T(8,128)(2,1)} %get-tuple-element.93), channel_id=1, source_target_pairs={{0,4},{4,8},{8,12},{12,16},{16,20},{20,24},{24,28},{28,0},{1,5},{5... | collective-permute-start | bytes 98312 | tf_op jit(solution)/shard_map/ppermute | solution.py:544
  19.9 5.0 %collective-permute-start.25 = (bf16[64,256]{1,0:T(8,128)(2,1)}, bf16[64,256]{1,0:T(8,128)(2,1)S(1)}, u32[]{:S(2)}, u32[]{:S(2)}) collective-permute-start(bf16[64,256]{1,0:T(8,128)(2,1)} %get-tuple-element.94), channel_id=1, source_target_pairs={{0,28},{4,0},{8,4},{12,8},{16,12},{20,16},{24,20},{28,24},{1,29},{... | collective-permute-start | bytes 98312 | tf_op jit(solution)/shard_map/ppermute | solution.py:545
  24.9 0.6 copy-start.2
  24.9 0.6 copy-start.3
  45.5 1.5 %collective-permute-start.26 = (f32[168,128]{1,0:T(8,128)}, f32[168,128]{1,0:T(8,128)S(1)}, u32[]{:S(2)}, u32[]{:S(2)}) collective-permute-start(f32[168,128]{1,0:T(8,128)} %get-tuple-element.103), channel_id=1, source_target_pairs={{0,4},{4,0},{8,12},{12,8},{16,20},{20,16},{24,28},{28,24},{1,5},{5... | collective-permute-start | bytes 258056 | tf_op jit(solution)/shard_map/ppermute | solution.py:612
  47.9 5.3 %collective-permute-start.27 = (f32[168,128]{1,0:T(8,128)S(1)}, f32[168,128]{1,0:T(8,128)S(1)}, u32[]{:S(2)}, u32[]{:S(2)}) collective-permute-start(f32[168,128]{1,0:T(8,128)S(1)} %add.15), channel_id=1, source_target_pairs={{0,8},{4,12},{8,0},{12,4},{16,24},{20,28},{24,16},{28,20},{1,9},{5... | collective-permute-start | bytes 258056 | tf_op jit(solution)/shard_map/ppermute | solution.py:612
  53.2 4.6 %collective-permute-start.28 = (f32[168,128]{1,0:T(8,128)S(1)}, f32[168,128]{1,0:T(8,128)S(1)}, u32[]{:S(2)}, u32[]{:S(2)}) collective-permute-start(f32[168,128]{1,0:T(8,128)S(1)} %add.16), channel_id=1, source_target_pairs={{0,16},{4,20},{8,24},{12,28},{16,0},{20,4},{24,8},{28,12},{1,17},{... | collective-permute-start | bytes 258056 | tf_op jit(solution)/shard_map/ppermute | solution.py:612
  57.8 4.6 %collective-permute-start.29 = (f32[168,128]{1,0:T(8,128)S(1)}, f32[168,128]{1,0:T(8,128)S(1)}, u32[]{:S(2)}, u32[]{:S(2)}) collective-permute-start(f32[168,128]{1,0:T(8,128)S(1)} %add.17), channel_id=1, source_target_pairs={{0,1},{1,0},{2,3},{3,2},{4,5},{5,4},{6,7},{7,6},{8,9},{9,8},{10,11... | collective-permute-start | bytes 258056 | tf_op jit(solution)/shard_map/ppermute | solution.py:612
  62.4 6.2 %collective-permute-start.30 = (f32[168,128]{1,0:T(8,128)S(1)}, f32[168,128]{1,0:T(8,128)S(1)}, u32[]{:S(2)}, u32[]{:S(2)}) collective-permute-start(f32[168,128]{1,0:T(8,128)S(1)} %add.18), channel_id=1, source_target_pairs={{0,2},{1,3},{2,0},{3,1},{4,6},{5,7},{6,4},{7,5},{8,10},{9,11},{10,... | collective-permute-start | bytes 258056 | tf_op jit(solution)/shard_map/ppermute | solution.py:612
  68.6 1.4 %copy-start = (f32[168,128]{1,0:T(8,128)}, f32[168,128]{1,0:T(8,128)S(1)}, u32[]{:S(2)}) copy-start(f32[168,128]{1,0:T(8,128)S(1)} %add.19.total) | copy-start | bytes 258052
  68.6 1.3 %collective-permute-start.31 = (f32[168,128]{1,0:T(8,128)S(1)}, f32[168,128]{1,0:T(8,128)S(1)}, u32[]{:S(2)}, u32[]{:S(2)}) collective-permute-start(f32[168,128]{1,0:T(8,128)S(1)} %add.19.total), channel_id=1, source_target_pairs={{0,4},{4,0},{8,12},{12,8},{16,20},{20,16},{24,28},{28,24},{1,5},{5... | collective-permute-start | bytes 258056 | tf_op jit(solution)/shard_map/ppermute | solution.py:612
  69.9 0.6 copy-start.1

commit v3 on v2

--- a/solution.py
+++ b/solution.py
@@ -171,7 +171,7 @@
 
 def normal_terms(v):
     cdf = 0.5 * (1.0 + lax.erf(v * (1.0 / math.sqrt(2.0))))
-    dens = jnp.exp(-0.5 * v * v) * (1.0 / math.sqrt(2.0 * math.pi))
+    dens = jnp.exp2(v * v * (-0.5 / math.log(2.0)) - 0.5 * math.log2(2.0 * math.pi))
     return cdf, dens
 
 
@@ -505,6 +505,7 @@
         in_specs=vmem(3),
         out_specs=vmem(4),
         scratch_shapes=[pltpu.VMEM((2, chans * rows, cols), F32)],
+        compiler_params=pltpu.CompilerParams(vmem_limit_bytes=8 * 2**20),
         name="pack",
     )(fields[0], cotangent[0], ocean_mask)
 
@@ -515,30 +516,31 @@
             rounds[lat % 2] += [(at(lon, lat), at(lon, lat + 1)), (at(lon, lat + 1), at(lon, lat))]
     fold_round = (n_lat - 1) % 2
 
+    axes = ("lon", "lat")
+    plain_round = 1 - fold_round
+    sends = (first, second)
+    met = lax.ppermute(sends[plain_round], axes, rounds[plain_round])
+    seam, top = lax.optimization_barrier((seam_partner, sends[fold_round]))
+
     def exchange(k):
-        def run(first, second):
+        def run(top):
             mirror = [
                 [(at(lon, n_lat - 1), at(k - j - lon, n_lat - 1)) for lon in range(n_lon)] for j in (0, 1)
             ]
-            plan = [list(rounds[0]), list(rounds[1])]
-            plan[fold_round] += mirror[0]
-            axes = ("lon", "lat")
-            top = first if fold_round == 0 else second
-            return (
-                lax.ppermute(first, axes, plan[0]),
-                lax.ppermute(second, axes, plan[1]),
-                lax.ppermute(top, axes, mirror[1]),
-            )
+            plan = rounds[fold_round] + mirror[0]
+            return lax.ppermute(top, axes, plan), lax.ppermute(top, axes, mirror[1])
 
         return run
 
-    turn = lax.div(seam_partner[0], jnp.int32(cols))
-    got_a, got_b, got_c = lax.switch(turn, [exchange(k) for k in range(n_lon)], first, second)
+    turn = lax.div(seam[0], jnp.int32(cols))
+    folded, got_c = lax.switch(turn, [exchange(k) for k in range(n_lon)], top)
+    got_a, got_b = (folded, met) if fold_round == 0 else (met, folded)
     low, up, sent_l, sent_r = pl.pallas_call(
         functools.partial(edge_kernel, fold_round == 0),
         out_shape=[sds((9, chans, cols), BF)] * 2 + [sds((chans, 2 * cols), BF)] * 2,
         in_specs=[smem()] + vmem(6),
         out_specs=vmem(4),
+        compiler_params=pltpu.CompilerParams(vmem_limit_bytes=8 * 2**20),
         name="edges",
     )(seam_partner, seam_partner.reshape(n_lon, cols), got_a, got_b, got_c, ft, gt)
     got_l = lax.ppermute(sent_r, "lon", [(i, (i + 1) % n_lon) for i in range(n_lon)])
@@ -556,6 +558,7 @@
         in_specs=vmem(7),
         out_specs=vmem(5),
         scratch_shapes=[pltpu.VMEM((2, 7, LANES, LANES), F32)],
+        compiler_params=pltpu.CompilerParams(vmem_limit_bytes=8 * 2**20),
         name="weights",
     )(
         depth_weight.transpose(1, 2, 0),
@@ -591,6 +594,7 @@
             pltpu.VMEM((3, chans, LANES), F32),
             pltpu.VMEM((chans, LANES), F32),
         ],
+        compiler_params=pltpu.CompilerParams(vmem_limit_bytes=20 * 2**20),
         name="block",
     )(
         ft,
@@ -629,6 +633,7 @@
         ],
         in_specs=vmem(2),
         out_specs=vmem(7),
+        compiler_params=pltpu.CompilerParams(vmem_limit_bytes=6 * 2**20),
         name="finish",
     )(total, other)
     return (

time: 73 us -> 66.3 us (0.908)
  Pallas kernels: 28.6 us -> 21.7 us
  waiting for transfers between devices: 18.1 us -> 14.1 us
  starting transfers between devices: 19.5 us -> 22.6 us
  local copies, waits for them, and re-layouts: 2.45 us -> 4.32 us
  other arithmetic: 0.95 us -> 0.07 us
    ppermute x6, starting transfers between devices: 8.97 us -> 14.2 us  [shards(): lax.ppermute(y, axis, [(i, i ^ b) for i in range(lax.axis_size(axis))])]
    ppermute x3, waiting for transfers between devices: 3.67 us -> 0.01 us  [the longest x2 0.01 us: run(): return (lax.ppermute(top, axes, plan), lax.ppermute(top, axes, mirror[1]))]
    unnamed x8 -> x24, local copies, waits for them, and re-layouts: 1.26 us -> 3.81 us
    ppermute x3, starting transfers between devices: 7.85 us -> 5.75 us  [the longest x1 3.12 us: shards(): met = lax.ppermute(sends[plain_round], axes, rounds[plain_round])]
    pallas_call x1, Pallas kernels: 2.2 us -> 0.38 us  [shards(): pl.pallas_call(pack_kernel, out_shape=[sds((rows, chans, cols), BF)] * 2...]
    pallas_call x1, Pallas kernels: 20 us -> 18.3 us  [shards(): pl.pallas_call(main_kernel, out_shape=[sds((chans, rows, cols), BF)] * 2...]
    pallas_call x1, Pallas kernels: 2.31 us -> 0.74 us  [shards(): pl.pallas_call(weight_kernel, out_shape=[sds((7, chans, LANES), F32), sds...]
    pallas_call x1, Pallas kernels: 1.68 us -> 0.75 us  [shards(): pl.pallas_call(finish_kernel, out_shape=[sds((7, 7, chans), F32), sds((ch...]
  transfers between devices with their start and end apart: 11 -> 11, of which waited for: 7 -> 7; matrix products, arithmetic and copies ran while one was open for 0% -> 1% of each run, Pallas kernels for 3% -> 1%
where the time goes in v3:
time: 66.3 us; the launch traced here: 65.6 us
  starting transfers between devices  22.6 us (34%)
  Pallas kernels  21.7 us (33%)
  waiting for transfers between devices  14.1 us (21%)
  local copies, waits for them, and re-layouts  4.32 us (7%)
  between operations  2.73 us (4%)
    pallas_call x1, Pallas kernels, shards(): pl.pallas_call(main_kernel, out_shape=[sds((chans, rows, cols), BF)] * 2...  18.3 us
    ppermute x6, starting transfers between devices, shards(): lax.ppermute(y, axis, [(i, i ^ b) for i in range(lax.axis_size(axis))])  14.2 us
    ppermute x6, waiting for transfers between devices, shards(): lax.ppermute(y, axis, [(i, i ^ b) for i in range(lax.axis_size(axis))])  14 us
    unnamed x24, local copies, waits for them, and re-layouts  3.81 us
    ppermute x1, starting transfers between devices, shards(): met = lax.ppermute(sends[plain_round], axes, rounds[plain_round])  3.12 us
    ppermute x1, starting transfers between devices, shards(): lax.ppermute(sent_l, 'lon', [(i, (i - 1) % n_lon) for i in range(n_lon)])  2.63 us
    ppermute x2, starting transfers between devices, run(): return (lax.ppermute(top, axes, plan), lax.ppermute(top, axes, mirror[1]))  2.63 us
    pallas_call x1, Pallas kernels, shards(): pl.pallas_call(functools.partial(edge_kernel, fold_round == 0), out_shape...  1.53 us
  transfers between devices with their start and end apart: 11, of which 7 were waited for; matrix products, arithmetic and copies ran while one was open for 1% of the time, Pallas kernels for 1%

profile of v3, /device:TPU:0, one launch (start us, length us, event | category | flops | bytes accessed | tf_op | source)
XLA Modules:
  0.0 65.6 jit_solution(2546010334685210572)
XLA Ops:
  0.7 0.9 %copy-done = bf16[1,64,16,128]{3,2,1,0:T(8,128)(2,1)S(1)} copy-done((bf16[1,64,16,128]{3,2,1,0:T(8,128)(2,1)S(1)}, bf16[1,64,16,128]{3,2,1,0:T(8,128)(2,1)}, u32[]{:S(2)}) %copy-start) | copy-done | bytes 262168
  1.6 0.9 %copy-done.1 = bf16[1,64,16,128]{3,2,1,0:T(8,128)(2,1)S(1)} copy-done((bf16[1,64,16,128]{3,2,1,0:T(8,128)(2,1)S(1)}, bf16[1,64,16,128]{3,2,1,0:T(8,128)(2,1)}, u32[]{:S(2)}) %copy-start.1) | copy-done | bytes 262168
  2.5 0.7 %copy-done.4 = s32[16,128]{1,0:T(8,128)S(1)} copy-done((s32[16,128]{1,0:T(8,128)S(1)}, s32[16,128]{1,0:T(8,128)}, u32[]{:S(2)}) %copy-start.4) | copy-done | bytes 8216
  3.2 0.4 pack.1
  3.6 3.1 %collective-permute-start.16 = (bf16[9,64,128]{2,1,0:T(8,128)(2,1)S(1)}, bf16[9,64,128]{2,1,0:T(8,128)(2,1)S(1)}, u32[]{:S(2)}, u32[]{:S(2)}) collective-permute-start(bf16[9,64,128]{2,1,0:T(8,128)(2,1)S(1)} %get-tuple-element.47), channel_id=1, source_target_pairs={{0,1},{1,0},{4,5},{5,4},{8,9},{9,8},{12,13},{13,12},{16,17},{17,16... | collective-permute-start | bytes 442376 | tf_op jit(solution)/shard_map/ppermute | solution.py:522
  6.8 0.5 slice.3
  9.2 2.7 %conditional.1 = (bf16[9,64,128]{2,1,0:T(8,128)(2,1)}, bf16[9,64,128]{2,1,0:T(8,128)(2,1)}) conditional(s32[]{:T(128)} %clamp.3, bf16[9,64,128]{2,1,0:T(8,128)(2,1)S(1)} %get-tuple-element.50, bf16[9,64,128]{2,1,0:T(8,128)(2,1)S(1)} %get-tuple-element.50, bf16[9,64,128]{2,1,0:T(8,128)(2,1)S(1)} %get-tuple-element.50, ...), branch_computations={%region_0.0_spmd, %region_1.0_spmd, %region_2.0_spmd, %region_3.0_... | conditional | bytes 1179744 | solution.py:536
  9.2 1.3 %collective-permute-start.9 = (bf16[9,64,128]{2,1,0:T(8,128)(2,1)S(1)}, bf16[9,64,128]{2,1,0:T(8,128)(2,1)}, u32[]{:S(2)}, u32[]{:S(2)}) collective-permute-start(bf16[9,64,128]{2,1,0:T(8,128)(2,1)S(1)} %param.4), channel_id=1, source_target_pairs={{3,15},{7,11},{11,7},{15,3},{19,31},{23,27},{27,23},{31,19}} | collective-permute-start | bytes 442376 | tf_op jit(solution)/shard_map/cond/branch_4_fun/ppermute | solution.py:531
  10.6 1.3 %collective-permute-start.8 = (bf16[9,64,128]{2,1,0:T(8,128)(2,1)S(1)}, bf16[9,64,128]{2,1,0:T(8,128)(2,1)}, u32[]{:S(2)}, u32[]{:S(2)}) collective-permute-start(bf16[9,64,128]{2,1,0:T(8,128)(2,1)S(1)} %param.4), channel_id=1, source_target_pairs={{1,2},{2,1},{5,6},{6,5},{9,10},{10,9},{13,14},{14,13},{17,18},{18,... | collective-permute-start | bytes 442376 | tf_op jit(solution)/shard_map/cond/branch_4_fun/ppermute | solution.py:531
  11.9 1.5 %edges.1 = (bf16[9,64,128]{2,1,0:T(8,128)(2,1)S(1)}, bf16[9,64,128]{2,1,0:T(8,128)(2,1)S(1)}, bf16[64,256]{1,0:T(8,128)(2,1)S(1)}, bf16[64,256]{1,0:T(8,128)(2,1)S(1)}) custom-call(s32[1024]{0:T(1024)S(1)} %copy-done.6, s32[8,128]{1,0:T(8,128)S(1)} %bitcast.14, bf16[9,64,128]{2,1,0:T(8,128)(2,1)S(1)} %collective-permute-done.16.got_a, ...), custom_call_target="tpu_custom_call" | custom-call | tf_op jit(solution)/shard_map/edges/pallas_call | solution.py:538
  13.5 0.1 collective-permute-start.17
  13.5 2.6 %collective-permute-start.18 = (bf16[64,256]{1,0:T(8,128)(2,1)S(1)}, bf16[64,256]{1,0:T(8,128)(2,1)S(1)}, u32[]{:S(2)}, u32[]{:S(2)}) collective-permute-start(bf16[64,256]{1,0:T(8,128)(2,1)S(1)} %get-tuple-element.56), channel_id=1, source_target_pairs={{0,28},{4,0},{8,4},{12,8},{16,12},{20,16},{24,20},{28,24},{1,29},{... | collective-permute-start | bytes 98312 | tf_op jit(solution)/shard_map/ppermute | solution.py:547
  16.2 0.6 copy-done.8
  16.8 0.0 copy-done.9
  16.8 0.0 copy-done.10
  16.9 0.7 %weights.1 = (f32[7,64,128]{2,1,0:T(8,128)S(1)}, f32[7,64,128]{2,1,0:T(8,128)S(1)}, f32[3,64,128]{2,1,0:T(8,128)S(1)}, bf16[256,80]{1,0:T(8,128)(2,1)S(1)}, bf16[256,64]{1,0:T(8,128)(2,1)S(1)}) custom-call(bf16[7,7,64]{2,1,0:T(8,128)(2,1)S(1)} %bitcast.15, bf16[64]{0:T(256)(128)(2,1)S(1)} %copy-done.8, bf16[64]{0:T(256)(128)(2,1)S(1)} %copy-done.9, ...), custom_call_target="tpu_custom_call" | custom-call | tf_op jit(solution)/shard_map/weights/pallas_call | solution.py:549
  17.6 0.1 collective-permute-done.17.got_l
  17.8 0.5 copy-done.5
  18.3 18.3 %block.1 = (bf16[64,16,128]{2,1,0:T(8,128)(2,1)}, bf16[64,16,128]{2,1,0:T(8,128)(2,1)}, f32[168,128]{1,0:T(8,128)S(1)}, f32[168,128]{1,0:T(8,128)S(1)}) custom-call(bf16[16,64,128]{2,1,0:T(8,128)(2,1)S(1)} %get-tuple-element.45.ft, bf16[16,64,128]{2,1,0:T(8,128)(2,1)S(1)} %get-tuple-element.46.gt, bf16[9,64,128]{2,1,0:T(8,128)(2,1)S(1)} %get-tuple-element.53.low, ...), custom_call_target="tpu_custom_call" | custom-call | tf_op jit(solution)/shard_map/block/pallas_call | solution.py:574
  36.6 0.2 collective-permute-start.19
  36.8 1.1 %collective-permute-done.19 = f32[168,128]{1,0:T(8,128)S(1)} collective-permute-done((f32[168,128]{1,0:T(8,128)S(1)}, f32[168,128]{1,0:T(8,128)S(1)}, u32[]{:S(2)}, u32[]{:S(2)}) %collective-permute-start.19) | collective-permute-done | bytes 86048 | tf_op jit(solution)/shard_map/ppermute | solution.py:616
  37.9 2.3 %collective-permute-start.20 = (f32[168,128]{1,0:T(8,128)S(1)}, f32[168,128]{1,0:T(8,128)S(1)}, u32[]{:S(2)}, u32[]{:S(2)}) collective-permute-start(f32[168,128]{1,0:T(8,128)S(1)} %add.15), channel_id=1, source_target_pairs={{0,8},{4,12},{8,0},{12,4},{16,24},{20,28},{24,16},{28,20},{1,9},{5... | collective-permute-start | bytes 258056 | tf_op jit(solution)/shard_map/ppermute | solution.py:616
  40.2 3.1 %collective-permute-done.20 = f32[168,128]{1,0:T(8,128)S(1)} collective-permute-done((f32[168,128]{1,0:T(8,128)S(1)}, f32[168,128]{1,0:T(8,128)S(1)}, u32[]{:S(2)}, u32[]{:S(2)}) %collective-permute-start.20) | collective-permute-done | bytes 86048 | tf_op jit(solution)/shard_map/ppermute | solution.py:616
  43.3 0.9 %collective-permute-start.21 = (f32[168,128]{1,0:T(8,128)S(1)}, f32[168,128]{1,0:T(8,128)S(1)}, u32[]{:S(2)}, u32[]{:S(2)}) collective-permute-start(f32[168,128]{1,0:T(8,128)S(1)} %add.16), channel_id=1, source_target_pairs={{0,16},{4,20},{8,24},{12,28},{16,0},{20,4},{24,8},{28,12},{1,17},{... | collective-permute-start | bytes 258056 | tf_op jit(solution)/shard_map/ppermute | solution.py:616
  44.2 3.6 %collective-permute-done.21 = f32[168,128]{1,0:T(8,128)S(1)} collective-permute-done((f32[168,128]{1,0:T(8,128)S(1)}, f32[168,128]{1,0:T(8,128)S(1)}, u32[]{:S(2)}, u32[]{:S(2)}) %collective-permute-start.21) | collective-permute-done | bytes 86048 | tf_op jit(solution)/shard_map/ppermute | solution.py:616
  47.8 7.5 %collective-permute-start.22 = (f32[168,128]{1,0:T(8,128)S(1)}, f32[168,128]{1,0:T(8,128)S(1)}, u32[]{:S(2)}, u32[]{:S(2)}) collective-permute-start(f32[168,128]{1,0:T(8,128)S(1)} %add.17), channel_id=1, source_target_pairs={{0,1},{1,0},{2,3},{3,2},{4,5},{5,4},{6,7},{7,6},{8,9},{9,8},{10,11... | collective-permute-start | bytes 258056 | tf_op jit(solution)/shard_map/ppermute | solution.py:616
  55.3 2.5 %collective-permute-done.22 = f32[168,128]{1,0:T(8,128)S(1)} collective-permute-done((f32[168,128]{1,0:T(8,128)S(1)}, f32[168,128]{1,0:T(8,128)S(1)}, u32[]{:S(2)}, u32[]{:S(2)}) %collective-permute-start.22) | collective-permute-done | bytes 86048 | tf_op jit(solution)/shard_map/ppermute | solution.py:616
  57.8 3.3 %collective-permute-start.23 = (f32[168,128]{1,0:T(8,128)S(1)}, f32[168,128]{1,0:T(8,128)S(1)}, u32[]{:S(2)}, u32[]{:S(2)}) collective-permute-start(f32[168,128]{1,0:T(8,128)S(1)} %add.18), channel_id=1, source_target_pairs={{0,2},{1,3},{2,0},{3,1},{4,6},{5,7},{6,4},{7,5},{8,10},{9,11},{10,... | collective-permute-start | bytes 258056 | tf_op jit(solution)/shard_map/ppermute | solution.py:616
  61.0 2.5 %collective-permute-done.23 = f32[168,128]{1,0:T(8,128)S(1)} collective-permute-done((f32[168,128]{1,0:T(8,128)S(1)}, f32[168,128]{1,0:T(8,128)S(1)}, u32[]{:S(2)}, u32[]{:S(2)}) %collective-permute-start.23) | collective-permute-done | bytes 86048 | tf_op jit(solution)/shard_map/ppermute | solution.py:616
  63.5 0.1 collective-permute-start.24
  63.6 1.3 %collective-permute-done.24.other = f32[168,128]{1,0:T(8,128)S(1)} collective-permute-done((f32[168,128]{1,0:T(8,128)S(1)}, f32[168,128]{1,0:T(8,128)S(1)}, u32[]{:S(2)}, u32[]{:S(2)}) %collective-permute-start.24) | collective-permute-done | bytes 86048 | tf_op jit(solution)/shard_map/ppermute | solution.py:616
  64.9 0.7 %finish.1 = (f32[7,7,64]{2,1,0:T(8,128)}, f32[64]{0:T(128)}, f32[64]{0:T(128)}, f32[64,256]{1,0:T(8,128)}, f32[256]{0:T(256)}, /*index=5*/f32[64,256]{1,0:T(8,128)}, f32[64]{0:T(128)}) custom-call(f32[168,128]{1,0:T(8,128)S(1)} %add.19.total, f32[168,128]{1,0:T(8,128)S(1)} %collective-permute-done.24.other), custom_call_target="tpu_custom_call" | custom-call | tf_op jit(solution)/shard_map/finish/pallas_call | solution.py:623
  (26 shorter events, 0.1 us)
Async XLA Ops:
  0.6 1.0 %copy-start = (bf16[1,64,16,128]{3,2,1,0:T(8,128)(2,1)S(1)}, bf16[1,64,16,128]{3,2,1,0:T(8,128)(2,1)}, u32[]{:S(2)}) copy-start(bf16[1,64,16,128]{3,2,1,0:T(8,128)(2,1)} %param.19) | copy-start | bytes 786436
  1.6 0.9 %copy-start.1 = (bf16[1,64,16,128]{3,2,1,0:T(8,128)(2,1)S(1)}, bf16[1,64,16,128]{3,2,1,0:T(8,128)(2,1)}, u32[]{:S(2)}) copy-start(bf16[1,64,16,128]{3,2,1,0:T(8,128)(2,1)} %param.20) | copy-start | bytes 786436
  2.5 0.7 %copy-start.4 = (s32[16,128]{1,0:T(8,128)S(1)}, s32[16,128]{1,0:T(8,128)}, u32[]{:S(2)}) copy-start(s32[16,128]{1,0:T(8,128)} %mask.3) | copy-start | bytes 24580
  3.2 3.5 %copy-start.6 = (s32[1024]{0:T(1024)S(1)}, s32[1024]{0:T(1024)}, u32[]{:S(2)}) copy-start(s32[1024]{0:T(1024)} %seam.1) | copy-start | bytes 12292
  3.6 8.2 %collective-permute-start.16 = (bf16[9,64,128]{2,1,0:T(8,128)(2,1)S(1)}, bf16[9,64,128]{2,1,0:T(8,128)(2,1)S(1)}, u32[]{:S(2)}, u32[]{:S(2)}) collective-permute-start(bf16[9,64,128]{2,1,0:T(8,128)(2,1)S(1)} %get-tuple-element.47), channel_id=1, source_target_pairs={{0,1},{1,0},{4,5},{5,4},{8,9},{9,8},{12,13},{13,12},{16,17},{17,16... | collective-permute-start | bytes 442376 | tf_op jit(solution)/shard_map/ppermute | solution.py:522
  9.2 2.6 %collective-permute-start.9 = (bf16[9,64,128]{2,1,0:T(8,128)(2,1)S(1)}, bf16[9,64,128]{2,1,0:T(8,128)(2,1)}, u32[]{:S(2)}, u32[]{:S(2)}) collective-permute-start(bf16[9,64,128]{2,1,0:T(8,128)(2,1)S(1)} %param.4), channel_id=1, source_target_pairs={{3,15},{7,11},{11,7},{15,3},{19,31},{23,27},{27,23},{31,19}} | collective-permute-start | bytes 442376 | tf_op jit(solution)/shard_map/cond/branch_4_fun/ppermute | solution.py:531
  10.6 1.3 %collective-permute-start.8 = (bf16[9,64,128]{2,1,0:T(8,128)(2,1)S(1)}, bf16[9,64,128]{2,1,0:T(8,128)(2,1)}, u32[]{:S(2)}, u32[]{:S(2)}) collective-permute-start(bf16[9,64,128]{2,1,0:T(8,128)(2,1)S(1)} %param.4), channel_id=1, source_target_pairs={{1,2},{2,1},{5,6},{6,5},{9,10},{10,9},{13,14},{14,13},{17,18},{18,... | collective-permute-start | bytes 442376 | tf_op jit(solution)/shard_map/cond/branch_4_fun/ppermute | solution.py:531
  11.9 4.3 %copy-start.2 = (bf16[256,64]{0,1:T(8,128)(2,1)S(1)}, bf16[256,64]{0,1:T(8,128)(2,1)}, u32[]{:S(2)}) copy-start(bf16[256,64]{0,1:T(8,128)(2,1)} %param.26) | copy-start | bytes 98308
  11.9 4.3 %copy-start.3 = (bf16[64,256]{1,0:T(8,128)(2,1)S(1)}, bf16[64,256]{1,0:T(8,128)(2,1)}, u32[]{:S(2)}) copy-start(bf16[64,256]{1,0:T(8,128)(2,1)} %down.3) | copy-start | bytes 98308
  11.9 4.3 %copy-start.7 = (bf16[64,7,7]{0,2,1:T(8,128)(2,1)S(1)}, bf16[64,7,7]{0,2,1:T(8,128)(2,1)}, u32[]{:S(2)}) copy-start(bf16[64,7,7]{0,2,1:T(8,128)(2,1)} %param.23) | copy-start | bytes 18820
  11.9 4.3 %copy-start.11 = (bf16[256]{0:T(256)(128)(2,1)S(1)}, bf16[256]{0:T(256)(128)(2,1)}, u32[]{:S(2)}) copy-start(bf16[256]{0:T(256)(128)(2,1)} %up_b.1) | copy-start | bytes 1540
  13.5 4.3 %collective-permute-start.17 = (bf16[64,256]{1,0:T(8,128)(2,1)S(1)}, bf16[64,256]{1,0:T(8,128)(2,1)S(1)}, u32[]{:S(2)}, u32[]{:S(2)}) collective-permute-start(bf16[64,256]{1,0:T(8,128)(2,1)S(1)} %get-tuple-element.55), channel_id=1, source_target_pairs={{0,4},{4,8},{8,12},{12,16},{16,20},{20,24},{24,28},{28,0},{1,5},{5... | collective-permute-start | bytes 98312 | tf_op jit(solution)/shard_map/ppermute | solution.py:546
  13.5 4.2 %collective-permute-start.18 = (bf16[64,256]{1,0:T(8,128)(2,1)S(1)}, bf16[64,256]{1,0:T(8,128)(2,1)S(1)}, u32[]{:S(2)}, u32[]{:S(2)}) collective-permute-start(bf16[64,256]{1,0:T(8,128)(2,1)S(1)} %get-tuple-element.56), channel_id=1, source_target_pairs={{0,28},{4,0},{8,4},{12,8},{16,12},{20,16},{24,20},{28,24},{1,29},{... | collective-permute-start | bytes 98312 | tf_op jit(solution)/shard_map/ppermute | solution.py:547
  16.2 0.7 copy-start.8
  16.2 0.7 %copy-start.9 = (bf16[64]{0:T(256)(128)(2,1)S(1)}, bf16[64]{0:T(256)(128)(2,1)}, u32[]{:S(2)}) copy-start(bf16[64]{0:T(256)(128)(2,1)} %bias.1) | copy-start | bytes 388
  16.2 0.7 %copy-start.10 = (bf16[64]{0:T(256)(128)(2,1)S(1)}, bf16[64]{0:T(256)(128)(2,1)}, u32[]{:S(2)}) copy-start(bf16[64]{0:T(256)(128)(2,1)} %scale.1) | copy-start | bytes 388
  17.6 0.7 %copy-start.5 = (s32[16,128]{1,0:T(8,128)S(1)}, s32[16,128]{1,0:T(8,128)}, u32[]{:S(2)}) copy-start(s32[16,128]{1,0:T(8,128)} %mask.3) | copy-start | bytes 24580
  36.6 1.3 %collective-permute-start.19 = (f32[168,128]{1,0:T(8,128)S(1)}, f32[168,128]{1,0:T(8,128)S(1)}, u32[]{:S(2)}, u32[]{:S(2)}) collective-permute-start(f32[168,128]{1,0:T(8,128)S(1)} %get-tuple-element.65), channel_id=1, source_target_pairs={{0,4},{4,0},{8,12},{12,8},{16,20},{20,16},{24,28},{28,24},{1,5},{5... | collective-permute-start | bytes 258056 | tf_op jit(solution)/shard_map/ppermute | solution.py:616
  37.9 5.3 %collective-permute-start.20 = (f32[168,128]{1,0:T(8,128)S(1)}, f32[168,128]{1,0:T(8,128)S(1)}, u32[]{:S(2)}, u32[]{:S(2)}) collective-permute-start(f32[168,128]{1,0:T(8,128)S(1)} %add.15), channel_id=1, source_target_pairs={{0,8},{4,12},{8,0},{12,4},{16,24},{20,28},{24,16},{28,20},{1,9},{5... | collective-permute-start | bytes 258056 | tf_op jit(solution)/shard_map/ppermute | solution.py:616
  43.3 4.6 %collective-permute-start.21 = (f32[168,128]{1,0:T(8,128)S(1)}, f32[168,128]{1,0:T(8,128)S(1)}, u32[]{:S(2)}, u32[]{:S(2)}) collective-permute-start(f32[168,128]{1,0:T(8,128)S(1)} %add.16), channel_id=1, source_target_pairs={{0,16},{4,20},{8,24},{12,28},{16,0},{20,4},{24,8},{28,12},{1,17},{... | collective-permute-start | bytes 258056 | tf_op jit(solution)/shard_map/ppermute | solution.py:616
  47.8 9.9 %collective-permute-start.22 = (f32[168,128]{1,0:T(8,128)S(1)}, f32[168,128]{1,0:T(8,128)S(1)}, u32[]{:S(2)}, u32[]{:S(2)}) collective-permute-start(f32[168,128]{1,0:T(8,128)S(1)} %add.17), channel_id=1, source_target_pairs={{0,1},{1,0},{2,3},{3,2},{4,5},{5,4},{6,7},{7,6},{8,9},{9,8},{10,11... | collective-permute-start | bytes 258056 | tf_op jit(solution)/shard_map/ppermute | solution.py:616
  57.8 5.7 %collective-permute-start.23 = (f32[168,128]{1,0:T(8,128)S(1)}, f32[168,128]{1,0:T(8,128)S(1)}, u32[]{:S(2)}, u32[]{:S(2)}) collective-permute-start(f32[168,128]{1,0:T(8,128)S(1)} %add.18), channel_id=1, source_target_pairs={{0,2},{1,3},{2,0},{3,1},{4,6},{5,7},{6,4},{7,5},{8,10},{9,11},{10,... | collective-permute-start | bytes 258056 | tf_op jit(solution)/shard_map/ppermute | solution.py:616
  63.5 1.3 %collective-permute-start.24 = (f32[168,128]{1,0:T(8,128)S(1)}, f32[168,128]{1,0:T(8,128)S(1)}, u32[]{:S(2)}, u32[]{:S(2)}) collective-permute-start(f32[168,128]{1,0:T(8,128)S(1)} %add.19.total), channel_id=1, source_target_pairs={{0,4},{4,0},{8,12},{12,8},{16,20},{20,16},{24,28},{28,24},{1,5},{5... | collective-permute-start | bytes 258056 | tf_op jit(solution)/shard_map/ppermute | solution.py:616

commit v4 on v3

--- a/solution.py
+++ b/solution.py
@@ -24,11 +24,18 @@
     return lax.broadcasted_iota(jnp.int32, shape, 1)
 
 
-def pack_kernel(fields, cot, mask, ft, gt, first, second, plane):
+def pack_kernel(fields_far, cot_far, mask_far, ft, gt, first, second, plane, fields, cot, mask, arrived):
     chans, rows, _ = fields.shape
     groups = chans // 8
-    sea = mask[...].astype(F32)
+    pairs = ((fields_far, fields), (cot_far, cot), (mask_far, mask))
+    copies = [pltpu.make_async_copy(src, dst, arrived.at[k]) for k, (src, dst) in enumerate(pairs)]
+    for copy in copies:
+        copy.start()
     for turn, dst in ((0, ft), (1, gt)):
+        copies[turn].wait()
+        if turn == 1:
+            copies[2].wait()
+            sea = mask[...].astype(F32)
         for c in range(chans):
             if turn == 0:
                 cell = fields[c].astype(F32)
@@ -175,7 +182,41 @@
     return cdf, dens
 
 
-def main_kernel(
+def edge_mask(lane, s):
+    return lane < s if s > 0 else lane >= LANES + s
+
+
+def rows_of(r, g, chans):
+    return pl.ds(pl.multiple_of(r * chans + g * 8, 8), 8)
+
+
+def twice(x):
+    return jnp.concatenate([x, x], axis=1)
+
+
+def norm_and_back(x, g, vecs, up_aug, up_t, down_t):
+    gain, bias, scale = twice(vecs[0]), twice(vecs[1]), twice(vecs[2])
+    centred = x - jnp.mean(x, axis=0, keepdims=True)
+    var = jnp.mean(centred * centred, axis=0, keepdims=True)
+    rstd = lax.rsqrt(var + 1e-06)
+    xhat = centred * rstd
+    pad = (up_aug.shape[1] - x.shape[0], x.shape[1])
+    ones = (lax.broadcasted_iota(jnp.int32, pad, 0) == 0).astype(F32).astype(BF)
+    normed = jnp.concatenate([(xhat * gain + bias).astype(BF), ones], axis=0)
+    pre = jnp.dot(up_aug[...], normed, preferred_element_type=F32)
+    cdf, dens = normal_terms(pre)
+    d_branch = (g * scale).astype(BF)
+    d_hidden = jnp.dot(down_t[...], d_branch, preferred_element_type=F32)
+    d_pre = (d_hidden * (cdf + pre * dens)).astype(BF)
+    d_normed = jnp.dot(up_t[...], d_pre, preferred_element_type=F32)
+    gd = d_normed * gain
+    m1 = jnp.mean(gd, axis=0, keepdims=True)
+    m2 = jnp.mean(gd * xhat, axis=0, keepdims=True)
+    dx = (rstd * (gd - m1 - xhat * m2)).astype(BF).astype(F32)
+    return dx, (pre, cdf, d_branch, d_pre, d_normed, normed, xhat, scale)
+
+
+def own_kernel(
     ft,
     gt,
     low,
@@ -191,15 +232,14 @@
     down,
     down_t,
     out,
-    grad,
+    conv_halo,
+    dcv,
     kept,
     passed,
     ext,
     rim,
     rhs,
     conv,
-    cots,
-    dcv,
     plane,
     band,
     band_up,
@@ -218,24 +258,7 @@
     top = lax.axis_index("lat") == lax.axis_size("lat") - 1
     lane = lane_iota((8, LANES))
     wide = slice(0, LANES), slice(LANES, 2 * LANES)
-
-    for r in range(rows):
-        cots[(r + 3) * chans : (r + 4) * chans, :] = gt[r].astype(F32)
-    for r in range(3):
-        cots[r * chans : (r + 1) * chans, :] = low[6 + r].astype(F32)
-        cots[(rows + 3 + r) * chans : (rows + 4 + r) * chans, :] = up[6 + r].astype(F32)
-    lane_c = lane_iota((chans, LANES))
-    for k, got in ((0, got_l), (1, got_r)):
-        first = shift(got[:, wide[0]].astype(F32), -84)
-        second = shift(got[:, wide[1]].astype(F32), 33 - 84)
-        value = jnp.where(lane_c < 33, first, jnp.where(lane_c < 3 * mid, second, 0.0))
-        cots[(mid + k) * chans : (mid + k + 1) * chans, :] = value
-
-    def edge_mask(s):
-        return lane < s if s > 0 else lane >= LANES + s
-
-    def at_row(r, g):
-        return pl.ds(pl.multiple_of(r * chans + g * 8, 8), 8)
+    at_row = lambda r, g: rows_of(r, g, chans)
 
     def conv_group(g, _):
         at = pl.ds(pl.multiple_of(g * 8, 8), 8)
@@ -282,17 +305,22 @@
                 part = slice(q * step + 8 * i, q * step + 8 * i + 8)
                 mine, edge = prod[part, wide[0]], prod[part, wide[1]]
                 if q != 3:
-                    swap = edge_mask(q - 3)
+                    swap = edge_mask(lane, q - 3)
                     mine, edge = jnp.where(swap, edge, mine), jnp.where(swap, mine, edge)
                     mine, edge = shift(mine, 3 - q), shift(edge, 3 - q)
                 inner = mine if inner is None else inner + mine
                 outer = edge if outer is None else outer + edge
-            conv[at_row(o, g), :] = inner
+            if o < 3:
+                conv_halo[at_row(o, g), :] = inner
+            elif o < rows + 3:
+                conv[at_row(o - 3, g), :] = inner
+            else:
+                conv_halo[at_row(o - rows, g), :] = inner
             inside = (lane >= 3 * o) & (lane < 3 * o + 3)
             sides[0] = jnp.where(inside, shift(outer, 3 * o + 3), sides[0])
             sides[1] = jnp.where(inside, shift(outer, 3 * o), sides[1])
         for k in (0, 1):
-            conv[at_row(mid + k, g), :] = sides[k]
+            conv_halo[at_row(6 + k, g), :] = sides[k]
         return 0
 
     lax.fori_loop(0, groups, conv_group, 0)
@@ -300,74 +328,131 @@
     g_down[...] = jnp.zeros_like(g_down)
     g_up[...] = jnp.zeros_like(g_up)
     sums[...] = jnp.zeros_like(sums)
-    pad_rows = up_aug.shape[1] - chans
-    ones = (lax.broadcasted_iota(jnp.int32, (pad_rows, 2 * LANES), 0) == 0).astype(F32).astype(BF)
-
-    def twice(x):
-        return jnp.concatenate([x, x], axis=1)
 
     def unit(u):
         return pl.ds(pl.multiple_of(u * chans, chans), chans)
 
-    def pair_of(ref, units):
-        return jnp.concatenate([ref[unit(u), :] for u in units], axis=1)
-
-    def block(units, own):
-        gain, bias, scale = twice(vecs[0]), twice(vecs[1]), twice(vecs[2])
-        x = pair_of(conv, units)
-        centred = x - jnp.mean(x, axis=0, keepdims=True)
-        var = jnp.mean(centred * centred, axis=0, keepdims=True)
-        rstd = lax.rsqrt(var + 1e-06)
-        xhat = centred * rstd
-        normed = (xhat * gain + bias).astype(BF)
-        normed = jnp.concatenate([normed, ones], axis=0)
-        pre = jnp.dot(up_aug[...], normed, preferred_element_type=F32)
-        cdf, dens = normal_terms(pre)
-        g = pair_of(cots, units)
-        d_branch = (g * scale).astype(BF)
-        d_hidden = jnp.dot(down_t[...], d_branch, preferred_element_type=F32)
-        d_pre = (d_hidden * (cdf + pre * dens)).astype(BF)
-        d_normed = jnp.dot(up_t[...], d_pre, preferred_element_type=F32)
-        if own:
-            hidden = (pre * cdf).astype(BF)
-            branch = jnp.dot(down[...], hidden, preferred_element_type=F32)
-            sea = [mask[pl.ds(u - 3, 1), :].astype(F32) for u in units]
-            fields = jnp.concatenate([ext[unit(u + 3), :] for u in units], axis=1)
-            res = (fields + scale * branch) * jnp.concatenate(sea, axis=1)
-            for k, u in enumerate(units):
-                for gr in range(groups):
-                    plane[0, pl.ds(gr * 8 * rows + u - 3, 8, stride=rows), :] = res[gr * 8 : gr * 8 + 8, wide[k]]
-            g_down[...] += lax.dot_general(d_branch, hidden, NT, preferred_element_type=F32)
-            g_up[...] += lax.dot_general(normed, d_pre, NT, preferred_element_type=F32)
-            for k, value in enumerate((d_normed * xhat, d_normed, g * branch)):
-                sums[k] += value[:, :LANES] + value[:, LANES:]
-        gd = d_normed * gain
-        m1 = jnp.mean(gd, axis=0, keepdims=True)
-        m2 = jnp.mean(gd * xhat, axis=0, keepdims=True)
-        dx = (rstd * (gd - m1 - xhat * m2)).astype(BF).astype(F32)
+    def own_block(b, _):
+        units = (b * 2, b * 2 + 1)
+        x = jnp.concatenate([conv[unit(u), :] for u in units], axis=1)
+        g = jnp.concatenate([gt[u].astype(F32) for u in units], axis=1)
+        dx, (pre, cdf, d_branch, d_pre, d_normed, normed, xhat, scale) = norm_and_back(
+            x, g, vecs, up_aug, up_t, down_t
+        )
+        hidden = (pre * cdf).astype(BF)
+        branch = jnp.dot(down[...], hidden, preferred_element_type=F32)
+        sea = [mask[pl.ds(u, 1), :].astype(F32) for u in units]
+        fields = jnp.concatenate([ft[u].astype(F32) for u in units], axis=1)
+        res = (fields + scale * branch) * jnp.concatenate(sea, axis=1)
         for k, u in enumerate(units):
+            for gr in range(groups):
+                plane[pl.ds(gr * 8 * rows + u, 8, stride=rows), :] = res[gr * 8 : gr * 8 + 8, wide[k]]
             dcv[unit(u), :] = dx[:, wide[k]]
-
-    def own_block(b, _):
-        block((b * 2 + 3, b * 2 + 4), True)
+        g_down[...] += lax.dot_general(d_branch, hidden, NT, preferred_element_type=F32)
+        g_up[...] += lax.dot_general(normed, d_pre, NT, preferred_element_type=F32)
+        for k, value in enumerate((d_normed * xhat, d_normed, g * branch)):
+            sums[k] += value[:, :LANES] + value[:, LANES:]
         return 0
 
+    lax.fori_loop(0, rows // 2, own_block, 0)
+
+    def taps_group(g, _):
+        at = pl.ds(pl.multiple_of(g * 8, 8), 8)
+        line = jnp.zeros((8, LANES), F32)
+        for q in range(7):
+            own = [shift(dcv[at_row(o, g), :], q - 3) for o in range(rows)]
+            tot = [None] * 7
+            for r in range(mid):
+                value = ext[at_row(r + 3, g), :]
+                if q != 3:
+                    value = jnp.where(edge_mask(lane, q - 3), rim[at_row(r + 3, g), :], value)
+                for a in range(7):
+                    o = r - a
+                    if 0 <= o < rows:
+                        term = value * own[o]
+                        tot[a] = term if tot[a] is None else tot[a] + term
+            for a in range(7):
+                total = jnp.sum(tot[a], axis=1, keepdims=True)
+                line = jnp.where(lane == 8 * a + q, total, line)
+        for k in range(3):
+            total = jnp.sum(sums[k, at, :], axis=1, keepdims=True)
+            line = jnp.where(lane == 56 + k, total, line)
+        taps_g[at, :] = line
+        return 0
+
+    lax.fori_loop(0, groups, taps_group, 0)
+    small = taps_g[...]
+    cut = 40
+
+    def fill(lower, upper):
+        for h, w in enumerate(wide):
+            lower[h * chans : (h + 1) * chans, :] = g_down[:, w]
+            upper[h * chans : (h + 1) * chans, :] = g_up[0:chans, w]
+            upper[2 * chans + 24 + 8 * h : 2 * chans + 32 + 8 * h, :] = g_up[chans : chans + 8, w]
+        lower[2 * chans : 2 * chans + cut, :] = small[:cut]
+        upper[2 * chans : 2 * chans + 24, :] = small[cut:]
+
+    @pl.when(odd_core == 0)
+    def _():
+        fill(kept, passed)
+
+    @pl.when(odd_core == 1)
+    def _():
+        fill(passed, kept)
+
+    for c in range(chans):
+        out[c] = plane[c * rows : (c + 1) * rows, :].astype(BF)
+
+
+def halo_kernel(conv_halo, low, up, got_l, got_r, vecs, up_aug, up_t, down_t, dcv_halo, cots):
+    _, chans, _ = low.shape
+    lane_c = lane_iota((chans, LANES))
+    wide = slice(0, LANES), slice(LANES, 2 * LANES)
+    for r in range(3):
+        cots[r * chans : (r + 1) * chans, :] = low[6 + r].astype(F32)
+        cots[(3 + r) * chans : (4 + r) * chans, :] = up[6 + r].astype(F32)
+    for k, got in ((0, got_l), (1, got_r)):
+        first = shift(got[:, wide[0]].astype(F32), -84)
+        second = shift(got[:, wide[1]].astype(F32), 33 - 84)
+        value = jnp.where(lane_c < 33, first, jnp.where(lane_c < 66, second, 0.0))
+        cots[(6 + k) * chans : (7 + k) * chans, :] = value
+
     def halo_block(b, _):
-        one = jnp.where(b < 2, 2 * b, rows + 2 * b)
-        two = jnp.where(b == 0, 1, rows + 1 + 2 * b)
-        block((one, two), False)
+        units = [pl.ds(pl.multiple_of((2 * b + k) * chans, chans), chans) for k in (0, 1)]
+        x = jnp.concatenate([conv_halo[u, :] for u in units], axis=1)
+        g = jnp.concatenate([cots[u, :] for u in units], axis=1)
+        dx, _ = norm_and_back(x, g, vecs, up_aug, up_t, down_t)
+        for k, u in enumerate(units):
+            dcv_halo[u, :] = dx[:, wide[k]]
         return 0
 
-    lax.fori_loop(0, rows // 2, own_block, 0)
     lax.fori_loop(0, 4, halo_block, 0)
+
+
+def adjoint_kernel(part, *refs):
+    dcv, dcv_halo, gt, plain, turned = refs[:5]
+    grad, rhs, plane, band, band_up, prod_1, prod_3 = refs[-7:]
+    rows, chans, cols = gt.shape
+    some = grad.shape[0]
+    first = part * (some // 8)
+    mid = rows + 6
+    top = lax.axis_index("lat") == lax.axis_size("lat") - 1
+    lane = lane_iota((8, LANES))
+    wide = slice(0, LANES), slice(LANES, 2 * LANES)
+    at_row = lambda r, g: rows_of(r, g, chans)
 
     def adjoint_group(g, _):
         at = pl.ds(pl.multiple_of(g * 8, 8), 8)
-        left, right = dcv[at_row(mid, g), :], dcv[at_row(mid + 1, g), :]
+        left, right = dcv_halo[at_row(6, g), :], dcv_halo[at_row(7, g), :]
         for r0 in range(0, mid, 2):
             pair = []
             for r in (r0, r0 + 1):
-                value = dcv[at_row(r, g), :]
+                if r < 3:
+                    value = dcv_halo[at_row(r, g), :]
+                elif r < rows + 3:
+                    value = dcv[at_row(r - 3, g), :]
+                else:
+                    value = dcv_halo[at_row(r - rows, g), :]
                 beyond = jnp.where(lane < 64, shift(right, -3 * r), shift(left, LANES - 3 - 3 * r))
                 pair.append(jnp.concatenate([value, beyond], axis=1))
             rhs[8 * r0 : 8 * r0 + 16, :] = jnp.concatenate(pair, axis=0).astype(BF)
@@ -385,59 +470,19 @@
         prod_3[...] = jnp.dot(band_up[:, 0:96], rhs[80:176, :], preferred_element_type=F32)
         for o in range(rows):
             prod, step, i = (prod_1, 80, o) if o < 10 else (prod_3, 48, o - 10)
-            inner = cots[at_row(o + 3, g), :]
+            inner = gt[o, at, :].astype(F32)
             for q in range(7):
                 part = slice(q * step + 8 * i, q * step + 8 * i + 8)
                 mine = prod[part, wide[0]]
                 if q != 3:
-                    mine = shift(jnp.where(edge_mask(q - 3), prod[part, wide[1]], mine), 3 - q)
+                    mine = shift(jnp.where(edge_mask(lane, q - 3), prod[part, wide[1]], mine), 3 - q)
                 inner = inner + mine
-            plane[1, pl.ds(g * (8 * rows) + o, 8, stride=rows), :] = inner
-        line = jnp.zeros((8, LANES), F32)
-        for q in range(7):
-            own = [shift(dcv[at_row(o + 3, g), :], q - 3) for o in range(rows)]
-            tot = [None] * 7
-            for r in range(mid):
-                value = ext[at_row(r + 3, g), :]
-                if q != 3:
-                    value = jnp.where(edge_mask(q - 3), rim[at_row(r + 3, g), :], value)
-                for a in range(7):
-                    o = r - a
-                    if 0 <= o < rows:
-                        term = value * own[o]
-                        tot[a] = term if tot[a] is None else tot[a] + term
-            for a in range(7):
-                total = jnp.sum(tot[a], axis=1, keepdims=True)
-                line = jnp.where(lane == 8 * a + q, total, line)
-        for k in range(3):
-            total = jnp.sum(sums[k, at, :], axis=1, keepdims=True)
-            line = jnp.where(lane == 56 + k, total, line)
-        taps_g[at, :] = line
+            plane[pl.ds((g - first) * (8 * rows) + o, 8, stride=rows), :] = inner
         return 0
 
-    lax.fori_loop(0, groups, adjoint_group, 0)
-    small = taps_g[...]
-    cut = 40
-
-    def fill(lower, upper):
-        for h, w in enumerate(wide):
-            lower[h * chans : (h + 1) * chans, :] = g_down[:, w]
-            upper[h * chans : (h + 1) * chans, :] = g_up[0:chans, w]
-            upper[2 * chans + 24 + 8 * h : 2 * chans + 32 + 8 * h, :] = g_up[chans : chans + 8, w]
-        lower[2 * chans : 2 * chans + cut, :] = small[:cut]
-        upper[2 * chans : 2 * chans + 24, :] = small[cut:]
-
-    @pl.when(odd_core == 0)
-    def _():
-        fill(kept, passed)
-
-    @pl.when(odd_core == 1)
-    def _():
-        fill(passed, kept)
-
-    for c in range(chans):
-        out[c] = plane[0, c * rows : (c + 1) * rows, :].astype(BF)
-        grad[c] = plane[1, c * rows : (c + 1) * rows, :].astype(BF)
+    lax.fori_loop(first, first + some // 8, adjoint_group, 0)
+    for c in range(some):
+        grad[c] = plane[c * rows : (c + 1) * rows, :].astype(BF)
 
 
 def finish_kernel(total, other, g_depth, g_gain, g_bias, g_up, g_up_b, g_down, g_scale):
@@ -502,12 +547,18 @@
     ft, gt, first, second = pl.pallas_call(
         pack_kernel,
         out_shape=[sds((rows, chans, cols), BF)] * 2 + [sds((9, chans, cols), BF)] * 2,
-        in_specs=vmem(3),
+        in_specs=[pl.BlockSpec(memory_space=pltpu.HBM)] * 3,
         out_specs=vmem(4),
-        scratch_shapes=[pltpu.VMEM((2, chans * rows, cols), F32)],
+        scratch_shapes=[
+            pltpu.VMEM((2, chans * rows, cols), F32),
+            pltpu.VMEM((chans, rows, cols), BF),
+            pltpu.VMEM((chans, rows, cols), BF),
+            pltpu.VMEM((rows, cols), jnp.int32),
+            pltpu.SemaphoreType.DMA((3,)),
+        ],
         compiler_params=pltpu.CompilerParams(vmem_limit_bytes=8 * 2**20),
         name="pack",
-    )(fields[0], cotangent[0], ocean_mask)
+    )(*[pltpu.with_memory_space_constraint(v, pltpu.HBM) for v in (fields[0], cotangent[0], ocean_mask)])
 
     at = lambda lon, lat: (lon % n_lon) * n_lat + lat
     rounds = [[], []]
@@ -528,7 +579,8 @@
                 [(at(lon, n_lat - 1), at(k - j - lon, n_lat - 1)) for lon in range(n_lon)] for j in (0, 1)
             ]
             plan = rounds[fold_round] + mirror[0]
-            return lax.ppermute(top, axes, plan), lax.ppermute(top, axes, mirror[1])
+            last = lax.ppermute(top, axes, mirror[1])
+            return lax.ppermute(top, axes, plan), last
 
         return run
 
@@ -569,33 +621,38 @@
         up_weight.T,
         down_weight,
     )
-    units = rows + 8
     big, small = 2 * chans, 40
-    output, grad, kept, passed = pl.pallas_call(
-        main_kernel,
-        out_shape=[sds((chans, rows, cols), BF)] * 2 + [sds((big + small, LANES), F32)] * 2,
+    up_t = up_weight.T
+    band_rows = (rows + 12) * 8
+    output, conv_halo, dcv, kept, passed = pl.pallas_call(
+        own_kernel,
+        out_shape=[
+            sds((chans, rows, cols), BF),
+            sds((8 * chans, cols), F32),
+            sds((rows * chans, cols), F32),
+            sds((big + small, LANES), F32),
+            sds((big + small, LANES), F32),
+        ],
         in_specs=vmem(14),
-        out_specs=vmem(4),
+        out_specs=vmem(5),
         scratch_shapes=[
             pltpu.VMEM(((rows + 12) * chans, cols), F32),
             pltpu.VMEM(((rows + 12) * chans, cols), F32),
-            pltpu.VMEM(((rows + 12) * 8, 2 * cols), BF),
-            pltpu.VMEM((units * chans, cols), F32),
-            pltpu.VMEM((units * chans, cols), F32),
-            pltpu.VMEM((units * chans, cols), F32),
-            pltpu.VMEM((2, chans * rows, cols), F32),
+            pltpu.VMEM((band_rows, 2 * cols), BF),
+            pltpu.VMEM((rows * chans, cols), F32),
+            pltpu.VMEM((chans * rows, cols), F32),
             pltpu.VMEM((7 * 80, LANES), BF),
-            pltpu.VMEM((7 * 48, LANES), BF),
+            pltpu.VMEM((7 * 32, LANES), BF),
             pltpu.VMEM((7 * 80, 2 * cols), F32),
             pltpu.VMEM((7 * 80, 2 * cols), F32),
-            pltpu.VMEM((7 * 48, 2 * cols), F32),
+            pltpu.VMEM((7 * 32, 2 * cols), F32),
             pltpu.VMEM((chans, hidden_n), F32),
             pltpu.VMEM((chans + 16, hidden_n), F32),
             pltpu.VMEM((3, chans, LANES), F32),
             pltpu.VMEM((chans, LANES), F32),
         ],
         compiler_params=pltpu.CompilerParams(vmem_limit_bytes=20 * 2**20),
-        name="block",
+        name="own",
     )(
         ft,
         gt,
@@ -608,17 +665,59 @@
         turned,
         vecs,
         up_aug,
-        up_weight.T,
+        up_t,
         down_weight,
         down_t,
     )
 
+    dcv_halo = pl.pallas_call(
+        halo_kernel,
+        out_shape=sds((8 * chans, cols), F32),
+        in_specs=vmem(9),
+        out_specs=vmem(1)[0],
+        scratch_shapes=[pltpu.VMEM((8 * chans, cols), F32)],
+        cost_estimate=pl.CostEstimate(flops=150_000_000, bytes_accessed=2**20, transcendentals=2**18),
+        compiler_params=pltpu.CompilerParams(vmem_limit_bytes=8 * 2**20),
+        name="halo",
+    )(conv_halo, low, up, got_l, got_r, vecs, up_aug, up_t, down_t)
+
+    def adjoint(part, *earlier):
+        half = chans // 2
+        return pl.pallas_call(
+            functools.partial(adjoint_kernel, part),
+            grid=(1,),
+            out_shape=sds((chans, rows, cols), BF),
+            in_specs=vmem(5) + [pl.BlockSpec(memory_space=pl.ANY)] * len(earlier),
+            out_specs=pl.BlockSpec((half, rows, cols), lambda _: (part, 0, 0)),
+            scratch_shapes=[
+                pltpu.VMEM((band_rows, 2 * cols), BF),
+                pltpu.VMEM((half * rows, cols), F32),
+                pltpu.VMEM((7 * 80, LANES), BF),
+                pltpu.VMEM((7 * 48, LANES), BF),
+                pltpu.VMEM((7 * 80, 2 * cols), F32),
+                pltpu.VMEM((7 * 48, 2 * cols), F32),
+            ],
+            input_output_aliases={5: 0} if earlier else {},
+            cost_estimate=pl.CostEstimate(flops=200_000_000, bytes_accessed=2**21, transcendentals=0),
+            compiler_params=pltpu.CompilerParams(vmem_limit_bytes=12 * 2**20),
+            name="adjoint",
+        )(dcv, dcv_halo, gt, plain, turned, *earlier)
+
     flip = lambda y, axis, b: lax.ppermute(y, axis, [(i, i ^ b) for i in range(lax.axis_size(axis))])
     total = kept + flip(passed, "lon", 1)
-    for axis, b in [("lon", 1 << i) for i in range(1, n_lon.bit_length() - 1)] + [
-        ("lat", 1 << i) for i in range(n_lat.bit_length() - 1)
-    ]:
+    steps = [("lon", 1 << i) for i in range(1, n_lon.bit_length() - 1)]
+    steps += [("lat", 1 << i) for i in range(n_lat.bit_length() - 1)]
+    grad = None
+    for k, (axis, b) in enumerate(steps):
         total = total + flip(total, axis, b)
+        if k == 0:
+            total, dcv_halo = lax.optimization_barrier((total, dcv_halo))
+        elif k == 1:
+            grad = adjoint(0)
+            total, grad = lax.optimization_barrier((total, grad))
+        elif k == 2:
+            grad = adjoint(1, grad)
+            total, grad = lax.optimization_barrier((total, grad))
     other = flip(total, "lon", 1)
     g_depth, g_gain, g_bias, g_up, g_up_b, g_down, g_scale = pl.pallas_call(
         finish_kernel,

time: 66.3 us -> 62.2 us (0.938)
  waiting for transfers between devices: 14.1 us -> 7.39 us
  Pallas kernels: 21.7 us -> 25.5 us
  local copies, waits for them, and re-layouts: 4.32 us -> 1.73 us
  starting transfers between devices: 22.6 us -> 24.3 us
    ppermute x6, waiting for transfers between devices: 14 us -> 7.23 us  [shards(): lax.ppermute(y, axis, [(i, i ^ b) for i in range(lax.axis_size(axis))])]
    pallas_call x1 -> x4, Pallas kernels: 18.3 us -> 21.1 us  [the longest x1 14.4 us: shards(): pl.pallas_call(own_kernel, out_shape=[sds((chans, rows, cols), BF), sds((...]
    unnamed x24 -> x18, local copies, waits for them, and re-layouts: 3.81 us -> 1.22 us
    ppermute x6, starting transfers between devices: 14.2 us -> 15.8 us  [shards(): lax.ppermute(y, axis, [(i, i ^ b) for i in range(lax.axis_size(axis))])]
    pallas_call x1, Pallas kernels: 0.38 us -> 1.37 us  [shards(): pl.pallas_call(pack_kernel, out_shape=[sds((rows, chans, cols), BF)] * 2...]
  transfers between devices with their start and end apart: 11 -> 11, of which waited for: 7 -> 6; matrix products, arithmetic and copies ran while one was open for 1% -> 1% of each run, Pallas kernels for 1% -> 12%
where the time goes in v4:
time: 62.2 us; the launch traced here: 61.7 us
  Pallas kernels  25.5 us (41%)
  starting transfers between devices  24.3 us (39%)
  waiting for transfers between devices  7.39 us (12%)
  between operations  2.73 us (4%)
  local copies, waits for them, and re-layouts  1.73 us (3%)
    ppermute x6, starting transfers between devices, shards(): lax.ppermute(y, axis, [(i, i ^ b) for i in range(lax.axis_size(axis))])  15.8 us
    pallas_call x1, Pallas kernels, shards(): pl.pallas_call(own_kernel, out_shape=[sds((chans, rows, cols), BF), sds((...  14.4 us
    ppermute x6, waiting for transfers between devices, shards(): lax.ppermute(y, axis, [(i, i ^ b) for i in range(lax.axis_size(axis))])  7.23 us
    pallas_call x2, Pallas kernels, adjoint(): pl.pallas_call(functools.partial(adjoint_kernel, part), grid=(1,), out_sh...  4.83 us
    ppermute x1, starting transfers between devices, shards(): met = lax.ppermute(sends[plain_round], axes, rounds[plain_round])  3.13 us
    ppermute x1, starting transfers between devices, shards(): lax.ppermute(sent_l, 'lon', [(i, (i - 1) % n_lon) for i in range(n_lon)])  2.63 us
    pallas_call x1, Pallas kernels, shards(): pl.pallas_call(halo_kernel, out_shape=sds((8 * chans, cols), F32), in_spe...  1.9 us
    pallas_call x1, Pallas kernels, shards(): pl.pallas_call(functools.partial(edge_kernel, fold_round == 0), out_shape...  1.53 us
  transfers between devices with their start and end apart: 11, of which 6 were waited for; matrix products, arithmetic and copies ran while one was open for 1% of the time, Pallas kernels for 12%

profile of v4, /device:TPU:0, one launch (start us, length us, event | category | flops | bytes accessed | tf_op | source)
XLA Modules:
  0.0 61.7 jit_solution(16236727375033878682)
XLA Ops:
  0.7 1.4 %pack.1 = (bf16[16,64,128]{2,1,0:T(8,128)(2,1)S(1)}, bf16[16,64,128]{2,1,0:T(8,128)(2,1)S(1)}, bf16[9,64,128]{2,1,0:T(8,128)(2,1)S(1)}, bf16[9,64,128]{2,1,0:T(8,128)(2,1)S(1)}) custom-call(bf16[64,16,128]{2,1,0:T(8,128)(2,1)} %bitcast.16, bf16[64,16,128]{2,1,0:T(8,128)(2,1)} %bitcast.17, s32[16,128]{1,0:T(8,128)} %mask.1), custom_call_target="tpu_custom_call" | custom-call | tf_op jit(solution)/shard_map/pack/pallas_call | solution.py:547
  2.0 3.1 %collective-permute-start.16 = (bf16[9,64,128]{2,1,0:T(8,128)(2,1)S(1)}, bf16[9,64,128]{2,1,0:T(8,128)(2,1)S(1)}, u32[]{:S(2)}, u32[]{:S(2)}) collective-permute-start(bf16[9,64,128]{2,1,0:T(8,128)(2,1)S(1)} %get-tuple-element.54), channel_id=1, source_target_pairs={{0,1},{1,0},{4,5},{5,4},{8,9},{9,8},{12,13},{13,12},{16,17},{17,16... | collective-permute-start | bytes 442376 | tf_op jit(solution)/shard_map/ppermute | solution.py:573
  5.2 0.5 slice.3
  7.6 2.7 %conditional.1 = (bf16[9,64,128]{2,1,0:T(8,128)(2,1)}, bf16[9,64,128]{2,1,0:T(8,128)(2,1)}) conditional(s32[]{:T(128)} %clamp.3, bf16[9,64,128]{2,1,0:T(8,128)(2,1)S(1)} %get-tuple-element.57, bf16[9,64,128]{2,1,0:T(8,128)(2,1)S(1)} %get-tuple-element.57, bf16[9,64,128]{2,1,0:T(8,128)(2,1)S(1)} %get-tuple-element.57, ...), branch_computations={%region_0.0_spmd, %region_1.0_spmd, %region_2.0_spmd, %region_3.0_... | conditional | bytes 1179744 | solution.py:588
  7.7 1.3 %collective-permute-start.15 = (bf16[9,64,128]{2,1,0:T(8,128)(2,1)S(1)}, bf16[9,64,128]{2,1,0:T(8,128)(2,1)}, u32[]{:S(2)}, u32[]{:S(2)}) collective-permute-start(bf16[9,64,128]{2,1,0:T(8,128)(2,1)S(1)} %param.7), channel_id=1, source_target_pairs={{3,27},{7,23},{11,19},{15,15},{19,11},{23,7},{27,3},{31,31}} | collective-permute-start | bytes 442376 | tf_op jit(solution)/shard_map/cond/branch_7_fun/ppermute | solution.py:582
  9.0 1.3 %collective-permute-start.14 = (bf16[9,64,128]{2,1,0:T(8,128)(2,1)S(1)}, bf16[9,64,128]{2,1,0:T(8,128)(2,1)}, u32[]{:S(2)}, u32[]{:S(2)}) collective-permute-start(bf16[9,64,128]{2,1,0:T(8,128)(2,1)S(1)} %param.7), channel_id=1, source_target_pairs={{1,2},{2,1},{5,6},{6,5},{9,10},{10,9},{13,14},{14,13},{17,18},{18,... | collective-permute-start | bytes 442376 | tf_op jit(solution)/shard_map/cond/branch_7_fun/ppermute | solution.py:583
  10.4 1.5 %edges.1 = (bf16[9,64,128]{2,1,0:T(8,128)(2,1)S(1)}, bf16[9,64,128]{2,1,0:T(8,128)(2,1)S(1)}, bf16[64,256]{1,0:T(8,128)(2,1)S(1)}, bf16[64,256]{1,0:T(8,128)(2,1)S(1)}) custom-call(s32[1024]{0:T(1024)S(1)} %copy-done.3, s32[8,128]{1,0:T(8,128)S(1)} %bitcast.13, bf16[9,64,128]{2,1,0:T(8,128)(2,1)S(1)} %collective-permute-done.16.got_a, ...), custom_call_target="tpu_custom_call" | custom-call | tf_op jit(solution)/shard_map/edges/pallas_call | solution.py:590
  11.9 0.1 collective-permute-start.17
  12.0 2.6 %collective-permute-start.18 = (bf16[64,256]{1,0:T(8,128)(2,1)S(1)}, bf16[64,256]{1,0:T(8,128)(2,1)S(1)}, u32[]{:S(2)}, u32[]{:S(2)}) collective-permute-start(bf16[64,256]{1,0:T(8,128)(2,1)S(1)} %get-tuple-element.63), channel_id=1, source_target_pairs={{0,28},{4,0},{8,4},{12,8},{16,12},{20,16},{24,20},{28,24},{1,29},{... | collective-permute-start | bytes 98312 | tf_op jit(solution)/shard_map/ppermute | solution.py:599
  14.6 0.6 copy-done.5
  15.3 0.0 copy-done.6
  15.3 0.0 copy-done.7
  15.3 0.7 %weights.1 = (f32[7,64,128]{2,1,0:T(8,128)S(1)}, f32[7,64,128]{2,1,0:T(8,128)S(1)}, f32[3,64,128]{2,1,0:T(8,128)S(1)}, bf16[256,80]{1,0:T(8,128)(2,1)S(1)}, bf16[256,64]{1,0:T(8,128)(2,1)S(1)}) custom-call(bf16[7,7,64]{2,1,0:T(8,128)(2,1)S(1)} %bitcast.14, bf16[64]{0:T(256)(128)(2,1)S(1)} %copy-done.5, bf16[64]{0:T(256)(128)(2,1)S(1)} %copy-done.6, ...), custom_call_target="tpu_custom_call" | custom-call | tf_op jit(solution)/shard_map/weights/pallas_call | solution.py:601
  16.0 0.1 collective-permute-done.17.got_l
  16.2 0.5 copy-done.2
  16.7 14.4 %own.1 = (bf16[64,16,128]{2,1,0:T(8,128)(2,1)}, f32[512,128]{1,0:T(8,128)S(1)}, f32[1024,128]{1,0:T(8,128)S(1)}, f32[168,128]{1,0:T(8,128)S(1)}, f32[168,128]{1,0:T(8,128)S(1)}) custom-call(bf16[16,64,128]{2,1,0:T(8,128)(2,1)S(1)} %get-tuple-element.52.ft, bf16[16,64,128]{2,1,0:T(8,128)(2,1)S(1)} %get-tuple-element.53.gt.refs_2_, ...), custom_call_target="tpu_custom_call" | custom-call | tf_op jit(solution)/shard_map/own/pallas_call | solution.py:627
  31.1 0.2 collective-permute-start.19
  31.3 1.1 %collective-permute-done.19 = f32[168,128]{1,0:T(8,128)S(1)} collective-permute-done((f32[168,128]{1,0:T(8,128)S(1)}, f32[168,128]{1,0:T(8,128)S(1)}, u32[]{:S(2)}, u32[]{:S(2)}) %collective-permute-start.19) | collective-permute-done | bytes 86048 | tf_op jit(solution)/shard_map/ppermute | solution.py:706
  32.4 2.3 %collective-permute-start.20 = (f32[168,128]{1,0:T(8,128)S(1)}, f32[168,128]{1,0:T(8,128)S(1)}, u32[]{:S(2)}, u32[]{:S(2)}) collective-permute-start(f32[168,128]{1,0:T(8,128)S(1)} %add.15), channel_id=1, source_target_pairs={{0,8},{4,12},{8,0},{12,4},{16,24},{20,28},{24,16},{28,20},{1,9},{5... | collective-permute-start | bytes 258056 | tf_op jit(solution)/shard_map/ppermute | solution.py:706
  34.7 1.9 %halo.1.refs_1_ = f32[512,128]{1,0:T(8,128)S(1)} custom-call(f32[512,128]{1,0:T(8,128)S(1)} %get-tuple-element.72.conv_halo, bf16[9,64,128]{2,1,0:T(8,128)(2,1)S(1)} %get-tuple-element.60.low, bf16[9,64,128]{2,1,0:T(8,128)(2,1)S(1)} %get-tuple-element.61.up, bf16[64,256]{1,0:T(8,128)(2,1)S(1)} %collective-permute-done.17.got_l, ...), custom_call_target="tpu_custom_call" | custom-call | flops 150000000 | bytes 1048576 | tf_op jit(solution)/shard_map/halo/pallas_call | solution.py:673
  36.6 1.1 %collective-permute-done.20 = f32[168,128]{1,0:T(8,128)S(1)} collective-permute-done((f32[168,128]{1,0:T(8,128)S(1)}, f32[168,128]{1,0:T(8,128)S(1)}, u32[]{:S(2)}, u32[]{:S(2)}) %collective-permute-start.20) | collective-permute-done | bytes 86048 | tf_op jit(solution)/shard_map/ppermute | solution.py:706
  37.7 0.9 %collective-permute-start.21 = (f32[168,128]{1,0:T(8,128)S(1)}, f32[168,128]{1,0:T(8,128)S(1)}, u32[]{:S(2)}, u32[]{:S(2)}) collective-permute-start(f32[168,128]{1,0:T(8,128)S(1)} %add.16), channel_id=1, source_target_pairs={{0,16},{4,20},{8,24},{12,28},{16,0},{20,4},{24,8},{28,12},{1,17},{... | collective-permute-start | bytes 258056 | tf_op jit(solution)/shard_map/ppermute | solution.py:706
  38.7 2.4 %adjoint.2.refs_5_ = bf16[64,16,128]{2,1,0:T(8,128)(2,1)} custom-call(f32[1024,128]{1,0:T(8,128)S(1)} %get-tuple-element.74.refs_0_, f32[512,128]{1,0:T(8,128)S(1)} %halo.1.refs_1_, bf16[16,64,128]{2,1,0:T(8,128)(2,1)S(1)} %get-tuple-element.53.gt.refs_2_, f32[7,64,128]{2,1,0:T(8,128)S(1)} %get-tuple-element.64.plain.refs_3_, ...), custom_call_target="tpu_custom_call" | custom-call | flops 200000000 | bytes 2097152 | tf_op jit(solution)/shard_map/adjoint/pallas_call | solution.py:686
  41.1 1.2 %collective-permute-done.21 = f32[168,128]{1,0:T(8,128)S(1)} collective-permute-done((f32[168,128]{1,0:T(8,128)S(1)}, f32[168,128]{1,0:T(8,128)S(1)}, u32[]{:S(2)}, u32[]{:S(2)}) %collective-permute-start.21) | collective-permute-done | bytes 86048 | tf_op jit(solution)/shard_map/ppermute | solution.py:706
  42.3 7.5 %collective-permute-start.22 = (f32[168,128]{1,0:T(8,128)S(1)}, f32[168,128]{1,0:T(8,128)S(1)}, u32[]{:S(2)}, u32[]{:S(2)}) collective-permute-start(f32[168,128]{1,0:T(8,128)S(1)} %add.17), channel_id=1, source_target_pairs={{0,1},{1,0},{2,3},{3,2},{4,5},{5,4},{6,7},{7,6},{8,9},{9,8},{10,11... | collective-permute-start | bytes 258056 | tf_op jit(solution)/shard_map/ppermute | solution.py:706
  49.8 2.4 %adjoint.3 = bf16[64,16,128]{2,1,0:T(8,128)(2,1)} custom-call(f32[1024,128]{1,0:T(8,128)S(1)} %get-tuple-element.74.refs_0_, f32[512,128]{1,0:T(8,128)S(1)} %halo.1.refs_1_, bf16[16,64,128]{2,1,0:T(8,128)(2,1)S(1)} %get-tuple-element.53.gt.refs_2_, f32[7,64,128]{2,1,0:T(8,128)S(1)} %get-tuple-element.64.plain.refs_3_, ...), custom_call_target="tpu_custom_call", output_to_operand_aliasing={{}: (5, {})} | custom-call | flops 200000000 | bytes 2097152 | tf_op jit(solution)/shard_map/adjoint/pallas_call | solution.py:686
  52.2 0.0 collective-permute-done.22
  52.2 4.9 %collective-permute-start.23 = (f32[168,128]{1,0:T(8,128)S(1)}, f32[168,128]{1,0:T(8,128)S(1)}, u32[]{:S(2)}, u32[]{:S(2)}) collective-permute-start(f32[168,128]{1,0:T(8,128)S(1)} %add.18), channel_id=1, source_target_pairs={{0,2},{1,3},{2,0},{3,1},{4,6},{5,7},{6,4},{7,5},{8,10},{9,11},{10,... | collective-permute-start | bytes 258056 | tf_op jit(solution)/shard_map/ppermute | solution.py:706
  57.1 2.5 %collective-permute-done.23 = f32[168,128]{1,0:T(8,128)S(1)} collective-permute-done((f32[168,128]{1,0:T(8,128)S(1)}, f32[168,128]{1,0:T(8,128)S(1)}, u32[]{:S(2)}, u32[]{:S(2)}) %collective-permute-start.23) | collective-permute-done | bytes 86048 | tf_op jit(solution)/shard_map/ppermute | solution.py:706
  59.6 0.1 collective-permute-start.24
  59.7 1.3 %collective-permute-done.24.other = f32[168,128]{1,0:T(8,128)S(1)} collective-permute-done((f32[168,128]{1,0:T(8,128)S(1)}, f32[168,128]{1,0:T(8,128)S(1)}, u32[]{:S(2)}, u32[]{:S(2)}) %collective-permute-start.24) | collective-permute-done | bytes 86048 | tf_op jit(solution)/shard_map/ppermute | solution.py:706
  61.0 0.7 %finish.1 = (f32[7,7,64]{2,1,0:T(8,128)}, f32[64]{0:T(128)}, f32[64]{0:T(128)}, f32[64,256]{1,0:T(8,128)}, f32[256]{0:T(256)}, /*index=5*/f32[64,256]{1,0:T(8,128)}, f32[64]{0:T(128)}) custom-call(f32[168,128]{1,0:T(8,128)S(1)} %add.19.total, f32[168,128]{1,0:T(8,128)S(1)} %collective-permute-done.24.other), custom_call_target="tpu_custom_call" | custom-call | tf_op jit(solution)/shard_map/finish/pallas_call | solution.py:722
  (23 shorter events, 0.1 us)
Async XLA Ops:
  0.6 4.5 %copy-start.3 = (s32[1024]{0:T(1024)S(1)}, s32[1024]{0:T(1024)}, u32[]{:S(2)}) copy-start(s32[1024]{0:T(1024)} %seam.1) | copy-start | bytes 12292
  2.0 8.3 %collective-permute-start.16 = (bf16[9,64,128]{2,1,0:T(8,128)(2,1)S(1)}, bf16[9,64,128]{2,1,0:T(8,128)(2,1)S(1)}, u32[]{:S(2)}, u32[]{:S(2)}) collective-permute-start(bf16[9,64,128]{2,1,0:T(8,128)(2,1)S(1)} %get-tuple-element.54), channel_id=1, source_target_pairs={{0,1},{1,0},{4,5},{5,4},{8,9},{9,8},{12,13},{13,12},{16,17},{17,16... | collective-permute-start | bytes 442376 | tf_op jit(solution)/shard_map/ppermute | solution.py:573
  7.7 2.6 %collective-permute-start.15 = (bf16[9,64,128]{2,1,0:T(8,128)(2,1)S(1)}, bf16[9,64,128]{2,1,0:T(8,128)(2,1)}, u32[]{:S(2)}, u32[]{:S(2)}) collective-permute-start(bf16[9,64,128]{2,1,0:T(8,128)(2,1)S(1)} %param.7), channel_id=1, source_target_pairs={{3,27},{7,23},{11,19},{15,15},{19,11},{23,7},{27,3},{31,31}} | collective-permute-start | bytes 442376 | tf_op jit(solution)/shard_map/cond/branch_7_fun/ppermute | solution.py:582
  9.0 1.3 %collective-permute-start.14 = (bf16[9,64,128]{2,1,0:T(8,128)(2,1)S(1)}, bf16[9,64,128]{2,1,0:T(8,128)(2,1)}, u32[]{:S(2)}, u32[]{:S(2)}) collective-permute-start(bf16[9,64,128]{2,1,0:T(8,128)(2,1)S(1)} %param.7), channel_id=1, source_target_pairs={{1,2},{2,1},{5,6},{6,5},{9,10},{10,9},{13,14},{14,13},{17,18},{18,... | collective-permute-start | bytes 442376 | tf_op jit(solution)/shard_map/cond/branch_7_fun/ppermute | solution.py:583
  10.3 4.3 %copy-start = (bf16[256,64]{0,1:T(8,128)(2,1)S(1)}, bf16[256,64]{0,1:T(8,128)(2,1)}, u32[]{:S(2)}) copy-start(bf16[256,64]{0,1:T(8,128)(2,1)} %param.26) | copy-start | bytes 98308
  10.3 4.3 %copy-start.1 = (bf16[64,256]{1,0:T(8,128)(2,1)S(1)}, bf16[64,256]{1,0:T(8,128)(2,1)}, u32[]{:S(2)}) copy-start(bf16[64,256]{1,0:T(8,128)(2,1)} %down.3) | copy-start | bytes 98308
  10.3 4.3 %copy-start.4 = (bf16[64,7,7]{0,2,1:T(8,128)(2,1)S(1)}, bf16[64,7,7]{0,2,1:T(8,128)(2,1)}, u32[]{:S(2)}) copy-start(bf16[64,7,7]{0,2,1:T(8,128)(2,1)} %param.23) | copy-start | bytes 18820
  10.3 4.3 %copy-start.8 = (bf16[256]{0:T(256)(128)(2,1)S(1)}, bf16[256]{0:T(256)(128)(2,1)}, u32[]{:S(2)}) copy-start(bf16[256]{0:T(256)(128)(2,1)} %up_b.1) | copy-start | bytes 1540
  11.9 4.3 %collective-permute-start.17 = (bf16[64,256]{1,0:T(8,128)(2,1)S(1)}, bf16[64,256]{1,0:T(8,128)(2,1)S(1)}, u32[]{:S(2)}, u32[]{:S(2)}) collective-permute-start(bf16[64,256]{1,0:T(8,128)(2,1)S(1)} %get-tuple-element.62), channel_id=1, source_target_pairs={{0,4},{4,8},{8,12},{12,16},{16,20},{20,24},{24,28},{28,0},{1,5},{5... | collective-permute-start | bytes 98312 | tf_op jit(solution)/shard_map/ppermute | solution.py:598
  12.0 4.2 %collective-permute-start.18 = (bf16[64,256]{1,0:T(8,128)(2,1)S(1)}, bf16[64,256]{1,0:T(8,128)(2,1)S(1)}, u32[]{:S(2)}, u32[]{:S(2)}) collective-permute-start(bf16[64,256]{1,0:T(8,128)(2,1)S(1)} %get-tuple-element.63), channel_id=1, source_target_pairs={{0,28},{4,0},{8,4},{12,8},{16,12},{20,16},{24,20},{28,24},{1,29},{... | collective-permute-start | bytes 98312 | tf_op jit(solution)/shard_map/ppermute | solution.py:599
  14.6 0.7 %copy-start.5 = (bf16[64]{0:T(256)(128)(2,1)S(1)}, bf16[64]{0:T(256)(128)(2,1)}, u32[]{:S(2)}) copy-start(bf16[64]{0:T(256)(128)(2,1)} %gain.1) | copy-start | bytes 388
  14.6 0.7 %copy-start.6 = (bf16[64]{0:T(256)(128)(2,1)S(1)}, bf16[64]{0:T(256)(128)(2,1)}, u32[]{:S(2)}) copy-start(bf16[64]{0:T(256)(128)(2,1)} %bias.1) | copy-start | bytes 388
  14.6 0.7 %copy-start.7 = (bf16[64]{0:T(256)(128)(2,1)S(1)}, bf16[64]{0:T(256)(128)(2,1)}, u32[]{:S(2)}) copy-start(bf16[64]{0:T(256)(128)(2,1)} %scale.1) | copy-start | bytes 388
  16.0 0.7 %copy-start.2 = (s32[16,128]{1,0:T(8,128)S(1)}, s32[16,128]{1,0:T(8,128)}, u32[]{:S(2)}) copy-start(s32[16,128]{1,0:T(8,128)} %mask.1) | copy-start | bytes 24580
  31.1 1.3 %collective-permute-start.19 = (f32[168,128]{1,0:T(8,128)S(1)}, f32[168,128]{1,0:T(8,128)S(1)}, u32[]{:S(2)}, u32[]{:S(2)}) collective-permute-start(f32[168,128]{1,0:T(8,128)S(1)} %get-tuple-element.71), channel_id=1, source_target_pairs={{0,4},{4,0},{8,12},{12,8},{16,20},{20,16},{24,28},{28,24},{1,5},{5... | collective-permute-start | bytes 258056 | tf_op jit(solution)/shard_map/ppermute | solution.py:706
  32.4 5.3 %collective-permute-start.20 = (f32[168,128]{1,0:T(8,128)S(1)}, f32[168,128]{1,0:T(8,128)S(1)}, u32[]{:S(2)}, u32[]{:S(2)}) collective-permute-start(f32[168,128]{1,0:T(8,128)S(1)} %add.15), channel_id=1, source_target_pairs={{0,8},{4,12},{8,0},{12,4},{16,24},{20,28},{24,16},{28,20},{1,9},{5... | collective-permute-start | bytes 258056 | tf_op jit(solution)/shard_map/ppermute | solution.py:706
  37.7 4.6 %collective-permute-start.21 = (f32[168,128]{1,0:T(8,128)S(1)}, f32[168,128]{1,0:T(8,128)S(1)}, u32[]{:S(2)}, u32[]{:S(2)}) collective-permute-start(f32[168,128]{1,0:T(8,128)S(1)} %add.16), channel_id=1, source_target_pairs={{0,16},{4,20},{8,24},{12,28},{16,0},{20,4},{24,8},{28,12},{1,17},{... | collective-permute-start | bytes 258056 | tf_op jit(solution)/shard_map/ppermute | solution.py:706
  42.3 9.9 %collective-permute-start.22 = (f32[168,128]{1,0:T(8,128)S(1)}, f32[168,128]{1,0:T(8,128)S(1)}, u32[]{:S(2)}, u32[]{:S(2)}) collective-permute-start(f32[168,128]{1,0:T(8,128)S(1)} %add.17), channel_id=1, source_target_pairs={{0,1},{1,0},{2,3},{3,2},{4,5},{5,4},{6,7},{7,6},{8,9},{9,8},{10,11... | collective-permute-start | bytes 258056 | tf_op jit(solution)/shard_map/ppermute | solution.py:706
  52.2 7.4 %collective-permute-start.23 = (f32[168,128]{1,0:T(8,128)S(1)}, f32[168,128]{1,0:T(8,128)S(1)}, u32[]{:S(2)}, u32[]{:S(2)}) collective-permute-start(f32[168,128]{1,0:T(8,128)S(1)} %add.18), channel_id=1, source_target_pairs={{0,2},{1,3},{2,0},{3,1},{4,6},{5,7},{6,4},{7,5},{8,10},{9,11},{10,... | collective-permute-start | bytes 258056 | tf_op jit(solution)/shard_map/ppermute | solution.py:706
  59.6 1.3 %collective-permute-start.24 = (f32[168,128]{1,0:T(8,128)S(1)}, f32[168,128]{1,0:T(8,128)S(1)}, u32[]{:S(2)}, u32[]{:S(2)}) collective-permute-start(f32[168,128]{1,0:T(8,128)S(1)} %add.19.total), channel_id=1, source_target_pairs={{0,4},{4,0},{8,12},{12,8},{16,20},{20,16},{24,28},{28,24},{1,5},{5... | collective-permute-start | bytes 258056 | tf_op jit(solution)/shard_map/ppermute | solution.py:706

commit v5 on v4

--- a/solution.py
+++ b/solution.py
@@ -24,26 +24,39 @@
     return lax.broadcasted_iota(jnp.int32, shape, 1)
 
 
-def pack_kernel(fields_far, cot_far, mask_far, ft, gt, first, second, plane, fields, cot, mask, arrived):
-    chans, rows, _ = fields.shape
+def pack_kernel(
+    seam, fields_far, cot_far, mask_far, ft, gt, first, second, partner, turn, *scratch
+):
+    plane, fields, cot, mask, head, index, arrived = scratch
+    chans, rows, cols = fields.shape
     groups = chans // 8
-    pairs = ((fields_far, fields), (cot_far, cot), (mask_far, mask))
+    pairs = (
+        (fields_far, fields),
+        (cot_far, cot),
+        (mask_far, mask),
+        (seam.at[pl.ds(0, 1), :], head),
+        (seam.at[pl.ds(lax.axis_index("lon"), 1), :], partner),
+    )
     copies = [pltpu.make_async_copy(src, dst, arrived.at[k]) for k, (src, dst) in enumerate(pairs)]
-    for copy in copies:
-        copy.start()
-    for turn, dst in ((0, ft), (1, gt)):
-        copies[turn].wait()
-        if turn == 1:
+    for k in (3, 0, 1, 2, 4):
+        copies[k].start()
+    copies[3].wait()
+    index[0] = head[0, 0] // cols
+    answer = pltpu.make_async_copy(index, turn, arrived.at[5])
+    answer.start()
+    for k, dst in ((0, ft), (1, gt)):
+        copies[k].wait()
+        if k == 1:
             copies[2].wait()
             sea = mask[...].astype(F32)
         for c in range(chans):
-            if turn == 0:
+            if k == 0:
                 cell = fields[c].astype(F32)
             else:
                 cell = cot[c].astype(F32) * sea
-            plane[turn, c * rows : (c + 1) * rows, :] = cell
+            plane[k, c * rows : (c + 1) * rows, :] = cell
         for r in range(rows):
-            parts = [plane[turn, pl.ds(g * 8 * rows + r, 8, stride=rows), :] for g in range(groups)]
+            parts = [plane[k, pl.ds(g * 8 * rows + r, 8, stride=rows), :] for g in range(groups)]
             dst[r] = jnp.concatenate(parts, axis=0).astype(BF)
 
     def edge(dst, top):
@@ -64,6 +77,9 @@
         edge(first, False)
         edge(second, True)
 
+    copies[4].wait()
+    answer.wait()
+
 
 def field_lane(r):
     return LANES * (r // 14) + 6 * (r % 14)
@@ -73,10 +89,9 @@
     return LANES * (g // 11) + 84 + 3 * (g % 11)
 
 
-def edge_kernel(fold_first, seam, partner, got_a, got_b, got_c, ft, gt, low, up, sent_l, sent_r):
+def edge_kernel(fold_first, partner, got_a, got_b, got_c, ft, gt, low, up, sent_l, sent_r):
     rows, chans, cols = ft.shape
-    n_lon = partner.shape[0]
-    x = lax.axis_index("lon")
+    total = lax.axis_size("lon") * cols
     z = lax.axis_index("lat")
     odd = z % 2
     top = z == lax.axis_size("lat") - 1
@@ -93,11 +108,12 @@
     def _():
         got_1 = got_a if fold_first else got_b
         src = lax.broadcasted_iota(jnp.int32, (cols, cols), 0)
-        want = jnp.broadcast_to(partner[pl.ds(x, 1), :], (cols, cols))
-        near = (seam[0] // cols - x + n_lon) % n_lon
-        far = (near + n_lon - 1) % n_lon
-        pick_1 = (src + near * cols == want).astype(F32).astype(BF)
-        pick_2 = (src + far * cols == want).astype(F32).astype(BF)
+        want = jnp.broadcast_to(partner[...], (cols, cols))
+        leading = jnp.broadcast_to(partner[:, 0:1], (cols, cols))
+        near = leading - lax.rem(leading, jnp.full_like(leading, cols))
+        far = jnp.where(near == 0, total, near) - cols
+        pick_1 = (src + near == want).astype(F32).astype(BF)
+        pick_2 = (src + far == want).astype(F32).astype(BF)
         for k in range(9):
             m = 5 - k if k < 6 else 14 - k
             mixed = jnp.dot(got_1[m], pick_1, preferred_element_type=F32)
@@ -144,8 +160,11 @@
         dst[...] = jnp.concatenate([acc[side, 0], acc[side, 1]], axis=1).astype(BF)
 
 
-def weight_kernel(taps, gain, bias, scale, up_b, up_t, down, plain, turned, vecs, up_aug, down_t, line):
+def weight_kernel(
+    taps, gain, bias, scale, up_b, up_t, down, plain, turned, vecs, up_aug, down_t, band, band_up, line
+):
     chans, hidden_n = up_t.shape
+    top = lax.axis_index("lat") == lax.axis_size("lat") - 1
     line[...] = jnp.zeros_like(line)
     for a in range(7):
         block = taps[a].astype(F32)
@@ -155,6 +174,21 @@
     for q in range(7):
         plain[q] = line[0, q].T[:chans]
         turned[q] = line[1, q].T[:chans]
+
+    def spread(g, _):
+        at = pl.ds(pl.multiple_of(g * 8, 8), 8)
+        for q in range(7):
+            one, two = plain[q, at, :], turned[q, at, :]
+            above = jnp.where(top, two, one)
+            band[g, q * 80 : q * 80 + 80, :] = jnp.concatenate(
+                [pltpu.roll(one, 8 * i, 1, stride=1, stride_axis=0) for i in range(10)], axis=0
+            ).astype(BF)
+            band_up[g, q * 32 : q * 32 + 32, :] = jnp.concatenate(
+                [pltpu.roll(above, 8 * i, 1, stride=1, stride_axis=0) for i in range(6, 10)], axis=0
+            ).astype(BF)
+        return 0
+
+    lax.fori_loop(0, chans // 8, spread, 0)
     wide = LANES - chans
     columns = jnp.concatenate(
         [v[...].astype(F32).reshape(1, chans) for v in (gain, bias, scale)] + [jnp.zeros((5, chans), F32)],
@@ -224,8 +258,8 @@
     got_l,
     got_r,
     mask,
-    plain,
-    turned,
+    band,
+    band_up,
     vecs,
     up_aug,
     up_t,
@@ -241,8 +275,6 @@
     rhs,
     conv,
     plane,
-    band,
-    band_up,
     prod_1,
     prod_2,
     prod_3,
@@ -255,7 +287,6 @@
     groups = chans // 8
     mid = rows + 6
     odd_core = lax.axis_index("lon") % 2
-    top = lax.axis_index("lat") == lax.axis_size("lat") - 1
     lane = lane_iota((8, LANES))
     wide = slice(0, LANES), slice(LANES, 2 * LANES)
     at_row = lambda r, g: rows_of(r, g, chans)
@@ -280,18 +311,9 @@
                 rim[at_row(r, g), :] = beyond
                 pair.append(jnp.concatenate([value, beyond], axis=1))
             rhs[8 * r0 : 8 * r0 + 16, :] = jnp.concatenate(pair, axis=0).astype(BF)
-        for q in range(7):
-            one, two = plain[q, at, :], turned[q, at, :]
-            above = jnp.where(top, two, one)
-            band[q * 80 : q * 80 + 80, :] = jnp.concatenate(
-                [pltpu.roll(one, 8 * i, 1, stride=1, stride_axis=0) for i in range(10)], axis=0
-            ).astype(BF)
-            band_up[q * 32 : q * 32 + 32, :] = jnp.concatenate(
-                [pltpu.roll(above, 8 * i, 1, stride=1, stride_axis=0) for i in range(6, 10)], axis=0
-            ).astype(BF)
-        prod_1[...] = jnp.dot(band[...], rhs[0:128, :], preferred_element_type=F32)
-        prod_2[...] = jnp.dot(band[...], rhs[80:208, :], preferred_element_type=F32)
-        prod_3[0:224, :] = jnp.dot(band_up[0:224, :], rhs[96:224, :], preferred_element_type=F32)
+        prod_1[...] = jnp.dot(band[g], rhs[0:128, :], preferred_element_type=F32)
+        prod_2[...] = jnp.dot(band[g], rhs[80:208, :], preferred_element_type=F32)
+        prod_3[...] = jnp.dot(band_up[g], rhs[96:224, :], preferred_element_type=F32)
         sides = [jnp.zeros((8, LANES), F32)] * 2
         for o in range(mid):
             if o < 10:
@@ -354,7 +376,7 @@
             sums[k] += value[:, :LANES] + value[:, LANES:]
         return 0
 
-    lax.fori_loop(0, rows // 2, own_block, 0)
+    lax.fori_loop(0, rows // 2, own_block, 0, unroll=2)
 
     def taps_group(g, _):
         at = pl.ds(pl.multiple_of(g * 8, 8), 8)
@@ -426,7 +448,7 @@
             dcv_halo[u, :] = dx[:, wide[k]]
         return 0
 
-    lax.fori_loop(0, 4, halo_block, 0)
+    lax.fori_loop(0, 4, halo_block, 0, unroll=2)
 
 
 def adjoint_kernel(part, *refs):
@@ -523,10 +545,6 @@
     return [pl.BlockSpec(memory_space=pltpu.VMEM)] * n
 
 
-def smem():
-    return pl.BlockSpec(memory_space=pltpu.SMEM)
-
-
 def shards(
     fields,
     cotangent,
@@ -544,21 +562,31 @@
     hidden_n = up_weight.shape[0]
     n_lon, n_lat = lax.axis_size("lon"), lax.axis_size("lat")
     sds = jax.ShapeDtypeStruct
-    ft, gt, first, second = pl.pallas_call(
+    hbm = pl.BlockSpec(memory_space=pltpu.HBM)
+    ft, gt, first, second, partner, turn = pl.pallas_call(
         pack_kernel,
-        out_shape=[sds((rows, chans, cols), BF)] * 2 + [sds((9, chans, cols), BF)] * 2,
-        in_specs=[pl.BlockSpec(memory_space=pltpu.HBM)] * 3,
-        out_specs=vmem(4),
+        out_shape=[sds((rows, chans, cols), BF)] * 2
+        + [sds((9, chans, cols), BF)] * 2
+        + [sds((1, cols), jnp.int32), sds((1,), jnp.int32)],
+        in_specs=[hbm] * 4,
+        out_specs=vmem(5) + [hbm],
         scratch_shapes=[
             pltpu.VMEM((2, chans * rows, cols), F32),
             pltpu.VMEM((chans, rows, cols), BF),
             pltpu.VMEM((chans, rows, cols), BF),
             pltpu.VMEM((rows, cols), jnp.int32),
-            pltpu.SemaphoreType.DMA((3,)),
+            pltpu.SMEM((1, cols), jnp.int32),
+            pltpu.SMEM((1,), jnp.int32),
+            pltpu.SemaphoreType.DMA((6,)),
         ],
         compiler_params=pltpu.CompilerParams(vmem_limit_bytes=8 * 2**20),
         name="pack",
-    )(*[pltpu.with_memory_space_constraint(v, pltpu.HBM) for v in (fields[0], cotangent[0], ocean_mask)])
+    )(
+        *[
+            pltpu.with_memory_space_constraint(v, pltpu.HBM)
+            for v in (seam_partner.reshape(n_lon, cols), fields[0], cotangent[0], ocean_mask)
+        ]
+    )
 
     at = lambda lon, lat: (lon % n_lon) * n_lat + lat
     rounds = [[], []]
@@ -571,7 +599,7 @@
     plain_round = 1 - fold_round
     sends = (first, second)
     met = lax.ppermute(sends[plain_round], axes, rounds[plain_round])
-    seam, top = lax.optimization_barrier((seam_partner, sends[fold_round]))
+    top = sends[fold_round]
 
     def exchange(k):
         def run(top):
@@ -579,26 +607,24 @@
                 [(at(lon, n_lat - 1), at(k - j - lon, n_lat - 1)) for lon in range(n_lon)] for j in (0, 1)
             ]
             plan = rounds[fold_round] + mirror[0]
-            last = lax.ppermute(top, axes, mirror[1])
-            return lax.ppermute(top, axes, plan), last
+            return lax.ppermute(top, axes, mirror[1]), lax.ppermute(top, axes, plan)
 
         return run
 
-    turn = lax.div(seam[0], jnp.int32(cols))
-    folded, got_c = lax.switch(turn, [exchange(k) for k in range(n_lon)], top)
+    got_c, folded = lax.switch(turn[0], [exchange(k) for k in range(n_lon)], top)
     got_a, got_b = (folded, met) if fold_round == 0 else (met, folded)
     low, up, sent_l, sent_r = pl.pallas_call(
         functools.partial(edge_kernel, fold_round == 0),
         out_shape=[sds((9, chans, cols), BF)] * 2 + [sds((chans, 2 * cols), BF)] * 2,
-        in_specs=[smem()] + vmem(6),
+        in_specs=vmem(6),
         out_specs=vmem(4),
         compiler_params=pltpu.CompilerParams(vmem_limit_bytes=8 * 2**20),
         name="edges",
-    )(seam_partner, seam_partner.reshape(n_lon, cols), got_a, got_b, got_c, ft, gt)
+    )(partner, got_a, got_b, got_c, ft, gt)
     got_l = lax.ppermute(sent_r, "lon", [(i, (i + 1) % n_lon) for i in range(n_lon)])
     got_r = lax.ppermute(sent_l, "lon", [(i, (i - 1) % n_lon) for i in range(n_lon)])
 
-    plain, turned, vecs, up_aug, down_t = pl.pallas_call(
+    plain, turned, vecs, up_aug, down_t, band, band_up = pl.pallas_call(
         weight_kernel,
         out_shape=[
             sds((7, chans, LANES), F32),
@@ -606,9 +632,11 @@
             sds((3, chans, LANES), F32),
             sds((hidden_n, chans + 16), BF),
             sds((hidden_n, chans), BF),
+            sds((chans // 8, 7 * 80, LANES), BF),
+            sds((chans // 8, 7 * 32, LANES), BF),
         ],
         in_specs=vmem(7),
-        out_specs=vmem(5),
+        out_specs=vmem(7),
         scratch_shapes=[pltpu.VMEM((2, 7, LANES, LANES), F32)],
         compiler_params=pltpu.CompilerParams(vmem_limit_bytes=8 * 2**20),
         name="weights",
@@ -641,8 +669,6 @@
             pltpu.VMEM((band_rows, 2 * cols), BF),
             pltpu.VMEM((rows * chans, cols), F32),
             pltpu.VMEM((chans * rows, cols), F32),
-            pltpu.VMEM((7 * 80, LANES), BF),
-            pltpu.VMEM((7 * 32, LANES), BF),
             pltpu.VMEM((7 * 80, 2 * cols), F32),
             pltpu.VMEM((7 * 80, 2 * cols), F32),
             pltpu.VMEM((7 * 32, 2 * cols), F32),
@@ -661,8 +687,8 @@
         got_l,
         got_r,
         ocean_mask,
-        plain,
-        turned,
+        band,
+        band_up,
         vecs,
         up_aug,
         up_t,

time: 62.2 us -> 57.3 us (0.921)
  starting transfers between devices: 24.3 us -> 22.4 us
  local copies, waits for them, and re-layouts: 1.73 us -> 0.03 us
  between operations: 2.73 us -> 1.47 us
  waiting for transfers between devices: 7.39 us -> 8.03 us
    ppermute x6, starting transfers between devices: 15.8 us -> 14 us  [shards(): lax.ppermute(y, axis, [(i, i ^ b) for i in range(lax.axis_size(axis))])]
    unnamed x18 -> x16, local copies, waits for them, and re-layouts: 1.22 us -> 0.03 us
    pallas_call x1, Pallas kernels: 14.4 us -> 13.5 us  [shards(): pl.pallas_call(own_kernel, out_shape=[sds((chans, rows, cols), BF), sds((...]
    pallas_call x1, Pallas kernels: 0.74 us -> 1.57 us  [shards(): pl.pallas_call(weight_kernel, out_shape=[sds((7, chans, LANES), F32), sds...]
  transfers between devices with their start and end apart: 11 -> 11, of which waited for: 6 -> 6; matrix products, arithmetic and copies ran while one was open for 1% -> 0% of each run, Pallas kernels for 12% -> 14%
where the time goes in v5:
time: 57.3 us; the launch traced here: 57.1 us
  Pallas kernels  25 us (44%)
  starting transfers between devices  22.4 us (39%)
  waiting for transfers between devices  8.03 us (14%)
  between operations  1.47 us (3%)
    ppermute x6, starting transfers between devices, shards(): lax.ppermute(y, axis, [(i, i ^ b) for i in range(lax.axis_size(axis))])  14 us
    pallas_call x1, Pallas kernels, shards(): pl.pallas_call(own_kernel, out_shape=[sds((chans, rows, cols), BF), sds((...  13.5 us
    ppermute x6, waiting for transfers between devices, shards(): lax.ppermute(y, axis, [(i, i ^ b) for i in range(lax.axis_size(axis))])  7.49 us
    pallas_call x2, Pallas kernels, adjoint(): pl.pallas_call(functools.partial(adjoint_kernel, part), grid=(1,), out_sh...  4.83 us
    ppermute x1, starting transfers between devices, shards(): met = lax.ppermute(sends[plain_round], axes, rounds[plain_round])  3.13 us
    ppermute x2, starting transfers between devices, run(): return (lax.ppermute(top, axes, mirror[1]), lax.ppermute(top, axes, plan))  2.64 us
    ppermute x1, starting transfers between devices, shards(): lax.ppermute(sent_l, 'lon', [(i, (i - 1) % n_lon) for i in range(n_lon)])  2.63 us
    pallas_call x1, Pallas kernels, shards(): pl.pallas_call(weight_kernel, out_shape=[sds((7, chans, LANES), F32), sds...  1.57 us
  transfers between devices with their start and end apart: 11, of which 6 were waited for; matrix products, arithmetic and copies ran while one was open for 0% of the time, Pallas kernels for 14%

profile of v5, /device:TPU:0, one launch (start us, length us, event | category | flops | bytes accessed | tf_op | source)
XLA Modules:
  0.0 57.1 jit_solution(10205436148130820066)
XLA Ops:
  0.6 0.0 copy-start.2
  0.7 1.5 %pack.1 = (bf16[16,64,128]{2,1,0:T(8,128)(2,1)S(1)}, bf16[16,64,128]{2,1,0:T(8,128)(2,1)S(1)}, bf16[9,64,128]{2,1,0:T(8,128)(2,1)S(1)}, bf16[9,64,128]{2,1,0:T(8...) custom-call(s32[8,128]{1,0:T(8,128)} %bitcast.17, bf16[64,16,128]{2,1,0:T(8,128)(2,1)} %bitcast.15, ...), custom_call_target="tpu_custom_call" | custom-call | tf_op jit(solution)/shard_map/pack/pallas_call | solution.py:566
  2.2 3.1 %collective-permute-start.16 = (bf16[9,64,128]{2,1,0:T(8,128)(2,1)S(1)}, bf16[9,64,128]{2,1,0:T(8,128)(2,1)S(1)}, u32[]{:S(2)}, u32[]{:S(2)}) collective-permute-start(bf16[9,64,128]{2,1,0:T(8,128)(2,1)S(1)} %get-tuple-element.57), channel_id=1, source_target_pairs={{0,1},{1,0},{4,5},{5,4},{8,9},{9,8},{12,13},{13,12},{16,17},{17,16... | collective-permute-start | bytes 442376 | tf_op jit(solution)/shard_map/ppermute | solution.py:601
  6.0 2.7 %conditional.1 = (bf16[9,64,128]{2,1,0:T(8,128)(2,1)}, bf16[9,64,128]{2,1,0:T(8,128)(2,1)}) conditional(s32[]{:T(128)} %bitcast.3, bf16[9,64,128]{2,1,0:T(8,128)(2,1)S(1)} %get-tuple-element.59, bf16[9,64,128]{2,1,0:T(8,128)(2,1)S(1)} %get-tuple-element.59, bf16[9,64,128]{2,1,0:T(8,128)(2,1)S(1)} %get-tuple-element.59, ...), branch_computations={%region_0.0_spmd, %region_1.0_spmd, %region_2.0_spmd, %region_3.0_... | conditional | bytes 1179744 | solution.py:614
  6.0 1.3 %collective-permute-start.5 = (bf16[9,64,128]{2,1,0:T(8,128)(2,1)S(1)}, bf16[9,64,128]{2,1,0:T(8,128)(2,1)}, u32[]{:S(2)}, u32[]{:S(2)}) collective-permute-start(bf16[9,64,128]{2,1,0:T(8,128)(2,1)S(1)} %param.2), channel_id=1, source_target_pairs={{1,2},{2,1},{5,6},{6,5},{9,10},{10,9},{13,14},{14,13},{17,18},{18,... | collective-permute-start | bytes 442376 | tf_op jit(solution)/shard_map/cond/branch_2_fun/ppermute | solution.py:610
  7.3 1.3 %collective-permute-start.4 = (bf16[9,64,128]{2,1,0:T(8,128)(2,1)S(1)}, bf16[9,64,128]{2,1,0:T(8,128)(2,1)}, u32[]{:S(2)}, u32[]{:S(2)}) collective-permute-start(bf16[9,64,128]{2,1,0:T(8,128)(2,1)S(1)} %param.2), channel_id=1, source_target_pairs={{3,7},{7,3},{11,31},{15,27},{19,23},{23,19},{27,15},{31,11}} | collective-permute-start | bytes 442376 | tf_op jit(solution)/shard_map/cond/branch_2_fun/ppermute | solution.py:610
  8.6 0.0 collective-permute-done.5
  8.6 0.0 collective-permute-done.4
  8.6 0.5 collective-permute-done.16.got_a
  9.2 1.5 %edges.1 = (bf16[9,64,128]{2,1,0:T(8,128)(2,1)S(1)}, bf16[9,64,128]{2,1,0:T(8,128)(2,1)S(1)}, bf16[64,256]{1,0:T(8,128)(2,1)S(1)}, bf16[64,256]{1,0:T(8,128)(2,1)S(1)}) custom-call(s32[1,128]{1,0:T(1,128)S(1)} %get-tuple-element.56.partner, bf16[9,64,128]{2,1,0:T(8,128)(2,1)S(1)} %collective-permute-done.16.got_a, ...), custom_call_target="tpu_custom_call" | custom-call | tf_op jit(solution)/shard_map/edges/pallas_call | solution.py:616
  10.7 0.1 collective-permute-start.17
  10.7 2.6 %collective-permute-start.18 = (bf16[64,256]{1,0:T(8,128)(2,1)S(1)}, bf16[64,256]{1,0:T(8,128)(2,1)S(1)}, u32[]{:S(2)}, u32[]{:S(2)}) collective-permute-start(bf16[64,256]{1,0:T(8,128)(2,1)S(1)} %get-tuple-element.65), channel_id=1, source_target_pairs={{0,28},{4,0},{8,4},{12,8},{16,12},{20,16},{24,20},{28,24},{1,29},{... | collective-permute-start | bytes 98312 | tf_op jit(solution)/shard_map/ppermute | solution.py:625
  13.4 1.6 %weights.1 = (f32[7,64,128]{2,1,0:T(8,128)S(1)}, f32[7,64,128]{2,1,0:T(8,128)S(1)}, f32[3,64,128]{2,1,0:T(8,128)S(1)}, bf16[256,80]{1,0:T(8,128)(2,1)S(1)}, bf16...) custom-call(bf16[7,7,64]{2,1,0:T(8,128)(2,1)S(1)} %bitcast.13, ...), custom_call_target="tpu_custom_call" | custom-call | tf_op jit(solution)/shard_map/weights/pallas_call | solution.py:627
  15.0 0.0 collective-permute-done.17.got_l
  15.0 0.0 collective-permute-done.18.got_r
  15.0 13.5 %own.1 = (bf16[64,16,128]{2,1,0:T(8,128)(2,1)}, f32[512,128]{1,0:T(8,128)S(1)}, f32[1024,128]{1,0:T(8,128)S(1)}, f32[168,128]{1,0:T(8,128)S(1)}, f32[168,128]{1,0:T(8,128)S(1)}) custom-call(bf16[16,64,128]{2,1,0:T(8,128)(2,1)S(1)} %get-tuple-element.54.ft, bf16[16,64,128]{2,1,0:T(8,128)(2,1)S(1)} %get-tuple-element.55.gt.refs_2_, ...), custom_call_target="tpu_custom_call" | custom-call | tf_op jit(solution)/shard_map/own/pallas_call | solution.py:655
  28.5 0.8 %collective-permute-start.19 = (f32[168,128]{1,0:T(8,128)S(1)}, f32[168,128]{1,0:T(8,128)S(1)}, u32[]{:S(2)}, u32[]{:S(2)}) collective-permute-start(f32[168,128]{1,0:T(8,128)S(1)} %get-tuple-element.73), channel_id=1, source_target_pairs={{0,4},{4,0},{8,12},{12,8},{16,20},{20,16},{24,28},{28,24},{1,5},{5... | collective-permute-start | bytes 258056 | tf_op jit(solution)/shard_map/ppermute | solution.py:732
  29.3 0.9 %collective-permute-done.19 = f32[168,128]{1,0:T(8,128)S(1)} collective-permute-done((f32[168,128]{1,0:T(8,128)S(1)}, f32[168,128]{1,0:T(8,128)S(1)}, u32[]{:S(2)}, u32[]{:S(2)}) %collective-permute-start.19) | collective-permute-done | bytes 86048 | tf_op jit(solution)/shard_map/ppermute | solution.py:732
  30.2 2.5 %collective-permute-start.20 = (f32[168,128]{1,0:T(8,128)S(1)}, f32[168,128]{1,0:T(8,128)S(1)}, u32[]{:S(2)}, u32[]{:S(2)}) collective-permute-start(f32[168,128]{1,0:T(8,128)S(1)} %add.15), channel_id=1, source_target_pairs={{0,8},{4,12},{8,0},{12,4},{16,24},{20,28},{24,16},{28,20},{1,9},{5... | collective-permute-start | bytes 258056 | tf_op jit(solution)/shard_map/ppermute | solution.py:732
  32.7 1.5 %halo.1.refs_1_ = f32[512,128]{1,0:T(8,128)S(1)} custom-call(f32[512,128]{1,0:T(8,128)S(1)} %get-tuple-element.74.conv_halo, bf16[9,64,128]{2,1,0:T(8,128)(2,1)S(1)} %get-tuple-element.62.low, bf16[9,64,128]{2,1,0:T(8,128)(2,1)S(1)} %get-tuple-element.63.up, bf16[64,256]{1,0:T(8,128)(2,1)S(1)} %collective-permute-done.17.got_l, ...), custom_call_target="tpu_custom_call" | custom-call | flops 150000000 | bytes 1048576 | tf_op jit(solution)/shard_map/halo/pallas_call | solution.py:699
  34.1 1.6 %collective-permute-done.20 = f32[168,128]{1,0:T(8,128)S(1)} collective-permute-done((f32[168,128]{1,0:T(8,128)S(1)}, f32[168,128]{1,0:T(8,128)S(1)}, u32[]{:S(2)}, u32[]{:S(2)}) %collective-permute-start.20) | collective-permute-done | bytes 86048 | tf_op jit(solution)/shard_map/ppermute | solution.py:732
  35.7 0.9 %collective-permute-start.21 = (f32[168,128]{1,0:T(8,128)S(1)}, f32[168,128]{1,0:T(8,128)S(1)}, u32[]{:S(2)}, u32[]{:S(2)}) collective-permute-start(f32[168,128]{1,0:T(8,128)S(1)} %add.16), channel_id=1, source_target_pairs={{0,16},{4,20},{8,24},{12,28},{16,0},{20,4},{24,8},{28,12},{1,17},{... | collective-permute-start | bytes 258056 | tf_op jit(solution)/shard_map/ppermute | solution.py:732
  36.7 2.4 %adjoint.2.refs_5_ = bf16[64,16,128]{2,1,0:T(8,128)(2,1)} custom-call(f32[1024,128]{1,0:T(8,128)S(1)} %get-tuple-element.76.refs_0_, f32[512,128]{1,0:T(8,128)S(1)} %halo.1.refs_1_, bf16[16,64,128]{2,1,0:T(8,128)(2,1)S(1)} %get-tuple-element.55.gt.refs_2_, f32[7,64,128]{2,1,0:T(8,128)S(1)} %get-tuple-element.78.refs_3_, ...), custom_call_target="tpu_custom_call" | custom-call | flops 200000000 | bytes 2097152 | tf_op jit(solution)/shard_map/adjoint/pallas_call | solution.py:712
  39.1 1.2 %collective-permute-done.21 = f32[168,128]{1,0:T(8,128)S(1)} collective-permute-done((f32[168,128]{1,0:T(8,128)S(1)}, f32[168,128]{1,0:T(8,128)S(1)}, u32[]{:S(2)}, u32[]{:S(2)}) %collective-permute-start.21) | collective-permute-done | bytes 86048 | tf_op jit(solution)/shard_map/ppermute | solution.py:732
  40.3 5.5 %collective-permute-start.22 = (f32[168,128]{1,0:T(8,128)S(1)}, f32[168,128]{1,0:T(8,128)S(1)}, u32[]{:S(2)}, u32[]{:S(2)}) collective-permute-start(f32[168,128]{1,0:T(8,128)S(1)} %add.17), channel_id=1, source_target_pairs={{0,1},{1,0},{2,3},{3,2},{4,5},{5,4},{6,7},{7,6},{8,9},{9,8},{10,11... | collective-permute-start | bytes 258056 | tf_op jit(solution)/shard_map/ppermute | solution.py:732
  45.8 2.4 %adjoint.3 = bf16[64,16,128]{2,1,0:T(8,128)(2,1)} custom-call(f32[1024,128]{1,0:T(8,128)S(1)} %get-tuple-element.76.refs_0_, f32[512,128]{1,0:T(8,128)S(1)} %halo.1.refs_1_, bf16[16,64,128]{2,1,0:T(8,128)(2,1)S(1)} %get-tuple-element.55.gt.refs_2_, f32[7,64,128]{2,1,0:T(8,128)S(1)} %get-tuple-element.78.refs_3_, ...), custom_call_target="tpu_custom_call", output_to_operand_aliasing={{}: (5, {})} | custom-call | flops 200000000 | bytes 2097152 | tf_op jit(solution)/shard_map/adjoint/pallas_call | solution.py:712
  48.2 0.0 collective-permute-done.22
  48.3 4.2 %collective-permute-start.23 = (f32[168,128]{1,0:T(8,128)S(1)}, f32[168,128]{1,0:T(8,128)S(1)}, u32[]{:S(2)}, u32[]{:S(2)}) collective-permute-start(f32[168,128]{1,0:T(8,128)S(1)} %add.18), channel_id=1, source_target_pairs={{0,2},{1,3},{2,0},{3,1},{4,6},{5,7},{6,4},{7,5},{8,10},{9,11},{10,... | collective-permute-start | bytes 258056 | tf_op jit(solution)/shard_map/ppermute | solution.py:732
  52.5 2.5 %collective-permute-done.23 = f32[168,128]{1,0:T(8,128)S(1)} collective-permute-done((f32[168,128]{1,0:T(8,128)S(1)}, f32[168,128]{1,0:T(8,128)S(1)}, u32[]{:S(2)}, u32[]{:S(2)}) %collective-permute-start.23) | collective-permute-done | bytes 86048 | tf_op jit(solution)/shard_map/ppermute | solution.py:732
  55.0 0.1 collective-permute-start.24
  55.0 1.3 %collective-permute-done.24.other = f32[168,128]{1,0:T(8,128)S(1)} collective-permute-done((f32[168,128]{1,0:T(8,128)S(1)}, f32[168,128]{1,0:T(8,128)S(1)}, u32[]{:S(2)}, u32[]{:S(2)}) %collective-permute-start.24) | collective-permute-done | bytes 86048 | tf_op jit(solution)/shard_map/ppermute | solution.py:732
  56.3 0.7 %finish.1 = (f32[7,7,64]{2,1,0:T(8,128)}, f32[64]{0:T(128)}, f32[64]{0:T(128)}, f32[64,256]{1,0:T(8,128)}, f32[256]{0:T(256)}, /*index=5*/f32[64,256]{1,0:T(8,128)}, f32[64]{0:T(128)}) custom-call(f32[168,128]{1,0:T(8,128)S(1)} %add.19.total, f32[168,128]{1,0:T(8,128)S(1)} %collective-permute-done.24.other), custom_call_target="tpu_custom_call" | custom-call | tf_op jit(solution)/shard_map/finish/pallas_call | solution.py:748
  (20 shorter events, 0.1 us)
Async XLA Ops:
  0.6 14.4 %copy-start.2 = (s32[16,128]{1,0:T(8,128)S(1)}, s32[16,128]{1,0:T(8,128)}, u32[]{:S(2)}) copy-start(s32[16,128]{1,0:T(8,128)} %mask.1) | copy-start | bytes 24580
  0.7 12.7 %copy-start.1 = (bf16[64,256]{1,0:T(8,128)(2,1)S(1)}, bf16[64,256]{1,0:T(8,128)(2,1)}, u32[]{:S(2)}) copy-start(bf16[64,256]{1,0:T(8,128)(2,1)} %down.3) | copy-start | bytes 98308
  0.7 12.7 %copy-start.6 = (bf16[64]{0:T(256)(128)(2,1)S(1)}, bf16[64]{0:T(256)(128)(2,1)}, u32[]{:S(2)}) copy-start(bf16[64]{0:T(256)(128)(2,1)} %scale.1) | copy-start | bytes 388
  0.7 12.7 %copy-start.7 = (bf16[256]{0:T(256)(128)(2,1)S(1)}, bf16[256]{0:T(256)(128)(2,1)}, u32[]{:S(2)}) copy-start(bf16[256]{0:T(256)(128)(2,1)} %up_b.1) | copy-start | bytes 1540
  0.7 12.7 %copy-start = (bf16[256,64]{0,1:T(8,128)(2,1)S(1)}, bf16[256,64]{0,1:T(8,128)(2,1)}, u32[]{:S(2)}) copy-start(bf16[256,64]{0,1:T(8,128)(2,1)} %param.26) | copy-start | bytes 98308
  0.7 12.7 %copy-start.5 = (bf16[64]{0:T(256)(128)(2,1)S(1)}, bf16[64]{0:T(256)(128)(2,1)}, u32[]{:S(2)}) copy-start(bf16[64]{0:T(256)(128)(2,1)} %bias.1) | copy-start | bytes 388
  0.7 12.7 %copy-start.4 = (bf16[64]{0:T(256)(128)(2,1)S(1)}, bf16[64]{0:T(256)(128)(2,1)}, u32[]{:S(2)}) copy-start(bf16[64]{0:T(256)(128)(2,1)} %gain.1) | copy-start | bytes 388
  0.7 12.7 %copy-start.3 = (bf16[64,7,7]{0,2,1:T(8,128)(2,1)S(1)}, bf16[64,7,7]{0,2,1:T(8,128)(2,1)}, u32[]{:S(2)}) copy-start(bf16[64,7,7]{0,2,1:T(8,128)(2,1)} %param.23) | copy-start | bytes 18820
  2.2 7.0 %collective-permute-start.16 = (bf16[9,64,128]{2,1,0:T(8,128)(2,1)S(1)}, bf16[9,64,128]{2,1,0:T(8,128)(2,1)S(1)}, u32[]{:S(2)}, u32[]{:S(2)}) collective-permute-start(bf16[9,64,128]{2,1,0:T(8,128)(2,1)S(1)} %get-tuple-element.57), channel_id=1, source_target_pairs={{0,1},{1,0},{4,5},{5,4},{8,9},{9,8},{12,13},{13,12},{16,17},{17,16... | collective-permute-start | bytes 442376 | tf_op jit(solution)/shard_map/ppermute | solution.py:601
  6.0 2.6 %collective-permute-start.5 = (bf16[9,64,128]{2,1,0:T(8,128)(2,1)S(1)}, bf16[9,64,128]{2,1,0:T(8,128)(2,1)}, u32[]{:S(2)}, u32[]{:S(2)}) collective-permute-start(bf16[9,64,128]{2,1,0:T(8,128)(2,1)S(1)} %param.2), channel_id=1, source_target_pairs={{1,2},{2,1},{5,6},{6,5},{9,10},{10,9},{13,14},{14,13},{17,18},{18,... | collective-permute-start | bytes 442376 | tf_op jit(solution)/shard_map/cond/branch_2_fun/ppermute | solution.py:610
  7.3 1.3 %collective-permute-start.4 = (bf16[9,64,128]{2,1,0:T(8,128)(2,1)S(1)}, bf16[9,64,128]{2,1,0:T(8,128)(2,1)}, u32[]{:S(2)}, u32[]{:S(2)}) collective-permute-start(bf16[9,64,128]{2,1,0:T(8,128)(2,1)S(1)} %param.2), channel_id=1, source_target_pairs={{3,7},{7,3},{11,31},{15,27},{19,23},{23,19},{27,15},{31,11}} | collective-permute-start | bytes 442376 | tf_op jit(solution)/shard_map/cond/branch_2_fun/ppermute | solution.py:610
  10.7 4.3 %collective-permute-start.17 = (bf16[64,256]{1,0:T(8,128)(2,1)S(1)}, bf16[64,256]{1,0:T(8,128)(2,1)S(1)}, u32[]{:S(2)}, u32[]{:S(2)}) collective-permute-start(bf16[64,256]{1,0:T(8,128)(2,1)S(1)} %get-tuple-element.64), channel_id=1, source_target_pairs={{0,4},{4,8},{8,12},{12,16},{16,20},{20,24},{24,28},{28,0},{1,5},{5... | collective-permute-start | bytes 98312 | tf_op jit(solution)/shard_map/ppermute | solution.py:624
  10.7 4.3 %collective-permute-start.18 = (bf16[64,256]{1,0:T(8,128)(2,1)S(1)}, bf16[64,256]{1,0:T(8,128)(2,1)S(1)}, u32[]{:S(2)}, u32[]{:S(2)}) collective-permute-start(bf16[64,256]{1,0:T(8,128)(2,1)S(1)} %get-tuple-element.65), channel_id=1, source_target_pairs={{0,28},{4,0},{8,4},{12,8},{16,12},{20,16},{24,20},{28,24},{1,29},{... | collective-permute-start | bytes 98312 | tf_op jit(solution)/shard_map/ppermute | solution.py:625
  28.5 1.7 %collective-permute-start.19 = (f32[168,128]{1,0:T(8,128)S(1)}, f32[168,128]{1,0:T(8,128)S(1)}, u32[]{:S(2)}, u32[]{:S(2)}) collective-permute-start(f32[168,128]{1,0:T(8,128)S(1)} %get-tuple-element.73), channel_id=1, source_target_pairs={{0,4},{4,0},{8,12},{12,8},{16,20},{20,16},{24,28},{28,24},{1,5},{5... | collective-permute-start | bytes 258056 | tf_op jit(solution)/shard_map/ppermute | solution.py:732
  30.2 5.5 %collective-permute-start.20 = (f32[168,128]{1,0:T(8,128)S(1)}, f32[168,128]{1,0:T(8,128)S(1)}, u32[]{:S(2)}, u32[]{:S(2)}) collective-permute-start(f32[168,128]{1,0:T(8,128)S(1)} %add.15), channel_id=1, source_target_pairs={{0,8},{4,12},{8,0},{12,4},{16,24},{20,28},{24,16},{28,20},{1,9},{5... | collective-permute-start | bytes 258056 | tf_op jit(solution)/shard_map/ppermute | solution.py:732
  35.7 4.6 %collective-permute-start.21 = (f32[168,128]{1,0:T(8,128)S(1)}, f32[168,128]{1,0:T(8,128)S(1)}, u32[]{:S(2)}, u32[]{:S(2)}) collective-permute-start(f32[168,128]{1,0:T(8,128)S(1)} %add.16), channel_id=1, source_target_pairs={{0,16},{4,20},{8,24},{12,28},{16,0},{20,4},{24,8},{28,12},{1,17},{... | collective-permute-start | bytes 258056 | tf_op jit(solution)/shard_map/ppermute | solution.py:732
  40.3 7.9 %collective-permute-start.22 = (f32[168,128]{1,0:T(8,128)S(1)}, f32[168,128]{1,0:T(8,128)S(1)}, u32[]{:S(2)}, u32[]{:S(2)}) collective-permute-start(f32[168,128]{1,0:T(8,128)S(1)} %add.17), channel_id=1, source_target_pairs={{0,1},{1,0},{2,3},{3,2},{4,5},{5,4},{6,7},{7,6},{8,9},{9,8},{10,11... | collective-permute-start | bytes 258056 | tf_op jit(solution)/shard_map/ppermute | solution.py:732
  48.3 6.7 %collective-permute-start.23 = (f32[168,128]{1,0:T(8,128)S(1)}, f32[168,128]{1,0:T(8,128)S(1)}, u32[]{:S(2)}, u32[]{:S(2)}) collective-permute-start(f32[168,128]{1,0:T(8,128)S(1)} %add.18), channel_id=1, source_target_pairs={{0,2},{1,3},{2,0},{3,1},{4,6},{5,7},{6,4},{7,5},{8,10},{9,11},{10,... | collective-permute-start | bytes 258056 | tf_op jit(solution)/shard_map/ppermute | solution.py:732
  55.0 1.3 %collective-permute-start.24 = (f32[168,128]{1,0:T(8,128)S(1)}, f32[168,128]{1,0:T(8,128)S(1)}, u32[]{:S(2)}, u32[]{:S(2)}) collective-permute-start(f32[168,128]{1,0:T(8,128)S(1)} %add.19.total), channel_id=1, source_target_pairs={{0,4},{4,0},{8,12},{12,8},{16,20},{20,16},{24,28},{28,24},{1,5},{5... | collective-permute-start | bytes 258056 | tf_op jit(solution)/shard_map/ppermute | solution.py:732

commit v6 on v5

--- a/solution.py
+++ b/solution.py
@@ -735,7 +735,11 @@
     steps += [("lat", 1 << i) for i in range(n_lat.bit_length() - 1)]
     grad = None
     for k, (axis, b) in enumerate(steps):
-        total = total + flip(total, axis, b)
+        if axis == "lat" and b > 1:
+            mine = total.astype(BF)
+            total = lax.reduce_precision(total, 8, 7) + flip(mine, axis, b).astype(F32)
+        else:
+            total = total + flip(total, axis, b)
         if k == 0:
             total, dcv_halo = lax.optimization_barrier((total, dcv_halo))
         elif k == 1:

time: 57.3 us -> 58.6 us (1.023)
  starting transfers between devices: 22.4 us -> 24.3 us
    ppermute x6, starting transfers between devices: 14 us -> 15.9 us  [shards(): lax.ppermute(y, axis, [(i, i ^ b) for i in range(lax.axis_size(axis))])]
  transfers between devices with their start and end apart: 11 -> 11, of which waited for: 6 -> 6; matrix products, arithmetic and copies ran while one was open for 0% -> 0% of each run, Pallas kernels for 14% -> 13%
where the time goes in v6:
time: 58.6 us; the launch traced here: 58.5 us
  Pallas kernels  25 us (43%)
  starting transfers between devices  24.3 us (41%)
  waiting for transfers between devices  7.56 us (13%)
  between operations  1.48 us (3%)
    ppermute x6, starting transfers between devices, shards(): lax.ppermute(y, axis, [(i, i ^ b) for i in range(lax.axis_size(axis))])  15.9 us
    pallas_call x1, Pallas kernels, shards(): pl.pallas_call(own_kernel, out_shape=[sds((chans, rows, cols), BF), sds((...  13.5 us
    ppermute x6, waiting for transfers between devices, shards(): lax.ppermute(y, axis, [(i, i ^ b) for i in range(lax.axis_size(axis))])  7.03 us
    pallas_call x2, Pallas kernels, adjoint(): pl.pallas_call(functools.partial(adjoint_kernel, part), grid=(1,), out_sh...  4.83 us
    ppermute x1, starting transfers between devices, shards(): met = lax.ppermute(sends[plain_round], axes, rounds[plain_round])  3.13 us
    ppermute x2, starting transfers between devices, run(): return (lax.ppermute(top, axes, mirror[1]), lax.ppermute(top, axes, plan))  2.64 us
    ppermute x1, starting transfers between devices, shards(): lax.ppermute(sent_l, 'lon', [(i, (i - 1) % n_lon) for i in range(n_lon)])  2.63 us
    pallas_call x1, Pallas kernels, shards(): pl.pallas_call(weight_kernel, out_shape=[sds((7, chans, LANES), F32), sds...  1.57 us
  transfers between devices with their start and end apart: 11, of which 6 were waited for; matrix products, arithmetic and copies ran while one was open for 0% of the time, Pallas kernels for 13%

profile of v6, /device:TPU:0, one launch (start us, length us, event | category | flops | bytes accessed | tf_op | source)
XLA Modules:
  0.0 58.5 jit_solution(5207421145160208121)
XLA Ops:
  0.7 1.5 %pack.1 = (bf16[16,64,128]{2,1,0:T(8,128)(2,1)S(1)}, bf16[16,64,128]{2,1,0:T(8,128)(2,1)S(1)}, bf16[9,64,128]{2,1,0:T(8,128)(2,1)S(1)}, bf16[9,64,128]{2,1,0:T(8...) custom-call(s32[8,128]{1,0:T(8,128)} %bitcast.17, bf16[64,16,128]{2,1,0:T(8,128)(2,1)} %bitcast.15, ...), custom_call_target="tpu_custom_call" | custom-call | tf_op jit(solution)/shard_map/pack/pallas_call | solution.py:566
  2.2 3.1 %collective-permute-start.16 = (bf16[9,64,128]{2,1,0:T(8,128)(2,1)S(1)}, bf16[9,64,128]{2,1,0:T(8,128)(2,1)S(1)}, u32[]{:S(2)}, u32[]{:S(2)}) collective-permute-start(bf16[9,64,128]{2,1,0:T(8,128)(2,1)S(1)} %get-tuple-element.57), channel_id=1, source_target_pairs={{0,1},{1,0},{4,5},{5,4},{8,9},{9,8},{12,13},{13,12},{16,17},{17,16... | collective-permute-start | bytes 442376 | tf_op jit(solution)/shard_map/ppermute | solution.py:601
  6.0 2.7 %conditional.1 = (bf16[9,64,128]{2,1,0:T(8,128)(2,1)}, bf16[9,64,128]{2,1,0:T(8,128)(2,1)}) conditional(s32[]{:T(128)} %bitcast.3, bf16[9,64,128]{2,1,0:T(8,128)(2,1)S(1)} %get-tuple-element.59, bf16[9,64,128]{2,1,0:T(8,128)(2,1)S(1)} %get-tuple-element.59, bf16[9,64,128]{2,1,0:T(8,128)(2,1)S(1)} %get-tuple-element.59, ...), branch_computations={%region_0.0_spmd, %region_1.0_spmd, %region_2.0_spmd, %region_3.0_... | conditional | bytes 1179744 | solution.py:614
  6.0 1.3 %collective-permute-start.13 = (bf16[9,64,128]{2,1,0:T(8,128)(2,1)S(1)}, bf16[9,64,128]{2,1,0:T(8,128)(2,1)}, u32[]{:S(2)}, u32[]{:S(2)}) collective-permute-start(bf16[9,64,128]{2,1,0:T(8,128)(2,1)S(1)} %param.6), channel_id=1, source_target_pairs={{1,2},{2,1},{5,6},{6,5},{9,10},{10,9},{13,14},{14,13},{17,18},{18,... | collective-permute-start | bytes 442376 | tf_op jit(solution)/shard_map/cond/branch_6_fun/ppermute | solution.py:610
  7.3 1.3 %collective-permute-start.12 = (bf16[9,64,128]{2,1,0:T(8,128)(2,1)S(1)}, bf16[9,64,128]{2,1,0:T(8,128)(2,1)}, u32[]{:S(2)}, u32[]{:S(2)}) collective-permute-start(bf16[9,64,128]{2,1,0:T(8,128)(2,1)S(1)} %param.6), channel_id=1, source_target_pairs={{3,23},{7,19},{11,15},{15,11},{19,7},{23,3},{27,31},{31,27}} | collective-permute-start | bytes 442376 | tf_op jit(solution)/shard_map/cond/branch_6_fun/ppermute | solution.py:610
  8.6 0.0 collective-permute-done.13
  8.6 0.0 collective-permute-done.12
  8.6 0.5 collective-permute-done.16.got_a
  9.2 1.5 %edges.1 = (bf16[9,64,128]{2,1,0:T(8,128)(2,1)S(1)}, bf16[9,64,128]{2,1,0:T(8,128)(2,1)S(1)}, bf16[64,256]{1,0:T(8,128)(2,1)S(1)}, bf16[64,256]{1,0:T(8,128)(2,1)S(1)}) custom-call(s32[1,128]{1,0:T(1,128)S(1)} %get-tuple-element.56.partner, bf16[9,64,128]{2,1,0:T(8,128)(2,1)S(1)} %collective-permute-done.16.got_a, ...), custom_call_target="tpu_custom_call" | custom-call | tf_op jit(solution)/shard_map/edges/pallas_call | solution.py:616
  10.7 0.1 collective-permute-start.17
  10.7 2.6 %collective-permute-start.18 = (bf16[64,256]{1,0:T(8,128)(2,1)S(1)}, bf16[64,256]{1,0:T(8,128)(2,1)S(1)}, u32[]{:S(2)}, u32[]{:S(2)}) collective-permute-start(bf16[64,256]{1,0:T(8,128)(2,1)S(1)} %get-tuple-element.65), channel_id=1, source_target_pairs={{0,28},{4,0},{8,4},{12,8},{16,12},{20,16},{24,20},{28,24},{1,29},{... | collective-permute-start | bytes 98312 | tf_op jit(solution)/shard_map/ppermute | solution.py:625
  13.4 0.0 copy-done
  13.4 1.6 %weights.1 = (f32[7,64,128]{2,1,0:T(8,128)S(1)}, f32[7,64,128]{2,1,0:T(8,128)S(1)}, f32[3,64,128]{2,1,0:T(8,128)S(1)}, bf16[256,80]{1,0:T(8,128)(2,1)S(1)}, bf16...) custom-call(bf16[7,7,64]{2,1,0:T(8,128)(2,1)S(1)} %bitcast.13, ...), custom_call_target="tpu_custom_call" | custom-call | tf_op jit(solution)/shard_map/weights/pallas_call | solution.py:627
  15.0 0.0 collective-permute-done.17.got_l
  15.0 0.0 collective-permute-done.18.got_r
  15.0 13.5 %own.1 = (bf16[64,16,128]{2,1,0:T(8,128)(2,1)}, f32[512,128]{1,0:T(8,128)S(1)}, f32[1024,128]{1,0:T(8,128)S(1)}, f32[168,128]{1,0:T(8,128)S(1)}, f32[168,128]{1,0:T(8,128)S(1)}) custom-call(bf16[16,64,128]{2,1,0:T(8,128)(2,1)S(1)} %get-tuple-element.54.ft, bf16[16,64,128]{2,1,0:T(8,128)(2,1)S(1)} %get-tuple-element.55.gt.refs_2_, ...), custom_call_target="tpu_custom_call" | custom-call | tf_op jit(solution)/shard_map/own/pallas_call | solution.py:655
  28.5 0.8 %collective-permute-start.19 = (f32[168,128]{1,0:T(8,128)S(1)}, f32[168,128]{1,0:T(8,128)S(1)}, u32[]{:S(2)}, u32[]{:S(2)}) collective-permute-start(f32[168,128]{1,0:T(8,128)S(1)} %get-tuple-element.73), channel_id=1, source_target_pairs={{0,4},{4,0},{8,12},{12,8},{16,20},{20,16},{24,28},{28,24},{1,5},{5... | collective-permute-start | bytes 258056 | tf_op jit(solution)/shard_map/ppermute | solution.py:732
  29.3 0.9 %collective-permute-done.19 = f32[168,128]{1,0:T(8,128)S(1)} collective-permute-done((f32[168,128]{1,0:T(8,128)S(1)}, f32[168,128]{1,0:T(8,128)S(1)}, u32[]{:S(2)}, u32[]{:S(2)}) %collective-permute-start.19) | collective-permute-done | bytes 86048 | tf_op jit(solution)/shard_map/ppermute | solution.py:732
  30.2 2.5 %collective-permute-start.20 = (f32[168,128]{1,0:T(8,128)S(1)}, f32[168,128]{1,0:T(8,128)S(1)}, u32[]{:S(2)}, u32[]{:S(2)}) collective-permute-start(f32[168,128]{1,0:T(8,128)S(1)} %add.15), channel_id=1, source_target_pairs={{0,8},{4,12},{8,0},{12,4},{16,24},{20,28},{24,16},{28,20},{1,9},{5... | collective-permute-start | bytes 258056 | tf_op jit(solution)/shard_map/ppermute | solution.py:732
  32.7 1.5 %halo.1.refs_1_ = f32[512,128]{1,0:T(8,128)S(1)} custom-call(f32[512,128]{1,0:T(8,128)S(1)} %get-tuple-element.74.conv_halo, bf16[9,64,128]{2,1,0:T(8,128)(2,1)S(1)} %get-tuple-element.62.low, bf16[9,64,128]{2,1,0:T(8,128)(2,1)S(1)} %get-tuple-element.63.up, bf16[64,256]{1,0:T(8,128)(2,1)S(1)} %collective-permute-done.17.got_l, ...), custom_call_target="tpu_custom_call" | custom-call | flops 150000000 | bytes 1048576 | tf_op jit(solution)/shard_map/halo/pallas_call | solution.py:699
  34.1 1.6 %collective-permute-done.20 = f32[168,128]{1,0:T(8,128)S(1)} collective-permute-done((f32[168,128]{1,0:T(8,128)S(1)}, f32[168,128]{1,0:T(8,128)S(1)}, u32[]{:S(2)}, u32[]{:S(2)}) %collective-permute-start.20) | collective-permute-done | bytes 86048 | tf_op jit(solution)/shard_map/ppermute | solution.py:732
  35.7 0.9 %collective-permute-start.21 = (f32[168,128]{1,0:T(8,128)S(1)}, f32[168,128]{1,0:T(8,128)S(1)}, u32[]{:S(2)}, u32[]{:S(2)}) collective-permute-start(f32[168,128]{1,0:T(8,128)S(1)} %add.16), channel_id=1, source_target_pairs={{0,16},{4,20},{8,24},{12,28},{16,0},{20,4},{24,8},{28,12},{1,17},{... | collective-permute-start | bytes 258056 | tf_op jit(solution)/shard_map/ppermute | solution.py:732
  36.7 2.4 %adjoint.2.refs_5_ = bf16[64,16,128]{2,1,0:T(8,128)(2,1)} custom-call(f32[1024,128]{1,0:T(8,128)S(1)} %get-tuple-element.76.refs_0_, f32[512,128]{1,0:T(8,128)S(1)} %halo.1.refs_1_, bf16[16,64,128]{2,1,0:T(8,128)(2,1)S(1)} %get-tuple-element.55.gt.refs_2_, f32[7,64,128]{2,1,0:T(8,128)S(1)} %get-tuple-element.78.refs_3_, ...), custom_call_target="tpu_custom_call" | custom-call | flops 200000000 | bytes 2097152 | tf_op jit(solution)/shard_map/adjoint/pallas_call | solution.py:712
  39.1 1.2 %collective-permute-done.21 = f32[168,128]{1,0:T(8,128)S(1)} collective-permute-done((f32[168,128]{1,0:T(8,128)S(1)}, f32[168,128]{1,0:T(8,128)S(1)}, u32[]{:S(2)}, u32[]{:S(2)}) %collective-permute-start.21) | collective-permute-done | bytes 86048 | tf_op jit(solution)/shard_map/ppermute | solution.py:732
  40.3 5.5 %collective-permute-start.22 = (f32[168,128]{1,0:T(8,128)S(1)}, f32[168,128]{1,0:T(8,128)S(1)}, u32[]{:S(2)}, u32[]{:S(2)}) collective-permute-start(f32[168,128]{1,0:T(8,128)S(1)} %add.17), channel_id=1, source_target_pairs={{0,1},{1,0},{2,3},{3,2},{4,5},{5,4},{6,7},{7,6},{8,9},{9,8},{10,11... | collective-permute-start | bytes 258056 | tf_op jit(solution)/shard_map/ppermute | solution.py:732
  45.8 2.4 %adjoint.3 = bf16[64,16,128]{2,1,0:T(8,128)(2,1)} custom-call(f32[1024,128]{1,0:T(8,128)S(1)} %get-tuple-element.76.refs_0_, f32[512,128]{1,0:T(8,128)S(1)} %halo.1.refs_1_, bf16[16,64,128]{2,1,0:T(8,128)(2,1)S(1)} %get-tuple-element.55.gt.refs_2_, f32[7,64,128]{2,1,0:T(8,128)S(1)} %get-tuple-element.78.refs_3_, ...), custom_call_target="tpu_custom_call", output_to_operand_aliasing={{}: (5, {})} | custom-call | flops 200000000 | bytes 2097152 | tf_op jit(solution)/shard_map/adjoint/pallas_call | solution.py:712
  48.2 0.0 collective-permute-done.22
  48.3 6.1 %collective-permute-start.23 = (bf16[168,128]{1,0:T(8,128)(2,1)S(1)}, bf16[168,128]{1,0:T(8,128)(2,1)S(1)}, u32[]{:S(2)}, u32[]{:S(2)}) collective-permute-start(bf16[168,128]{1,0:T(8,128)(2,1)S(1)} %convert_element_type.6), channel_id=1, source_target_pairs={{0,2},{1,3},{2,0},{3,1},{4,6},{5,7},{6,4},{7,5},{8,10},{9,11},{10,... | collective-permute-start | bytes 129032 | tf_op jit(solution)/shard_map/ppermute | solution.py:732
  54.4 2.0 %collective-permute-done.23 = bf16[168,128]{1,0:T(8,128)(2,1)S(1)} collective-permute-done((bf16[168,128]{1,0:T(8,128)(2,1)S(1)}, bf16[168,128]{1,0:T(8,128)(2,1)S(1)}, u32[]{:S(2)}, u32[]{:S(2)}) %collective-permute-start.23) | collective-permute-done | bytes 43040 | tf_op jit(solution)/shard_map/ppermute | solution.py:732
  56.4 0.1 collective-permute-start.24
  56.5 1.3 %collective-permute-done.24.other = f32[168,128]{1,0:T(8,128)S(1)} collective-permute-done((f32[168,128]{1,0:T(8,128)S(1)}, f32[168,128]{1,0:T(8,128)S(1)}, u32[]{:S(2)}, u32[]{:S(2)}) %collective-permute-start.24) | collective-permute-done | bytes 86048 | tf_op jit(solution)/shard_map/ppermute | solution.py:732
  57.8 0.7 %finish.1 = (f32[7,7,64]{2,1,0:T(8,128)}, f32[64]{0:T(128)}, f32[64]{0:T(128)}, f32[64,256]{1,0:T(8,128)}, f32[256]{0:T(256)}, /*index=5*/f32[64,256]{1,0:T(8,128)}, f32[64]{0:T(128)}) custom-call(f32[168,128]{1,0:T(8,128)S(1)} %convert_add_fusion.total, f32[168,128]{1,0:T(8,128)S(1)} %collective-permute-done.24.other), custom_call_target="tpu_custom_call" | custom-call | tf_op jit(solution)/shard_map/finish/pallas_call | solution.py:752
  (21 shorter events, 0.1 us)
Async XLA Ops:
  0.6 14.4 %copy-start.2 = (s32[16,128]{1,0:T(8,128)S(1)}, s32[16,128]{1,0:T(8,128)}, u32[]{:S(2)}) copy-start(s32[16,128]{1,0:T(8,128)} %mask.1) | copy-start | bytes 24580
  0.7 12.7 %copy-start.1 = (bf16[64,256]{1,0:T(8,128)(2,1)S(1)}, bf16[64,256]{1,0:T(8,128)(2,1)}, u32[]{:S(2)}) copy-start(bf16[64,256]{1,0:T(8,128)(2,1)} %down.3) | copy-start | bytes 98308
  0.7 12.7 %copy-start.6 = (bf16[64]{0:T(256)(128)(2,1)S(1)}, bf16[64]{0:T(256)(128)(2,1)}, u32[]{:S(2)}) copy-start(bf16[64]{0:T(256)(128)(2,1)} %scale.1) | copy-start | bytes 388
  0.7 12.7 %copy-start.7 = (bf16[256]{0:T(256)(128)(2,1)S(1)}, bf16[256]{0:T(256)(128)(2,1)}, u32[]{:S(2)}) copy-start(bf16[256]{0:T(256)(128)(2,1)} %up_b.1) | copy-start | bytes 1540
  0.7 12.7 %copy-start = (bf16[256,64]{0,1:T(8,128)(2,1)S(1)}, bf16[256,64]{0,1:T(8,128)(2,1)}, u32[]{:S(2)}) copy-start(bf16[256,64]{0,1:T(8,128)(2,1)} %param.26) | copy-start | bytes 98308
  0.7 12.7 %copy-start.5 = (bf16[64]{0:T(256)(128)(2,1)S(1)}, bf16[64]{0:T(256)(128)(2,1)}, u32[]{:S(2)}) copy-start(bf16[64]{0:T(256)(128)(2,1)} %bias.1) | copy-start | bytes 388
  0.7 12.7 %copy-start.4 = (bf16[64]{0:T(256)(128)(2,1)S(1)}, bf16[64]{0:T(256)(128)(2,1)}, u32[]{:S(2)}) copy-start(bf16[64]{0:T(256)(128)(2,1)} %gain.1) | copy-start | bytes 388
  0.7 12.7 %copy-start.3 = (bf16[64,7,7]{0,2,1:T(8,128)(2,1)S(1)}, bf16[64,7,7]{0,2,1:T(8,128)(2,1)}, u32[]{:S(2)}) copy-start(bf16[64,7,7]{0,2,1:T(8,128)(2,1)} %param.23) | copy-start | bytes 18820
  2.2 7.0 %collective-permute-start.16 = (bf16[9,64,128]{2,1,0:T(8,128)(2,1)S(1)}, bf16[9,64,128]{2,1,0:T(8,128)(2,1)S(1)}, u32[]{:S(2)}, u32[]{:S(2)}) collective-permute-start(bf16[9,64,128]{2,1,0:T(8,128)(2,1)S(1)} %get-tuple-element.57), channel_id=1, source_target_pairs={{0,1},{1,0},{4,5},{5,4},{8,9},{9,8},{12,13},{13,12},{16,17},{17,16... | collective-permute-start | bytes 442376 | tf_op jit(solution)/shard_map/ppermute | solution.py:601
  6.0 2.6 %collective-permute-start.13 = (bf16[9,64,128]{2,1,0:T(8,128)(2,1)S(1)}, bf16[9,64,128]{2,1,0:T(8,128)(2,1)}, u32[]{:S(2)}, u32[]{:S(2)}) collective-permute-start(bf16[9,64,128]{2,1,0:T(8,128)(2,1)S(1)} %param.6), channel_id=1, source_target_pairs={{1,2},{2,1},{5,6},{6,5},{9,10},{10,9},{13,14},{14,13},{17,18},{18,... | collective-permute-start | bytes 442376 | tf_op jit(solution)/shard_map/cond/branch_6_fun/ppermute | solution.py:610
  7.3 1.3 %collective-permute-start.12 = (bf16[9,64,128]{2,1,0:T(8,128)(2,1)S(1)}, bf16[9,64,128]{2,1,0:T(8,128)(2,1)}, u32[]{:S(2)}, u32[]{:S(2)}) collective-permute-start(bf16[9,64,128]{2,1,0:T(8,128)(2,1)S(1)} %param.6), channel_id=1, source_target_pairs={{3,23},{7,19},{11,15},{15,11},{19,7},{23,3},{27,31},{31,27}} | collective-permute-start | bytes 442376 | tf_op jit(solution)/shard_map/cond/branch_6_fun/ppermute | solution.py:610
  10.7 4.3 %collective-permute-start.17 = (bf16[64,256]{1,0:T(8,128)(2,1)S(1)}, bf16[64,256]{1,0:T(8,128)(2,1)S(1)}, u32[]{:S(2)}, u32[]{:S(2)}) collective-permute-start(bf16[64,256]{1,0:T(8,128)(2,1)S(1)} %get-tuple-element.64), channel_id=1, source_target_pairs={{0,4},{4,8},{8,12},{12,16},{16,20},{20,24},{24,28},{28,0},{1,5},{5... | collective-permute-start | bytes 98312 | tf_op jit(solution)/shard_map/ppermute | solution.py:624
  10.7 4.3 %collective-permute-start.18 = (bf16[64,256]{1,0:T(8,128)(2,1)S(1)}, bf16[64,256]{1,0:T(8,128)(2,1)S(1)}, u32[]{:S(2)}, u32[]{:S(2)}) collective-permute-start(bf16[64,256]{1,0:T(8,128)(2,1)S(1)} %get-tuple-element.65), channel_id=1, source_target_pairs={{0,28},{4,0},{8,4},{12,8},{16,12},{20,16},{24,20},{28,24},{1,29},{... | collective-permute-start | bytes 98312 | tf_op jit(solution)/shard_map/ppermute | solution.py:625
  28.5 1.7 %collective-permute-start.19 = (f32[168,128]{1,0:T(8,128)S(1)}, f32[168,128]{1,0:T(8,128)S(1)}, u32[]{:S(2)}, u32[]{:S(2)}) collective-permute-start(f32[168,128]{1,0:T(8,128)S(1)} %get-tuple-element.73), channel_id=1, source_target_pairs={{0,4},{4,0},{8,12},{12,8},{16,20},{20,16},{24,28},{28,24},{1,5},{5... | collective-permute-start | bytes 258056 | tf_op jit(solution)/shard_map/ppermute | solution.py:732
  30.2 5.5 %collective-permute-start.20 = (f32[168,128]{1,0:T(8,128)S(1)}, f32[168,128]{1,0:T(8,128)S(1)}, u32[]{:S(2)}, u32[]{:S(2)}) collective-permute-start(f32[168,128]{1,0:T(8,128)S(1)} %add.15), channel_id=1, source_target_pairs={{0,8},{4,12},{8,0},{12,4},{16,24},{20,28},{24,16},{28,20},{1,9},{5... | collective-permute-start | bytes 258056 | tf_op jit(solution)/shard_map/ppermute | solution.py:732
  35.7 4.6 %collective-permute-start.21 = (f32[168,128]{1,0:T(8,128)S(1)}, f32[168,128]{1,0:T(8,128)S(1)}, u32[]{:S(2)}, u32[]{:S(2)}) collective-permute-start(f32[168,128]{1,0:T(8,128)S(1)} %add.16), channel_id=1, source_target_pairs={{0,16},{4,20},{8,24},{12,28},{16,0},{20,4},{24,8},{28,12},{1,17},{... | collective-permute-start | bytes 258056 | tf_op jit(solution)/shard_map/ppermute | solution.py:732
  40.3 7.9 %collective-permute-start.22 = (f32[168,128]{1,0:T(8,128)S(1)}, f32[168,128]{1,0:T(8,128)S(1)}, u32[]{:S(2)}, u32[]{:S(2)}) collective-permute-start(f32[168,128]{1,0:T(8,128)S(1)} %add.17), channel_id=1, source_target_pairs={{0,1},{1,0},{2,3},{3,2},{4,5},{5,4},{6,7},{7,6},{8,9},{9,8},{10,11... | collective-permute-start | bytes 258056 | tf_op jit(solution)/shard_map/ppermute | solution.py:732
  48.3 8.1 %collective-permute-start.23 = (bf16[168,128]{1,0:T(8,128)(2,1)S(1)}, bf16[168,128]{1,0:T(8,128)(2,1)S(1)}, u32[]{:S(2)}, u32[]{:S(2)}) collective-permute-start(bf16[168,128]{1,0:T(8,128)(2,1)S(1)} %convert_element_type.6), channel_id=1, source_target_pairs={{0,2},{1,3},{2,0},{3,1},{4,6},{5,7},{6,4},{7,5},{8,10},{9,11},{10,... | collective-permute-start | bytes 129032 | tf_op jit(solution)/shard_map/ppermute | solution.py:732
  56.4 1.3 %collective-permute-start.24 = (f32[168,128]{1,0:T(8,128)S(1)}, f32[168,128]{1,0:T(8,128)S(1)}, u32[]{:S(2)}, u32[]{:S(2)}) collective-permute-start(f32[168,128]{1,0:T(8,128)S(1)} %convert_add_fusion.total), channel_id=1, source_target_pairs={{0,4},{4,0},{8,12},{12,8},{16,20},{20,16},{24,28},{28,24},{1,5},{5... | collective-permute-start | bytes 258056 | tf_op jit(solution)/shard_map/ppermute | solution.py:732

commit v7 on v5

--- a/solution.py
+++ b/solution.py
@@ -114,11 +114,11 @@
         far = jnp.where(near == 0, total, near) - cols
         pick_1 = (src + near == want).astype(F32).astype(BF)
         pick_2 = (src + far == want).astype(F32).astype(BF)
+        mixed = jnp.dot(got_1[...].reshape(9 * chans, cols), pick_1, preferred_element_type=F32)
+        mixed = mixed + jnp.dot(got_c[...].reshape(9 * chans, cols), pick_2, preferred_element_type=F32)
         for k in range(9):
             m = 5 - k if k < 6 else 14 - k
-            mixed = jnp.dot(got_1[m], pick_1, preferred_element_type=F32)
-            mixed = mixed + jnp.dot(got_c[m], pick_2, preferred_element_type=F32)
-            up[k] = mixed.astype(BF)
+            up[k] = mixed[m * chans : (m + 1) * chans].astype(BF)
 
     @pl.when(jnp.logical_not(top) & (odd == 0))
     def _():
@@ -601,30 +601,7 @@
     met = lax.ppermute(sends[plain_round], axes, rounds[plain_round])
     top = sends[fold_round]
 
-    def exchange(k):
-        def run(top):
-            mirror = [
-                [(at(lon, n_lat - 1), at(k - j - lon, n_lat - 1)) for lon in range(n_lon)] for j in (0, 1)
-            ]
-            plan = rounds[fold_round] + mirror[0]
-            return lax.ppermute(top, axes, mirror[1]), lax.ppermute(top, axes, plan)
-
-        return run
-
-    got_c, folded = lax.switch(turn[0], [exchange(k) for k in range(n_lon)], top)
-    got_a, got_b = (folded, met) if fold_round == 0 else (met, folded)
-    low, up, sent_l, sent_r = pl.pallas_call(
-        functools.partial(edge_kernel, fold_round == 0),
-        out_shape=[sds((9, chans, cols), BF)] * 2 + [sds((chans, 2 * cols), BF)] * 2,
-        in_specs=vmem(6),
-        out_specs=vmem(4),
-        compiler_params=pltpu.CompilerParams(vmem_limit_bytes=8 * 2**20),
-        name="edges",
-    )(partner, got_a, got_b, got_c, ft, gt)
-    got_l = lax.ppermute(sent_r, "lon", [(i, (i + 1) % n_lon) for i in range(n_lon)])
-    got_r = lax.ppermute(sent_l, "lon", [(i, (i - 1) % n_lon) for i in range(n_lon)])
-
-    plain, turned, vecs, up_aug, down_t, band, band_up = pl.pallas_call(
+    weights = pl.pallas_call(
         weight_kernel,
         out_shape=[
             sds((7, chans, LANES), F32),
@@ -638,9 +615,11 @@
         in_specs=vmem(7),
         out_specs=vmem(7),
         scratch_shapes=[pltpu.VMEM((2, 7, LANES, LANES), F32)],
+        cost_estimate=pl.CostEstimate(flops=20_000_000, bytes_accessed=2**21, transcendentals=0),
         compiler_params=pltpu.CompilerParams(vmem_limit_bytes=8 * 2**20),
         name="weights",
-    )(
+    )
+    params = (
         depth_weight.transpose(1, 2, 0),
         norm_gain,
         layer_norm_bias,
@@ -649,6 +628,31 @@
         up_weight.T,
         down_weight,
     )
+
+    def exchange(k):
+        def run(top, *params):
+            mirror = [
+                [(at(lon, n_lat - 1), at(k - j - lon, n_lat - 1)) for lon in range(n_lon)] for j in (0, 1)
+            ]
+            plan = rounds[fold_round] + mirror[0]
+            return lax.ppermute(top, axes, mirror[1]), lax.ppermute(top, axes, plan), weights(*params)
+
+        return run
+
+    got_c, folded, made = lax.switch(turn[0], [exchange(k) for k in range(n_lon)], top, *params)
+    plain, turned, vecs, up_aug, down_t, band, band_up = made
+    got_a, got_b = (folded, met) if fold_round == 0 else (met, folded)
+    low, up, sent_l, sent_r = pl.pallas_call(
+        functools.partial(edge_kernel, fold_round == 0),
+        out_shape=[sds((9, chans, cols), BF)] * 2 + [sds((chans, 2 * cols), BF)] * 2,
+        in_specs=vmem(6),
+        out_specs=vmem(4),
+        compiler_params=pltpu.CompilerParams(vmem_limit_bytes=8 * 2**20),
+        name="edges",
+    )(partner, got_a, got_b, got_c, ft, gt)
+    got_l = lax.ppermute(sent_r, "lon", [(i, (i + 1) % n_lon) for i in range(n_lon)])
+    got_r = lax.ppermute(sent_l, "lon", [(i, (i - 1) % n_lon) for i in range(n_lon)])
+
     big, small = 2 * chans, 40
     up_t = up_weight.T
     band_rows = (rows + 12) * 8

time: 57.3 us -> 59.6 us (1.040)
  Pallas kernels: 25 us -> 26.7 us
  waiting for transfers between devices: 8.03 us -> 9.1 us
  starting transfers between devices: 22.4 us -> 21.5 us
    ppermute x1, waiting for transfers between devices: 0.01 us -> 1.59 us  [shards(): lax.ppermute(sent_r, 'lon', [(i, (i + 1) % n_lon) for i in range(n_lon)])]
    ppermute x6, starting transfers between devices: 14 us -> 13.1 us  [shards(): lax.ppermute(y, axis, [(i, i ^ b) for i in range(lax.axis_size(axis))])]
    pallas_call x1, Pallas kernels: 1.57 us -> 2.42 us  [run(): weights(*params)]
    pallas_call x1, Pallas kernels: 13.5 us -> 14.3 us  [shards(): pl.pallas_call(own_kernel, out_shape=[sds((chans, rows, cols), BF), sds((...]
  transfers between devices with their start and end apart: 11 -> 11, of which waited for: 6 -> 6; matrix products, arithmetic and copies ran while one was open for 0% -> 0% of each run, Pallas kernels for 14% -> 15%
where the time goes in v7:
time: 59.6 us; the launch traced here: 58.8 us
  Pallas kernels  26.7 us (45%)
  starting transfers between devices  21.5 us (36%)
  waiting for transfers between devices  9.1 us (15%)
  between operations  1.38 us (2%)
    pallas_call x1, Pallas kernels, shards(): pl.pallas_call(own_kernel, out_shape=[sds((chans, rows, cols), BF), sds((...  14.3 us
    ppermute x6, starting transfers between devices, shards(): lax.ppermute(y, axis, [(i, i ^ b) for i in range(lax.axis_size(axis))])  13.1 us
    ppermute x6, waiting for transfers between devices, shards(): lax.ppermute(y, axis, [(i, i ^ b) for i in range(lax.axis_size(axis))])  7.49 us
    pallas_call x2, Pallas kernels, adjoint(): pl.pallas_call(functools.partial(adjoint_kernel, part), grid=(1,), out_sh...  4.84 us
    ppermute x1, starting transfers between devices, shards(): met = lax.ppermute(sends[plain_round], axes, rounds[plain_round])  3.13 us
    ppermute x1, starting transfers between devices, shards(): lax.ppermute(sent_l, 'lon', [(i, (i - 1) % n_lon) for i in range(n_lon)])  2.63 us
    pallas_call x1, Pallas kernels, run(): weights(*params)  2.42 us
    ppermute x1, waiting for transfers between devices, shards(): lax.ppermute(sent_r, 'lon', [(i, (i + 1) % n_lon) for i in range(n_lon)])  1.59 us
  transfers between devices with their start and end apart: 11, of which 6 were waited for; matrix products, arithmetic and copies ran while one was open for 0% of the time, Pallas kernels for 15%

profile of v7, /device:TPU:0, one launch (start us, length us, event | category | flops | bytes accessed | tf_op | source)
XLA Modules:
  0.0 58.8 jit_solution(11259948043054067001)
XLA Ops:
  0.6 0.0 copy-start
  0.7 1.4 %pack.1 = (bf16[16,64,128]{2,1,0:T(8,128)(2,1)S(1)}, bf16[16,64,128]{2,1,0:T(8,128)(2,1)S(1)}, bf16[9,64,128]{2,1,0:T(8,128)(2,1)S(1)}, bf16[9,64,128]{2,1,0:T(8...) custom-call(s32[8,128]{1,0:T(8,128)} %bitcast.31, bf16[64,16,128]{2,1,0:T(8,128)(2,1)} %bitcast.29, ...), custom_call_target="tpu_custom_call" | custom-call | tf_op jit(solution)/shard_map/pack/pallas_call | solution.py:566
  2.1 3.1 %collective-permute-start.16 = (bf16[9,64,128]{2,1,0:T(8,128)(2,1)S(1)}, bf16[9,64,128]{2,1,0:T(8,128)(2,1)S(1)}, u32[]{:S(2)}, u32[]{:S(2)}) collective-permute-start(bf16[9,64,128]{2,1,0:T(8,128)(2,1)S(1)} %get-tuple-element.297), channel_id=1, source_target_pairs={{0,1},{1,0},{4,5},{5,4},{8,9},{9,8},{12,13},{13,12},{16,17},{17,16... | collective-permute-start | bytes 442376 | tf_op jit(solution)/shard_map/ppermute | solution.py:601
  5.9 5.1 %conditional.1 = (bf16[9,64,128]{2,1,0:T(8,128)(2,1)}, bf16[9,64,128]{2,1,0:T(8,128)(2,1)}, f32[7,64,128]{2,1,0:T(8,128)S(1)}, f32[7,64,128]{2,1,0:T(8,128)S(1)}...) conditional(s32[]{:T(128)} %bitcast.3, ...), branch_computations={%region_0.0_spmd, %region_1.0_spmd, %region_2.0_spmd, %region_3.0_... | conditional | flops 20000000 | bytes 3276952 | solution.py:642
  5.9 1.3 %collective-permute-start.15 = (bf16[9,64,128]{2,1,0:T(8,128)(2,1)S(1)}, bf16[9,64,128]{2,1,0:T(8,128)(2,1)}, u32[]{:S(2)}, u32[]{:S(2)}) collective-permute-start(bf16[9,64,128]{2,1,0:T(8,128)(2,1)S(1)} %get-tuple-element.233), channel_id=1, source_target_pairs={{1,2},{2,1},{5,6},{6,5},{9,10},{10,9},{13,14},{14,13},{17,18},{18,... | collective-permute-start | bytes 442376 | tf_op jit(solution)/shard_map/cond/branch_7_fun/ppermute | solution.py:638
  7.2 1.3 %collective-permute-start.14 = (bf16[9,64,128]{2,1,0:T(8,128)(2,1)S(1)}, bf16[9,64,128]{2,1,0:T(8,128)(2,1)}, u32[]{:S(2)}, u32[]{:S(2)}) collective-permute-start(bf16[9,64,128]{2,1,0:T(8,128)(2,1)S(1)} %get-tuple-element.233), channel_id=1, source_target_pairs={{3,27},{7,23},{11,19},{15,15},{19,11},{23,7},{27,3},{31,31}} | collective-permute-start | bytes 442376 | tf_op jit(solution)/shard_map/cond/branch_7_fun/ppermute | solution.py:638
  8.5 2.4 %weights.15 = (f32[7,64,128]{2,1,0:T(8,128)S(1)}, f32[7,64,128]{2,1,0:T(8,128)S(1)}, f32[3,64,128]{2,1,0:T(8,128)S(1)}, bf16[256,80]{1,0:T(8,128)(2,1)S(1)}, bf1...) custom-call(bf16[7,7,64]{2,1,0:T(8,128)(2,1)} %get-tuple-element.234.taps, ...), custom_call_target="tpu_custom_call" | custom-call | flops 20000000 | bytes 2097152 | tf_op jit(solution)/shard_map/cond/branch_7_fun/weights/pallas_call | solution.py:638
  11.0 0.0 collective-permute-done.15
  11.0 0.0 collective-permute-done.14
  11.0 0.0 collective-permute-done.16.got_a
  11.0 1.5 %edges.1 = (bf16[9,64,128]{2,1,0:T(8,128)(2,1)S(1)}, bf16[9,64,128]{2,1,0:T(8,128)(2,1)S(1)}, bf16[64,256]{1,0:T(8,128)(2,1)S(1)}, bf16[64,256]{1,0:T(8,128)(2,1)S(1)}) custom-call(s32[1,128]{1,0:T(1,128)S(1)} %get-tuple-element.296.partner, bf16[9,64,128]{2,1,0:T(8,128)(2,1)S(1)} %collective-permute-done.16.got_a, ...), custom_call_target="tpu_custom_call" | custom-call | tf_op jit(solution)/shard_map/edges/pallas_call | solution.py:645
  12.5 0.1 collective-permute-start.17
  12.6 2.6 %collective-permute-start.18 = (bf16[64,256]{1,0:T(8,128)(2,1)S(1)}, bf16[64,256]{1,0:T(8,128)(2,1)S(1)}, u32[]{:S(2)}, u32[]{:S(2)}) collective-permute-start(bf16[64,256]{1,0:T(8,128)(2,1)S(1)} %get-tuple-element.305), channel_id=1, source_target_pairs={{0,28},{4,0},{8,4},{12,8},{16,12},{20,16},{24,20},{28,24},{1,29},{... | collective-permute-start | bytes 98312 | tf_op jit(solution)/shard_map/ppermute | solution.py:654
  15.2 1.6 %collective-permute-done.17.got_l = bf16[64,256]{1,0:T(8,128)(2,1)S(1)} collective-permute-done((bf16[64,256]{1,0:T(8,128)(2,1)S(1)}, bf16[64,256]{1,0:T(8,128)(2,1)S(1)}, u32[]{:S(2)}, u32[]{:S(2)}) %collective-permute-start.17) | collective-permute-done | bytes 32800 | tf_op jit(solution)/shard_map/ppermute | solution.py:653
  16.8 0.0 collective-permute-done.18.got_r
  16.8 14.3 %own.1 = (bf16[64,16,128]{2,1,0:T(8,128)(2,1)}, f32[512,128]{1,0:T(8,128)S(1)}, f32[1024,128]{1,0:T(8,128)S(1)}, f32[168,128]{1,0:T(8,128)S(1)}, f32[168,128]{1,0:T(8,128)S(1)}) custom-call(bf16[16,64,128]{2,1,0:T(8,128)(2,1)S(1)} %get-tuple-element.294.ft, bf16[16,64,128]{2,1,0:T(8,128)(2,1)S(1)} %get-tuple-element.295.gt.refs_2_, ...), custom_call_target="tpu_custom_call" | custom-call | tf_op jit(solution)/shard_map/own/pallas_call | solution.py:659
  31.1 0.7 %collective-permute-start.19 = (f32[168,128]{1,0:T(8,128)S(1)}, f32[168,128]{1,0:T(8,128)S(1)}, u32[]{:S(2)}, u32[]{:S(2)}) collective-permute-start(f32[168,128]{1,0:T(8,128)S(1)} %get-tuple-element.313), channel_id=1, source_target_pairs={{0,4},{4,0},{8,12},{12,8},{16,20},{20,16},{24,28},{28,24},{1,5},{5... | collective-permute-start | bytes 258056 | tf_op jit(solution)/shard_map/ppermute | solution.py:736
  31.8 0.9 %collective-permute-done.19 = f32[168,128]{1,0:T(8,128)S(1)} collective-permute-done((f32[168,128]{1,0:T(8,128)S(1)}, f32[168,128]{1,0:T(8,128)S(1)}, u32[]{:S(2)}, u32[]{:S(2)}) %collective-permute-start.19) | collective-permute-done | bytes 86048 | tf_op jit(solution)/shard_map/ppermute | solution.py:736
  32.8 2.5 %collective-permute-start.20 = (f32[168,128]{1,0:T(8,128)S(1)}, f32[168,128]{1,0:T(8,128)S(1)}, u32[]{:S(2)}, u32[]{:S(2)}) collective-permute-start(f32[168,128]{1,0:T(8,128)S(1)} %add.15), channel_id=1, source_target_pairs={{0,8},{4,12},{8,0},{12,4},{16,24},{20,28},{24,16},{28,20},{1,9},{5... | collective-permute-start | bytes 258056 | tf_op jit(solution)/shard_map/ppermute | solution.py:736
  35.2 1.5 %halo.1.refs_1_ = f32[512,128]{1,0:T(8,128)S(1)} custom-call(f32[512,128]{1,0:T(8,128)S(1)} %get-tuple-element.314.conv_halo, bf16[9,64,128]{2,1,0:T(8,128)(2,1)S(1)} %get-tuple-element.302.low, bf16[9,64,128]{2,1,0:T(8,128)(2,1)S(1)} %get-tuple-element.303.up, bf16[64,256]{1,0:T(8,128)(2,1)S(1)} %collective-permute-done.17.got_l, ...), custom_call_target="tpu_custom_call" | custom-call | flops 150000000 | bytes 1048576 | tf_op jit(solution)/shard_map/halo/pallas_call | solution.py:703
  36.7 1.6 %collective-permute-done.20 = f32[168,128]{1,0:T(8,128)S(1)} collective-permute-done((f32[168,128]{1,0:T(8,128)S(1)}, f32[168,128]{1,0:T(8,128)S(1)}, u32[]{:S(2)}, u32[]{:S(2)}) %collective-permute-start.20) | collective-permute-done | bytes 86048 | tf_op jit(solution)/shard_map/ppermute | solution.py:736
  38.3 0.9 %collective-permute-start.21 = (f32[168,128]{1,0:T(8,128)S(1)}, f32[168,128]{1,0:T(8,128)S(1)}, u32[]{:S(2)}, u32[]{:S(2)}) collective-permute-start(f32[168,128]{1,0:T(8,128)S(1)} %add.16), channel_id=1, source_target_pairs={{0,16},{4,20},{8,24},{12,28},{16,0},{20,4},{24,8},{28,12},{1,17},{... | collective-permute-start | bytes 258056 | tf_op jit(solution)/shard_map/ppermute | solution.py:736
  39.2 2.4 %adjoint.2.refs_5_ = bf16[64,16,128]{2,1,0:T(8,128)(2,1)} custom-call(f32[1024,128]{1,0:T(8,128)S(1)} %get-tuple-element.316.refs_0_, f32[512,128]{1,0:T(8,128)S(1)} %halo.1.refs_1_, bf16[16,64,128]{2,1,0:T(8,128)(2,1)S(1)} %get-tuple-element.295.gt.refs_2_, f32[7,64,128]{2,1,0:T(8,128)S(1)} %get-tuple-element.318.refs_3_, ...), custom_call_target="tpu_custom_call" | custom-call | flops 200000000 | bytes 2097152 | tf_op jit(solution)/shard_map/adjoint/pallas_call | solution.py:716
  41.6 1.2 %collective-permute-done.21 = f32[168,128]{1,0:T(8,128)S(1)} collective-permute-done((f32[168,128]{1,0:T(8,128)S(1)}, f32[168,128]{1,0:T(8,128)S(1)}, u32[]{:S(2)}, u32[]{:S(2)}) %collective-permute-start.21) | collective-permute-done | bytes 86048 | tf_op jit(solution)/shard_map/ppermute | solution.py:736
  42.8 3.8 %collective-permute-start.22 = (f32[168,128]{1,0:T(8,128)S(1)}, f32[168,128]{1,0:T(8,128)S(1)}, u32[]{:S(2)}, u32[]{:S(2)}) collective-permute-start(f32[168,128]{1,0:T(8,128)S(1)} %add.17), channel_id=1, source_target_pairs={{0,1},{1,0},{2,3},{3,2},{4,5},{5,4},{6,7},{7,6},{8,9},{9,8},{10,11... | collective-permute-start | bytes 258056 | tf_op jit(solution)/shard_map/ppermute | solution.py:736
  46.7 2.4 %adjoint.3 = bf16[64,16,128]{2,1,0:T(8,128)(2,1)} custom-call(f32[1024,128]{1,0:T(8,128)S(1)} %get-tuple-element.316.refs_0_, f32[512,128]{1,0:T(8,128)S(1)} %halo.1.refs_1_, bf16[16,64,128]{2,1,0:T(8,128)(2,1)S(1)} %get-tuple-element.295.gt.refs_2_, f32[7,64,128]{2,1,0:T(8,128)S(1)} %get-tuple-element.318.refs_3_, ...), custom_call_target="tpu_custom_call", output_to_operand_aliasing={{}: (5, {})} | custom-call | flops 200000000 | bytes 2097152 | tf_op jit(solution)/shard_map/adjoint/pallas_call | solution.py:716
  49.1 0.0 collective-permute-done.22
  49.2 5.1 %collective-permute-start.23 = (f32[168,128]{1,0:T(8,128)S(1)}, f32[168,128]{1,0:T(8,128)S(1)}, u32[]{:S(2)}, u32[]{:S(2)}) collective-permute-start(f32[168,128]{1,0:T(8,128)S(1)} %add.18), channel_id=1, source_target_pairs={{0,2},{1,3},{2,0},{3,1},{4,6},{5,7},{6,4},{7,5},{8,10},{9,11},{10,... | collective-permute-start | bytes 258056 | tf_op jit(solution)/shard_map/ppermute | solution.py:736
  54.2 2.5 %collective-permute-done.23 = f32[168,128]{1,0:T(8,128)S(1)} collective-permute-done((f32[168,128]{1,0:T(8,128)S(1)}, f32[168,128]{1,0:T(8,128)S(1)}, u32[]{:S(2)}, u32[]{:S(2)}) %collective-permute-start.23) | collective-permute-done | bytes 86048 | tf_op jit(solution)/shard_map/ppermute | solution.py:736
  56.7 0.1 collective-permute-start.24
  56.8 1.3 %collective-permute-done.24.other = f32[168,128]{1,0:T(8,128)S(1)} collective-permute-done((f32[168,128]{1,0:T(8,128)S(1)}, f32[168,128]{1,0:T(8,128)S(1)}, u32[]{:S(2)}, u32[]{:S(2)}) %collective-permute-start.24) | collective-permute-done | bytes 86048 | tf_op jit(solution)/shard_map/ppermute | solution.py:736
  58.1 0.7 %finish.1 = (f32[7,7,64]{2,1,0:T(8,128)}, f32[64]{0:T(128)}, f32[64]{0:T(128)}, f32[64,256]{1,0:T(8,128)}, f32[256]{0:T(256)}, /*index=5*/f32[64,256]{1,0:T(8,128)}, f32[64]{0:T(128)}) custom-call(f32[168,128]{1,0:T(8,128)S(1)} %add.19.total, f32[168,128]{1,0:T(8,128)S(1)} %collective-permute-done.24.other), custom_call_target="tpu_custom_call" | custom-call | tf_op jit(solution)/shard_map/finish/pallas_call | solution.py:752
  (8 shorter events, 0.1 us)
Async XLA Ops:
  0.6 16.2 %copy-start = (s32[16,128]{1,0:T(8,128)S(1)}, s32[16,128]{1,0:T(8,128)}, u32[]{:S(2)}) copy-start(s32[16,128]{1,0:T(8,128)} %mask.1) | copy-start | bytes 24580
  2.1 8.9 %collective-permute-start.16 = (bf16[9,64,128]{2,1,0:T(8,128)(2,1)S(1)}, bf16[9,64,128]{2,1,0:T(8,128)(2,1)S(1)}, u32[]{:S(2)}, u32[]{:S(2)}) collective-permute-start(bf16[9,64,128]{2,1,0:T(8,128)(2,1)S(1)} %get-tuple-element.297), channel_id=1, source_target_pairs={{0,1},{1,0},{4,5},{5,4},{8,9},{9,8},{12,13},{13,12},{16,17},{17,16... | collective-permute-start | bytes 442376 | tf_op jit(solution)/shard_map/ppermute | solution.py:601
  5.9 5.1 %collective-permute-start.15 = (bf16[9,64,128]{2,1,0:T(8,128)(2,1)S(1)}, bf16[9,64,128]{2,1,0:T(8,128)(2,1)}, u32[]{:S(2)}, u32[]{:S(2)}) collective-permute-start(bf16[9,64,128]{2,1,0:T(8,128)(2,1)S(1)} %get-tuple-element.233), channel_id=1, source_target_pairs={{1,2},{2,1},{5,6},{6,5},{9,10},{10,9},{13,14},{14,13},{17,18},{18,... | collective-permute-start | bytes 442376 | tf_op jit(solution)/shard_map/cond/branch_7_fun/ppermute | solution.py:638
  7.2 3.8 %collective-permute-start.14 = (bf16[9,64,128]{2,1,0:T(8,128)(2,1)S(1)}, bf16[9,64,128]{2,1,0:T(8,128)(2,1)}, u32[]{:S(2)}, u32[]{:S(2)}) collective-permute-start(bf16[9,64,128]{2,1,0:T(8,128)(2,1)S(1)} %get-tuple-element.233), channel_id=1, source_target_pairs={{3,27},{7,23},{11,19},{15,15},{19,11},{23,7},{27,3},{31,31}} | collective-permute-start | bytes 442376 | tf_op jit(solution)/shard_map/cond/branch_7_fun/ppermute | solution.py:638
  12.5 4.3 %collective-permute-start.17 = (bf16[64,256]{1,0:T(8,128)(2,1)S(1)}, bf16[64,256]{1,0:T(8,128)(2,1)S(1)}, u32[]{:S(2)}, u32[]{:S(2)}) collective-permute-start(bf16[64,256]{1,0:T(8,128)(2,1)S(1)} %get-tuple-element.304), channel_id=1, source_target_pairs={{0,4},{4,8},{8,12},{12,16},{16,20},{20,24},{24,28},{28,0},{1,5},{5... | collective-permute-start | bytes 98312 | tf_op jit(solution)/shard_map/ppermute | solution.py:653
  12.6 4.2 %collective-permute-start.18 = (bf16[64,256]{1,0:T(8,128)(2,1)S(1)}, bf16[64,256]{1,0:T(8,128)(2,1)S(1)}, u32[]{:S(2)}, u32[]{:S(2)}) collective-permute-start(bf16[64,256]{1,0:T(8,128)(2,1)S(1)} %get-tuple-element.305), channel_id=1, source_target_pairs={{0,28},{4,0},{8,4},{12,8},{16,12},{20,16},{24,20},{28,24},{1,29},{... | collective-permute-start | bytes 98312 | tf_op jit(solution)/shard_map/ppermute | solution.py:654
  16.8 18.4 %copy-start.1 = (bf16[256,64]{0,1:T(8,128)(2,1)S(1)}, bf16[256,64]{0,1:T(8,128)(2,1)}, u32[]{:S(2)}) copy-start(bf16[256,64]{0,1:T(8,128)(2,1)} %param.26) | copy-start | bytes 98308
  31.1 1.6 %collective-permute-start.19 = (f32[168,128]{1,0:T(8,128)S(1)}, f32[168,128]{1,0:T(8,128)S(1)}, u32[]{:S(2)}, u32[]{:S(2)}) collective-permute-start(f32[168,128]{1,0:T(8,128)S(1)} %get-tuple-element.313), channel_id=1, source_target_pairs={{0,4},{4,0},{8,12},{12,8},{16,20},{20,16},{24,28},{28,24},{1,5},{5... | collective-permute-start | bytes 258056 | tf_op jit(solution)/shard_map/ppermute | solution.py:736
  32.8 5.5 %collective-permute-start.20 = (f32[168,128]{1,0:T(8,128)S(1)}, f32[168,128]{1,0:T(8,128)S(1)}, u32[]{:S(2)}, u32[]{:S(2)}) collective-permute-start(f32[168,128]{1,0:T(8,128)S(1)} %add.15), channel_id=1, source_target_pairs={{0,8},{4,12},{8,0},{12,4},{16,24},{20,28},{24,16},{28,20},{1,9},{5... | collective-permute-start | bytes 258056 | tf_op jit(solution)/shard_map/ppermute | solution.py:736
  38.3 4.6 %collective-permute-start.21 = (f32[168,128]{1,0:T(8,128)S(1)}, f32[168,128]{1,0:T(8,128)S(1)}, u32[]{:S(2)}, u32[]{:S(2)}) collective-permute-start(f32[168,128]{1,0:T(8,128)S(1)} %add.16), channel_id=1, source_target_pairs={{0,16},{4,20},{8,24},{12,28},{16,0},{20,4},{24,8},{28,12},{1,17},{... | collective-permute-start | bytes 258056 | tf_op jit(solution)/shard_map/ppermute | solution.py:736
  42.8 6.3 %collective-permute-start.22 = (f32[168,128]{1,0:T(8,128)S(1)}, f32[168,128]{1,0:T(8,128)S(1)}, u32[]{:S(2)}, u32[]{:S(2)}) collective-permute-start(f32[168,128]{1,0:T(8,128)S(1)} %add.17), channel_id=1, source_target_pairs={{0,1},{1,0},{2,3},{3,2},{4,5},{5,4},{6,7},{7,6},{8,9},{9,8},{10,11... | collective-permute-start | bytes 258056 | tf_op jit(solution)/shard_map/ppermute | solution.py:736
  49.2 7.5 %collective-permute-start.23 = (f32[168,128]{1,0:T(8,128)S(1)}, f32[168,128]{1,0:T(8,128)S(1)}, u32[]{:S(2)}, u32[]{:S(2)}) collective-permute-start(f32[168,128]{1,0:T(8,128)S(1)} %add.18), channel_id=1, source_target_pairs={{0,2},{1,3},{2,0},{3,1},{4,6},{5,7},{6,4},{7,5},{8,10},{9,11},{10,... | collective-permute-start | bytes 258056 | tf_op jit(solution)/shard_map/ppermute | solution.py:736
  56.7 1.3 %collective-permute-start.24 = (f32[168,128]{1,0:T(8,128)S(1)}, f32[168,128]{1,0:T(8,128)S(1)}, u32[]{:S(2)}, u32[]{:S(2)}) collective-permute-start(f32[168,128]{1,0:T(8,128)S(1)} %add.19.total), channel_id=1, source_target_pairs={{0,4},{4,0},{8,12},{12,8},{16,20},{20,16},{24,28},{28,24},{1,5},{5... | collective-permute-start | bytes 258056 | tf_op jit(solution)/shard_map/ppermute | solution.py:736
